TPU v7x, 32 devices: a whole 2x2x4 slice. The times are simulated.
32 devices in a mesh: dp: 8 (over z, y), tensor: 4 (over x, core).
Axes of the slice: x: 2, y: 2, z: 4, core: 2. Of those that a mesh axis runs over, the one named last changes fastest.
Arguments:
- tokens: bfloat16 [16384, 1024], P('dp'), may hold values from -6 to 6
- segment_ids: int32 [16384], P('dp'), may hold values from 0 to 14, as said below
- positions: int32 [16384], P('dp'), may hold values from 0 to 1023, as said below
- pad_mask: int32 [16384], P('dp'), may hold values from 0 to 1, as said below
- w_query: bfloat16 [1024, 1024], P('dp', 'tensor'), may hold values from -0.1875 to 0.1875
- w_key: bfloat16 [1024, 512], P('dp', 'tensor'), may hold values from -0.1875 to 0.1875
- w_value: bfloat16 [1024, 512], P('dp', 'tensor'), may hold values from -0.1875 to 0.1875
- w_out: bfloat16 [1024, 1024], P('tensor', 'dp'), may hold values from -0.75 to 0.75
- w_gate: bfloat16 [1024, 4608], P('dp', 'tensor'), may hold values from -0.1875 to 0.1875
- w_up: bfloat16 [1024, 4608], P('dp', 'tensor'), may hold values from -0.1875 to 0.1875
- w_down: bfloat16 [4608, 1024], P('tensor', 'dp'), may hold values from -0.09375 to 0.09375
- attn_gain: bfloat16 [1024], P('dp'), may hold values from 0.5 to 1.5
- ffn_gain: bfloat16 [1024], P('dp'), may hold values from 0.5 to 1.5
- query_gain: bfloat16 [64], replicated, may hold values from 0.5 to 1.5
- key_gain: bfloat16 [64], replicated, may hold values from 0.5 to 1.5
- cotangent: bfloat16 [16384, 1024], P('dp'), may hold values from -6 to 6
Outputs:
- output: bfloat16 [16384, 1024], P('dp')
- grad_input: float32 [16384, 1024], P('dp')
- grad_query: float32 [1024, 1024], P('dp', 'tensor')
- grad_key: float32 [1024, 512], P('dp', 'tensor')
- grad_value: float32 [1024, 512], P('dp', 'tensor')
- grad_out: float32 [1024, 1024], P('tensor', 'dp')
- grad_gate: float32 [1024, 4608], P('dp', 'tensor')
- grad_up: float32 [1024, 4608], P('dp', 'tensor')
- grad_down: float32 [4608, 1024], P('tensor', 'dp')
- grad_attn_gain: float32 [1024], P('dp')
- grad_ffn_gain: float32 [1024], P('dp')
- grad_query_gain: float32 [64], replicated
- grad_key_gain: float32 [64], replicated
Inputs may be any that keep to these rules, and one draw needn't show every extreme that they name: `segment_ids`: within each row of 2048 tokens the numbers never fall; a document holds at most 1024 tokens, and some row holds one of exactly 1024; each row ends with a run of 1 to 128 pads, which form the row's last document and carry the number 8 + 2 * 2048 // 1024 + 2. `positions`: A token's place counted from the start of its document (pads from the start of the pad run). `pad_mask`: each row ends with a run of 1 to 128 pads.
All inputs are finite; a program needn't handle non-finite values.
Results may differ from a plain program's by a relative error of at most 0.02.
Values may be sent and summed in bfloat16 or wider, within the bound.
A program may use at most 256 MiB of HBM per device.

v0:
```python
import math

import jax
import jax.numpy as jnp
from jax import lax
from jax.sharding import PartitionSpec as P

HD = 64


EPSILON = 1e-05
THETA = 1000000.0
BIG_NEGATIVE = -1e30


def rms_norm(values, scales):
    return values * lax.rsqrt(jnp.mean(values * values, axis=-1, keepdims=True) + EPSILON) * scales


def rope_tables(position_ids):
    half_size = HD // 2
    inverse = THETA ** (-(jnp.arange(half_size).astype(jnp.float32) * 2.0 / HD))
    angles = position_ids.astype(jnp.float32)[:, None] * inverse[None, :]
    cos_half = jnp.cos(angles)
    sin_half = jnp.sin(angles)
    return (
        jnp.concatenate([cos_half, cos_half], axis=-1),
        jnp.concatenate([sin_half, sin_half], axis=-1),
    )


def rotate(values, cos_table, sin_table):
    half_size = values.shape[-1] // 2
    turned = jnp.concatenate([-values[..., half_size:], values[..., :half_size]], axis=-1)
    return values * cos_table + turned * sin_table


def swiglu(gate_in, up_in):
    return jax.nn.silu(gate_in) * up_in


def body(
    tokens,
    segment_ids,
    positions,
    pad_mask,
    w_query,
    w_key,
    w_value,
    w_out,
    w_gate,
    w_up,
    w_down,
    attn_gain,
    ffn_gain,
    query_gain,
    key_gain,
    cotangent,
):
    query_full, key_full, value_full, gate_full, up_full, attn_scale_b, ffn_scale_b = (
        lax.all_gather(w_query, "dp", axis=0, tiled=True),
        lax.all_gather(w_key, "dp", axis=0, tiled=True),
        lax.all_gather(w_value, "dp", axis=0, tiled=True),
        lax.all_gather(w_gate, "dp", axis=0, tiled=True),
        lax.all_gather(w_up, "dp", axis=0, tiled=True),
        lax.all_gather(attn_gain, "dp", axis=0, tiled=True),
        lax.all_gather(ffn_gain, "dp", axis=0, tiled=True),
    )
    out_full, down_full = (
        lax.all_gather(w_out, "dp", axis=1, tiled=True),
        lax.all_gather(w_down, "dp", axis=1, tiled=True),
    )
    attn_scales = attn_scale_b.astype(jnp.float32)
    ffn_scales = ffn_scale_b.astype(jnp.float32)
    query_scales = query_gain.astype(jnp.float32)
    key_scales = key_gain.astype(jnp.float32)
    seq_len = tokens.shape[0]
    block_len = min(512, seq_len)
    block_count = seq_len // block_len
    kv_heads = key_full.shape[1] // HD
    q_heads = query_full.shape[1] // HD
    repeat = q_heads // kv_heads
    score_scale = 1.0 / math.sqrt(HD)
    cos_table, sin_table = rope_tables(positions)

    def query_post(raw_values, scales):
        shaped = raw_values.reshape(seq_len, kv_heads, repeat, HD)
        return rotate(
            rms_norm(shaped, scales), cos_table[:, None, None, :], sin_table[:, None, None, :]
        )

    def key_post(raw_values, scales):
        shaped = raw_values.reshape(seq_len, kv_heads, HD)
        return rotate(rms_norm(shaped, scales), cos_table[:, None, :], sin_table[:, None, :])

    tokens32 = tokens.astype(jnp.float32)
    normed_one, norm_one_back = jax.vjp(rms_norm, tokens32, attn_scales)
    normed_one_b = normed_one.astype(jnp.bfloat16)
    raw_query = jnp.dot(normed_one_b, query_full, preferred_element_type=jnp.float32)
    raw_key = jnp.dot(normed_one_b, key_full, preferred_element_type=jnp.float32)
    raw_value = jnp.dot(normed_one_b, value_full, preferred_element_type=jnp.float32)
    query_vals, query_back = jax.vjp(query_post, raw_query, query_scales)
    key_vals, key_back = jax.vjp(key_post, raw_key, key_scales)
    query_b = query_vals.astype(jnp.bfloat16)
    key_b = key_vals.astype(jnp.bfloat16)
    value_b = raw_value.astype(jnp.bfloat16).reshape(seq_len, kv_heads, HD)
    token_place = jnp.arange(seq_len)
    key_open = pad_mask == 1

    def block_scores(block_index):
        row_start = block_index * block_len
        row_end = row_start + block_len
        rows_at = token_place[row_start:row_end]
        cols_at = token_place[:row_end]
        same_doc = segment_ids[row_start:row_end][:, None] == segment_ids[:row_end][None, :]
        causal = cols_at[None, :] <= rows_at[:, None]
        open_key = key_open[:row_end][None, :] | (cols_at[None, :] == rows_at[:, None])
        allowed = same_doc & causal & open_key
        raw_scores = (
            jnp.einsum(
                "qgrd,kgd->grqk",
                query_b[row_start:row_end],
                key_b[:row_end],
                preferred_element_type=jnp.float32,
            )
            * score_scale
        )
        return jnp.where(allowed[None, None], raw_scores, BIG_NEGATIVE)

    head_blocks = []
    lse_blocks = []
    for block_index in range(block_count):
        row_end = (block_index + 1) * block_len
        scores = block_scores(block_index)
        row_max = jnp.max(scores, axis=-1, keepdims=True)
        exp_scores = jnp.exp(scores - row_max)
        row_total = jnp.sum(exp_scores, axis=-1, keepdims=True)
        soft_weights = exp_scores / row_total
        lse_blocks.append(row_max + jnp.log(row_total))
        head_blocks.append(
            jnp.einsum(
                "grqk,kgd->qgrd",
                soft_weights.astype(jnp.bfloat16),
                value_b[:row_end],
                preferred_element_type=jnp.float32,
            )
        )
    heads_out = (
        jnp.concatenate(head_blocks, axis=0).reshape(seq_len, q_heads * HD).astype(jnp.bfloat16)
    )
    attn_total = lax.psum(
        jnp.dot(heads_out, out_full, preferred_element_type=jnp.float32).astype(jnp.bfloat16),
        "tensor",
    ).astype(jnp.float32)
    hidden_state = tokens32 + attn_total
    normed_two, norm_two_back = jax.vjp(rms_norm, hidden_state, ffn_scales)
    normed_two_b = normed_two.astype(jnp.bfloat16)
    gate_vals = jnp.dot(normed_two_b, gate_full, preferred_element_type=jnp.float32)
    up_vals = jnp.dot(normed_two_b, up_full, preferred_element_type=jnp.float32)
    act_vals, act_back = jax.vjp(swiglu, gate_vals, up_vals)
    hidden_b = act_vals.astype(jnp.bfloat16)
    ffn_total = lax.psum(
        jnp.dot(hidden_b, down_full, preferred_element_type=jnp.float32).astype(jnp.bfloat16),
        "tensor",
    ).astype(jnp.float32)
    output = (hidden_state + ffn_total).astype(jnp.bfloat16)
    query_use, key_use, value_use, gate_use, up_use = (
        lax.all_gather(w_query, "dp", axis=0, tiled=True),
        lax.all_gather(w_key, "dp", axis=0, tiled=True),
        lax.all_gather(w_value, "dp", axis=0, tiled=True),
        lax.all_gather(w_gate, "dp", axis=0, tiled=True),
        lax.all_gather(w_up, "dp", axis=0, tiled=True),
    )
    out_use, down_use = (
        lax.all_gather(w_out, "dp", axis=1, tiled=True),
        lax.all_gather(w_down, "dp", axis=1, tiled=True),
    )
    grad_f32 = cotangent.astype(jnp.float32)
    grad_down = jnp.einsum("sf,sd->fd", hidden_b, cotangent, preferred_element_type=jnp.float32)
    grad_hidden = jnp.einsum("sd,fd->sf", cotangent, down_use, preferred_element_type=jnp.float32)
    gate_grad, up_grad = act_back(grad_hidden)
    gate_grad_b = gate_grad.astype(jnp.bfloat16)
    up_grad_b = up_grad.astype(jnp.bfloat16)
    grad_gate = jnp.einsum(
        "sd,sf->df", normed_two_b, gate_grad_b, preferred_element_type=jnp.float32
    )
    grad_up = jnp.einsum("sd,sf->df", normed_two_b, up_grad_b, preferred_element_type=jnp.float32)
    ffn_input_part = jnp.einsum(
        "sf,df->sd", gate_grad_b, gate_use, preferred_element_type=jnp.float32
    ) + jnp.einsum("sf,df->sd", up_grad_b, up_use, preferred_element_type=jnp.float32)
    ffn_input_grad = lax.psum(ffn_input_part.astype(jnp.bfloat16), "tensor").astype(jnp.float32)
    state_norm_grad, grad_ffn_gain = norm_two_back(ffn_input_grad)
    state_grad = grad_f32 + state_norm_grad
    state_grad_b = state_grad.astype(jnp.bfloat16)
    grad_out = jnp.einsum("sk,sd->kd", heads_out, state_grad_b, preferred_element_type=jnp.float32)
    heads_grad = (
        jnp.einsum("sd,kd->sk", state_grad_b, out_use, preferred_element_type=jnp.float32)
        .astype(jnp.bfloat16)
        .reshape(seq_len, kv_heads, repeat, HD)
    )
    key_grad = jnp.zeros((seq_len, kv_heads, HD), jnp.float32)
    value_grad = jnp.zeros((seq_len, kv_heads, HD), jnp.float32)
    query_grad_blocks = []
    for block_index in range(block_count):
        row_start = block_index * block_len
        row_end = row_start + block_len
        scores = block_scores(block_index)
        soft_weights = jnp.exp(scores - lse_blocks[block_index])
        heads_block = heads_grad[row_start:row_end]
        weight_grad = jnp.einsum(
            "qgrd,kgd->grqk", heads_block, value_b[:row_end], preferred_element_type=jnp.float32
        )
        inner_sum = jnp.sum(soft_weights * weight_grad, axis=-1, keepdims=True)
        score_grad = (soft_weights * (weight_grad - inner_sum)).astype(jnp.bfloat16)
        query_grad_blocks.append(
            jnp.einsum(
                "grqk,kgd->qgrd", score_grad, key_b[:row_end], preferred_element_type=jnp.float32
            )
            * score_scale
        )
        key_grad = key_grad.at[:row_end].add(
            jnp.einsum(
                "grqk,qgrd->kgd",
                score_grad,
                query_b[row_start:row_end],
                preferred_element_type=jnp.float32,
            )
            * score_scale
        )
        value_grad = value_grad.at[:row_end].add(
            jnp.einsum(
                "grqk,qgrd->kgd",
                soft_weights.astype(jnp.bfloat16),
                heads_block,
                preferred_element_type=jnp.float32,
            )
        )
    query_grad = jnp.concatenate(query_grad_blocks, axis=0)
    raw_query_grad, query_gain_grad = query_back(query_grad)
    raw_key_grad, key_gain_grad = key_back(key_grad)
    query_grad_b = raw_query_grad.astype(jnp.bfloat16)
    key_grad_b = raw_key_grad.astype(jnp.bfloat16)
    value_grad_b = value_grad.reshape(seq_len, kv_heads * HD).astype(jnp.bfloat16)
    grad_query = jnp.einsum(
        "sd,sk->dk", normed_one_b, query_grad_b, preferred_element_type=jnp.float32
    )
    grad_key = jnp.einsum("sd,sk->dk", normed_one_b, key_grad_b, preferred_element_type=jnp.float32)
    grad_value = jnp.einsum(
        "sd,sk->dk", normed_one_b, value_grad_b, preferred_element_type=jnp.float32
    )
    attn_input_part = jnp.einsum(
        "sk,dk->sd", query_grad_b, query_use, preferred_element_type=jnp.float32
    )
    attn_input_part = attn_input_part + jnp.einsum(
        "sk,dk->sd", key_grad_b, key_use, preferred_element_type=jnp.float32
    )
    attn_input_part = attn_input_part + jnp.einsum(
        "sk,dk->sd", value_grad_b, value_use, preferred_element_type=jnp.float32
    )
    attn_input_grad = lax.psum(attn_input_part.astype(jnp.bfloat16), "tensor").astype(jnp.float32)
    token_norm_grad, grad_attn_gain = norm_one_back(attn_input_grad)
    grad_input = state_grad + token_norm_grad
    grad_query_gain, grad_key_gain = lax.psum((query_gain_grad, key_gain_grad), ("dp", "tensor"))
    row_grads = (
        lax.psum_scatter(grad_query, "dp", scatter_dimension=0, tiled=True),
        lax.psum_scatter(grad_key, "dp", scatter_dimension=0, tiled=True),
        lax.psum_scatter(grad_value, "dp", scatter_dimension=0, tiled=True),
        lax.psum_scatter(grad_gate, "dp", scatter_dimension=0, tiled=True),
        lax.psum_scatter(grad_up, "dp", scatter_dimension=0, tiled=True),
        lax.psum_scatter(grad_attn_gain, "dp", scatter_dimension=0, tiled=True),
        lax.psum_scatter(grad_ffn_gain, "dp", scatter_dimension=0, tiled=True),
    )
    column_grads = (
        lax.psum_scatter(grad_out, "dp", scatter_dimension=1, tiled=True),
        lax.psum_scatter(grad_down, "dp", scatter_dimension=1, tiled=True),
    )
    return (
        output,
        grad_input,
        row_grads[0],
        row_grads[1],
        row_grads[2],
        column_grads[0],
        row_grads[3],
        row_grads[4],
        column_grads[1],
        row_grads[5],
        row_grads[6],
        grad_query_gain,
        grad_key_gain,
    )


def solution(mesh):
    return jax.shard_map(
        body,
        mesh=mesh,
        in_specs=(
            P("dp", None),
            P("dp"),
            P("dp"),
            P("dp"),
            P("dp", "tensor"),
            P("dp", "tensor"),
            P("dp", "tensor"),
            P("tensor", "dp"),
            P("dp", "tensor"),
            P("dp", "tensor"),
            P("tensor", "dp"),
            P("dp"),
            P("dp"),
            P(),
            P(),
            P("dp", None),
        ),
        out_specs=(
            P("dp", None),
            P("dp", None),
            P("dp", "tensor"),
            P("dp", "tensor"),
            P("dp", "tensor"),
            P("tensor", "dp"),
            P("dp", "tensor"),
            P("dp", "tensor"),
            P("tensor", "dp"),
            P("dp"),
            P("dp"),
            P(),
            P(),
        ),
        check_vma=False,
    )
```

profile of v0, /device:TPU:0, one launch (start us, length us, event | category | flops | bytes accessed | tf_op | source)
XLA Modules:
  0.0 1193.3 jit_solution(8452105666874328358)
XLA Ops:
  9.9 22.5 %all-gather = bf16[8,1,128]{2,1,0:T(2,128)(2,1)S(1)} all-gather(bf16[1,1,128]{2,1,0:T(2,128)(2,1)} %bitcast.336), channel_id=1, replica_groups=mesh['dp'=8,'tensor'=4] {'dp'}, dimensions={0}, use_global_device_ids=true | all-gather | bytes 2304 | tf_op jit(solution)/shard_map/all_gather | solution.py:66
  35.5 31.0 %all_gather.35 = bf16[1024,128]{1,0:T(8,128)(2,1)S(1)} all-gather(bf16[128,128]{1,0:T(8,128)(2,1)} %param.42), channel_id=1, replica_groups=mesh['dp'=8,'tensor'=4] {'dp'}, dimensions={0}, use_global_device_ids=true | all-gather | bytes 294912 | tf_op jit(solution)/shard_map/all_gather | solution.py:63
  69.5 30.9 %all_gather.36 = bf16[1024,128]{1,0:T(8,128)(2,1)S(1)} all-gather(bf16[128,128]{1,0:T(8,128)(2,1)S(1)} %copy-done.59), channel_id=1, replica_groups=mesh['dp'=8,'tensor'=4] {'dp'}, dimensions={0}, use_global_device_ids=true | all-gather | bytes 294912 | tf_op jit(solution)/shard_map/all_gather | solution.py:62
  100.5 31.7 %all_gather.37 = bf16[1024,256]{1,0:T(8,128)(2,1)S(1)} all-gather(bf16[128,256]{1,0:T(8,128)(2,1)S(1)} %copy-done.55), channel_id=1, replica_groups=mesh['dp'=8,'tensor'=4] {'dp'}, dimensions={0}, use_global_device_ids=true | all-gather | bytes 589824 | tf_op jit(solution)/shard_map/all_gather | solution.py:61
  132.2 27.0 %all_gather.38 = bf16[256,1024]{1,0:T(8,128)(2,1)S(1)} all-gather(bf16[256,128]{1,0:T(8,128)(2,1)S(1)} %copy-done.56), channel_id=1, replica_groups=mesh['dp'=8,'tensor'=4] {'dp'}, dimensions={1}, use_global_device_ids=true | all-gather | bytes 589824 | tf_op jit(solution)/shard_map/all_gather | solution.py:70
  175.5 8.0 fusion.138
  191.8 8.0 fusion.3
  199.8 7.4 fusion.113
  213.4 16.7 %all-gather.1 = bf16[8,1,128]{2,1,0:T(2,128)(2,1)S(1)} all-gather(bf16[1,1,128]{2,1,0:T(2,128)(2,1)S(1)} %bitcast.337), channel_id=1, replica_groups=mesh['dp'=8,'tensor'=4] {'dp'}, dimensions={0}, use_global_device_ids=true | all-gather | bytes 2304 | tf_op jit(solution)/shard_map/all_gather | solution.py:67
  230.1 64.4 %all-reduce.15.cloned.1.call-done = bf16[2048,1024]{1,0:T(8,128)(2,1)} async-done(((bf16[2048,1024]{1,0:T(8,128)(2,1)}), bf16[2048,1024]{1,0:T(8,128)(2,1)}) %all-reduce.15.cloned.1.call-update) | async-done | bytes 4194320 | tf_op jit(solution)/shard_map/psum | solution.py:151
  294.5 5.0 multiply_reduce_fusion
  303.4 10.3 fusion.143
  315.6 10.3 fusion.142
  325.9 43.5 %all-gather.10.cloned.1.call-done = bf16[1152,1024]{1,0:T(8,128)(2,1)} async-done(((bf16[1152,128]{1,0:T(8,128)(2,1)}), bf16[1152,1024]{1,0:T(8,128)(2,1)}) %all-gather.10.cloned.1.call-update) | async-done | bytes 2359312 | tf_op jit(solution)/shard_map/all_gather | solution.py:71
  369.3 18.0 %multiply_convert_fusion = (bf16[2048,1152]{1,0:T(8,128)(2,1)}, bf16[2048,1152]{1,0:T(8,128)(2,1)}, bf16[2048,1152]{1,0:T(8,128)(2,1)}) fusion(f32[2048,1152]{1,0:T(8,128)} %fusion.142, f32[2048,1152]{1,0:T(8,128)} %fusion.143, bf16[2048,1024]{1,0:T(8,128)(2,1)} %param.51, bf16[1152,1024]{1,0:T(8,128)(2,1)} %all-gather.10.cloned.1.call-done), kind=kOutput, calls=%fused_computation.41 | convolution fusion | flops 4869586944 | bytes 39583744 | tf_op jit(solution)/shard_map/sd,fd->sf/dot_general | solution.py:180
  387.4 7.7 fusion.144
  395.0 7.7 add_convert_fusion.1
  402.9 9.5 convolution_convert_fusion
  412.4 74.2 %all-reduce.17.cloned.1.call-done = bf16[2048,1024]{1,0:T(8,128)(2,1)} async-done(((bf16[2048,1024]{1,0:T(8,128)(2,1)}), bf16[2048,1024]{1,0:T(8,128)(2,1)}) %all-reduce.17.cloned.1.call-update) | async-done | bytes 4194320 | tf_op jit(solution)/shard_map/psum | solution.py:191
  486.6 8.7 fusion.20
  495.4 5.4 fusion.22
  513.5 5.7 fusion.28
  520.8 10.9 fusion.5
  531.6 7.5 fusion.67
  539.2 8.3 fusion
  551.4 4.5 fusion.146
  555.9 8.9 fusion.30
  564.8 4.5 fusion.96
  571.7 9.6 fusion.7
  581.4 4.1 fusion.86
  589.0 8.1 fusion.2
  601.9 6.2 broadcast_multiply_fusion
  619.3 4.3 fusion.149
  623.6 5.1 fusion.148
  628.8 5.8 fusion.81
  635.0 4.5 fusion.147
  639.6 9.8 fusion.152
  649.4 10.3 fusion.151
  659.8 10.6 fusion.150
  672.3 40.4 %all-reduce.8 = (f32[64]{0:T(128)}, f32[64]{0:T(128)}) all-reduce(f32[64]{0:T(128)S(1)} %get-tuple-element.129, f32[64]{0:T(128)S(1)} %get-tuple-element.131), channel_id=1, replica_groups=mesh['dp'=8,'tensor'=4] {'dp','tensor'}, use_global_device_ids=true, to_apply=%region_36.37 | all-reduce | flops 128 | bytes 1024 | tf_op jit(solution)/shard_map/psum | solution.py:263
  712.7 61.0 %all-reduce.19.cloned.1.call-done = (bf16[2048,1024]{1,0:T(8,128)(2,1)}, bf16[2048,1024]{1,0:T(8,128)(2,1)}) async-done(((bf16[2048,1024]{1,0:T(8,128)(2,1)}, bf16[2048,1024]{1,0:T(8,128)(2,1)}), (bf16[2048,1024]{1,0:T(8,128)(2,1)}, bf16[2048,1024]{1,0:T(8,128)(2,1)})) %all-reduce.19.cloned.1.call-update) | async-done | bytes 8388624 | tf_op jit(solution)/shard_map/psum | solution.py:162
  773.7 5.7 fusion.21
  779.5 21.7 %all-reduce.9 = (f32[1024]{0:T(1024)S(1)}, f32[1024]{0:T(1024)S(1)}) all-reduce(f32[1024]{0:T(1024)S(1)} %get-tuple-element.127, f32[1024]{0:T(1024)S(1)} %copy-done.63), channel_id=9, replica_groups=mesh['dp'=8,'tensor'=4] {'dp'}, use_global_device_ids=true, to_apply=%region_32.33.clone | all-reduce | flops 2048 | bytes 16384
  802.4 15.0 %fusion.23 = (f32[2048,1024]{1,0:T(8,128)}, bf16[2048,1024]{1,0:T(8,128)(2,1)}) fusion(f32[2048,1024]{1,0:T(8,128)} %copy-done.4, bf16[2048,1024]{1,0:T(8,128)(2,1)} %get-tuple-element.138, bf16[2048,1024]{1,0:T(8,128)(2,1)} %param.36, f32[2048]{0:T(1024)S(1)} %multiply_multiply_fusion.4, f32[1024]{0:T(1024)S(1)} %bitcast.331, f32[2048]{0:T(1024)S(1)} %copy-done.47, ...), kind=kLoop, calls=%fused_computation.50 | loop fusion | flops 27262976 | bytes 37769216 | tf_op jit(solution)/shard_map/add | solution.py:262
  820.3 67.2 %reduce-scatter.8.cloned.1.call-done = f32[128,256]{1,0:T(8,128)} async-done(((f32[1024,256]{1,0:T(8,128)}), f32[128,256]{1,0:T(8,128)}) %reduce-scatter.8.cloned.1.call-update) | async-done | bytes 131088 | tf_op jit(solution)/shard_map/reduce_scatter | solution.py:265
  887.5 99.2 %reduce-scatter.20.cloned.1.call-done = f32[1152,128]{1,0:T(8,128)} async-done(((f32[1152,1024]{1,0:T(8,128)}), f32[1152,128]{1,0:T(8,128)}) %reduce-scatter.20.cloned.1.call-update) | async-done | bytes 589840 | tf_op jit(solution)/shard_map/reduce_scatter | solution.py:275
  986.7 99.4 %reduce-scatter.18.cloned.1.call-done = f32[128,1152]{1,0:T(8,128)} async-done(((f32[1024,1152]{1,0:T(8,128)}), f32[128,1152]{1,0:T(8,128)}) %reduce-scatter.18.cloned.1.call-update) | async-done | bytes 589840 | tf_op jit(solution)/shard_map/reduce_scatter | solution.py:269
  1086.1 99.6 %reduce-scatter.16.cloned.1.call-done = f32[128,1152]{1,0:T(8,128)} async-done(((f32[1024,1152]{1,0:T(8,128)}), f32[128,1152]{1,0:T(8,128)}) %reduce-scatter.16.cloned.1.call-update) | async-done | bytes 589840 | tf_op jit(solution)/shard_map/reduce_scatter | solution.py:268
  (298 shorter events, 89.4 us)
Async XLA Ops:
  8.0 286.5 %all-reduce.15.cloned.1.call-start = ((), (), s32[]{:S(2)}) async-start(), calls=%async_computation.7 | async-start | bytes 8388608 | tf_op jit(solution)/shard_map/psum | solution.py:151
  8.1 58.5 %copy-start = (bf16[2048,1024]{1,0:T(8,128)(2,1)S(1)}, bf16[2048,1024]{1,0:T(8,128)(2,1)}, u32[]{:S(2)}) copy-start(bf16[2048,1024]{1,0:T(8,128)(2,1)} %param.36) | copy-start | bytes 12582916
  8.9 58.8 %copy-start.61 = (pred[2048]{0:T(1024)(128)(4,1)}, pred[2048]{0:T(1024)(128)(4,1)S(1)}, u32[]{:S(2)}) copy-start(pred[2048]{0:T(1024)(128)(4,1)S(1)} %broadcast_compare_fusion) | copy-start | bytes 6148
  32.4 35.3 %copy-start.53 = (f32[8,1,128]{2,1,0:T(1,128)}, f32[8,1,128]{2,1,0:T(1,128)S(1)}, u32[]{:S(2)}) copy-start(f32[8,1,128]{2,1,0:T(1,128)S(1)} %convert_element_type.189) | copy-start | bytes 12292
  35.5 31.1 %copy-start.51 = (f32[2048]{0:T(1024)}, f32[2048]{0:T(1024)S(1)}, u32[]{:S(2)}) copy-start(f32[2048]{0:T(1024)S(1)} %fusion.26) | copy-start | bytes 24580
  35.5 31.0 %copy-start.46 = (f32[2048]{0:T(1024)}, f32[2048]{0:T(1024)S(1)}, u32[]{:S(2)}) copy-start(f32[2048]{0:T(1024)S(1)} %fusion.132) | copy-start | bytes 24580
  67.7 93.4 %copy-start.6 = (bf16[2048,1024]{1,0:T(8,128)(2,1)}, bf16[2048,1024]{1,0:T(8,128)(2,1)S(1)}, u32[]{:S(2)}) copy-start(bf16[2048,1024]{1,0:T(8,128)(2,1)S(1)} %fusion.18) | copy-start | bytes 12582916
  67.8 32.7 %copy-start.55 = (bf16[128,256]{1,0:T(8,128)(2,1)S(1)}, bf16[128,256]{1,0:T(8,128)(2,1)}, u32[]{:S(2)}) copy-start(bf16[128,256]{1,0:T(8,128)(2,1)} %param.40) | copy-start | bytes 196612
  67.8 64.4 %copy-start.56 = (bf16[256,128]{1,0:T(8,128)(2,1)S(1)}, bf16[256,128]{1,0:T(8,128)(2,1)}, u32[]{:S(2)}) copy-start(bf16[256,128]{1,0:T(8,128)(2,1)} %param.43) | copy-start | bytes 196612
  69.3 114.8 %copy-start.40 = (bf16[512,128]{0,1:T(8,128)(2,1)}, bf16[512,128]{0,1:T(8,128)(2,1)S(1)}, u32[]{:S(2)}) copy-start(bf16[512,128]{0,1:T(8,128)(2,1)S(1)} %slice.388) | copy-start | bytes 393220
  69.4 116.8 %copy-start.36 = (bf16[1024,128]{0,1:T(8,128)(2,1)}, bf16[1024,128]{0,1:T(8,128)(2,1)S(1)}, u32[]{:S(2)}) copy-start(bf16[1024,128]{0,1:T(8,128)(2,1)S(1)} %slice.396) | copy-start | bytes 786436
  69.4 119.9 %copy-start.34 = (bf16[1536,128]{0,1:T(8,128)(2,1)}, bf16[1536,128]{0,1:T(8,128)(2,1)S(1)}, u32[]{:S(2)}) copy-start(bf16[1536,128]{0,1:T(8,128)(2,1)S(1)} %slice.400) | copy-start | bytes 1179652
  69.5 95.3 %copy-start.64 = (f32[64]{0:T(128)}, f32[64]{0:T(128)S(1)}, u32[]{:S(2)}) copy-start(f32[64]{0:T(128)S(1)} %convert_element_type.151) | copy-start | bytes 772
  69.5 94.8 %copy-start.67 = (f32[64]{0:T(128)}, f32[64]{0:T(128)S(1)}, u32[]{:S(2)}) copy-start(f32[64]{0:T(128)S(1)} %convert_element_type.147) | copy-start | bytes 772
  100.5 60.3 %copy-start.31 = (bf16[1024,128]{1,0:T(8,128)(2,1)}, bf16[1024,128]{1,0:T(8,128)(2,1)S(1)}, u32[]{:S(2)}) copy-start(bf16[1024,128]{1,0:T(8,128)(2,1)S(1)} %all_gather.36) | copy-start | bytes 786436
  132.2 29.0 %copy-start.32 = (bf16[1024,256]{1,0:T(8,128)(2,1)}, bf16[1024,256]{1,0:T(8,128)(2,1)S(1)}, u32[]{:S(2)}) copy-start(bf16[1024,256]{1,0:T(8,128)(2,1)S(1)} %all_gather.37) | copy-start | bytes 1572868
  164.7 10.8 copy-start.25
  165.5 10.0 copy-start.28
  166.9 17.3 %copy-start.10 = (f32[2,2,512,512]{2,3,1,0:T(8,128)}, f32[2,2,512,512]{2,3,1,0:T(8,128)S(1)}, u32[]{:S(2)}) copy-start(f32[2,2,512,512]{2,3,1,0:T(8,128)S(1)} %get-tuple-element.175) | copy-start | bytes 12582916
  169.8 16.4 %copy-start.5 = (f32[2,2,512,1024]{2,3,1,0:T(8,128)}, f32[2,2,512,1024]{2,3,1,0:T(8,128)S(1)}, u32[]{:S(2)}) copy-start(f32[2,2,512,1024]{2,3,1,0:T(8,128)S(1)} %get-tuple-element.173) | copy-start | bytes 25165828
  173.7 15.7 %copy-start.3 = (f32[2,2,512,1536]{2,3,1,0:T(8,128)}, f32[2,2,512,1536]{2,3,1,0:T(8,128)S(1)}, u32[]{:S(2)}) copy-start(f32[2,2,512,1536]{2,3,1,0:T(8,128)S(1)} %get-tuple-element.171) | copy-start | bytes 37748740
  211.6 91.8 %all-gather.8.cloned.1.call-start = ((), (), s32[]{:S(2)}) async-start(), calls=%async_computation.9 | async-start | bytes 2654208 | tf_op jit(solution)/shard_map/all_gather | solution.py:65
  212.2 103.4 %all-gather.6.cloned.1.call-start = ((), (), s32[]{:S(2)}) async-start(), calls=%async_computation.8 | async-start | bytes 2654208 | tf_op jit(solution)/shard_map/all_gather | solution.py:64
  212.8 156.6 %all-gather.10.cloned.1.call-start = ((), (), s32[]{:S(2)}) async-start(), calls=%async_computation.10 | async-start | bytes 2654208 | tf_op jit(solution)/shard_map/all_gather | solution.py:71
  213.4 273.3 %all-reduce.17.cloned.1.call-start = ((), (), s32[]{:S(2)}) async-start(), calls=%async_computation.11 | async-start | bytes 8388608 | tf_op jit(solution)/shard_map/psum | solution.py:191
  369.3 18.0 %copy-start.71 = (bf16[1024,1152]{1,0:T(8,128)(2,1)S(1)}, bf16[1024,1152]{1,0:T(8,128)(2,1)}, u32[]{:S(2)}) copy-start(bf16[1024,1152]{1,0:T(8,128)(2,1)} %all-gather.6.cloned.1.call-done) | copy-start | bytes 7077892
  387.3 7.7 copy-start.75
  402.8 370.9 %all-reduce.19.cloned.1.call-start = ((), (), s32[]{:S(2)}) async-start(), calls=%async_computation.19 | async-start | bytes 16777216 | tf_op jit(solution)/shard_map/psum | solution.py:162
  486.6 8.8 copy-start.2
  486.6 8.8 copy-start.8
  486.6 8.8 copy-start.20
  520.7 18.4 %slice-start = ((s8[16777216]{0:T(1024)(128)(4,1)}), s8[4194304]{0:T(1024)(128)(4,1)S(1)}, s32[]{:S(2)}) async-start(s8[16777216]{0:T(1024)(128)(4,1)} %bitcast.294), calls=%async_computation.20 | async-start | bytes 8388608
  520.7 18.4 %slice-start.1 = ((s8[16777216]{0:T(1024)(128)(4,1)}), s8[4194304]{0:T(1024)(128)(4,1)S(1)}, s32[]{:S(2)}) async-start(s8[16777216]{0:T(1024)(128)(4,1)} %bitcast.294), calls=%async_computation.21 | async-start | bytes 8388608
  520.7 18.4 %slice-start.2 = ((s8[16777216]{0:T(1024)(128)(4,1)}), s8[4194304]{0:T(1024)(128)(4,1)S(1)}, s32[]{:S(2)}) async-start(s8[16777216]{0:T(1024)(128)(4,1)} %bitcast.294), calls=%async_computation.22 | async-start | bytes 8388608
  555.9 15.8 %slice-start.4 = ((s8[12582912]{0:T(1024)(128)(4,1)}), s8[4194304]{0:T(1024)(128)(4,1)S(1)}, s32[]{:S(2)}) async-start(s8[12582912]{0:T(1024)(128)(4,1)} %bitcast.296), calls=%async_computation.24 | async-start | bytes 8388608
  555.9 15.8 %slice-start.5 = ((s8[12582912]{0:T(1024)(128)(4,1)}), s8[4194304]{0:T(1024)(128)(4,1)S(1)}, s32[]{:S(2)}) async-start(s8[12582912]{0:T(1024)(128)(4,1)} %bitcast.296), calls=%async_computation.25 | async-start | bytes 8388608
  555.9 15.8 %slice-start.6 = ((s8[12582912]{0:T(1024)(128)(4,1)}), s8[4194304]{0:T(1024)(128)(4,1)S(1)}, s32[]{:S(2)}) async-start(s8[12582912]{0:T(1024)(128)(4,1)} %bitcast.296), calls=%async_computation.26 | async-start | bytes 8388608
  619.2 198.2 %reduce-scatter.12.cloned.1.call-start = ((), (), s32[]{:S(2)}) async-start(), calls=%async_computation.14 | async-start | bytes 589824 | tf_op jit(solution)/shard_map/reduce_scatter | solution.py:267
  623.6 193.9 %reduce-scatter.10.cloned.1.call-start = ((), (), s32[]{:S(2)}) async-start(), calls=%async_computation.13 | async-start | bytes 589824 | tf_op jit(solution)/shard_map/reduce_scatter | solution.py:266
  628.8 191.5 %reduce-scatter.14.cloned.1.call-start = ((), (), s32[]{:S(2)}) async-start(), calls=%async_computation.15 | async-start | bytes 1179648 | tf_op jit(solution)/shard_map/reduce_scatter | solution.py:274
  634.7 252.8 %reduce-scatter.8.cloned.1.call-start = ((), (), s32[]{:S(2)}) async-start(), calls=%async_computation.12 | async-start | bytes 1179648 | tf_op jit(solution)/shard_map/reduce_scatter | solution.py:265
  639.5 347.2 %reduce-scatter.20.cloned.1.call-start = ((), (), s32[]{:S(2)}) async-start(), calls=%async_computation.18 | async-start | bytes 5308416 | tf_op jit(solution)/shard_map/reduce_scatter | solution.py:275
  649.4 436.7 %reduce-scatter.18.cloned.1.call-start = ((), (), s32[]{:S(2)}) async-start(), calls=%async_computation.17 | async-start | bytes 5308416 | tf_op jit(solution)/shard_map/reduce_scatter | solution.py:269
  659.8 525.9 %reduce-scatter.16.cloned.1.call-start = ((), (), s32[]{:S(2)}) async-start(), calls=%async_computation.16 | async-start | bytes 5308416 | tf_op jit(solution)/shard_map/reduce_scatter | solution.py:268
  670.4 103.3 %copy-start.47 = (f32[2048]{0:T(1024)S(1)}, f32[2048]{0:T(1024)}, u32[]{:S(2)}) copy-start(f32[2048]{0:T(1024)} %copy-done.46) | copy-start | bytes 24580
  670.4 103.3 %copy-start.54 = (f32[8,1,128]{2,1,0:T(1,128)S(1)}, f32[8,1,128]{2,1,0:T(1,128)}, u32[]{:S(2)}) copy-start(f32[8,1,128]{2,1,0:T(1,128)} %copy-done.53) | copy-start | bytes 12292
  670.4 109.0 %copy-start.63 = (f32[1024]{0:T(1024)S(1)}, f32[1024]{0:T(1024)}, u32[]{:S(2)}) copy-start(f32[1024]{0:T(1024)} %get-tuple-element.125) | copy-start | bytes 12292
  670.4 131.9 %copy-start.52 = (f32[2048]{0:T(1024)S(1)}, f32[2048]{0:T(1024)}, u32[]{:S(2)}) copy-start(f32[2048]{0:T(1024)} %copy-done.51) | copy-start | bytes 24580
  (55 other events, 177.3 us)
Sparse Core Ops, SparseCore 0:
  211.7 82.7 all-reduce.14
  402.9 83.6 all-reduce.16
  619.4 154.3 all-reduce.18
Sparse Core Ops, SparseCore 1:
  214.3 48.9 all-gather.7
  265.3 50.2 all-gather.5
  317.5 51.8 all-gather.9
  623.9 62.7 reduce-scatter.11
  690.6 61.6 reduce-scatter.9
  756.3 63.9 reduce-scatter.13
  824.1 63.3 reduce-scatter.7
  891.6 95.1 reduce-scatter.19
  990.8 95.3 reduce-scatter.17
  1090.4 95.3 reduce-scatter.15
where the time goes:
time: 1200 us; the launch traced here: 1190 us
  waiting for transfers between devices  615 us (51%)
  matrix products  223 us (19%)
  blocking collectives  222 us (18%)
  other arithmetic  99.4 us (8%)
  between operations  18 us (2%)
  local copies, waits for them, and re-layouts  15.5 us (1%)
    reduce_scatter x1, waiting for transfers between devices, body(): lax.psum_scatter(grad_gate, 'dp', scatter_dimension=0, tiled=True)  99.6 us
    reduce_scatter x1, waiting for transfers between devices, body(): lax.psum_scatter(grad_up, 'dp', scatter_dimension=0, tiled=True)  99.4 us
    reduce_scatter x1, waiting for transfers between devices, body(): lax.psum_scatter(grad_down, 'dp', scatter_dimension=1, tiled=True)  99.2 us
    psum x1, waiting for transfers between devices, body(): lax.psum(ffn_input_part.astype(jnp.bfloat16), 'tensor').astype(jnp.float32)  74.2 us
    reduce_scatter x1, waiting for transfers between devices, body(): lax.psum_scatter(grad_query, 'dp', scatter_dimension=0, tiled=True)  67.2 us
    psum x1, waiting for transfers between devices, body(): lax.psum(jnp.dot(heads_out, out_full, preferred_element_type=jnp.float32)...  64.4 us
    psum x1, waiting for transfers between devices, body(): lax.psum(jnp.dot(hidden_b, down_full, preferred_element_type=jnp.float32)...  61 us
    all_gather x1, waiting for transfers between devices, body(): lax.all_gather(w_down, 'dp', axis=1, tiled=True)  43.5 us
  transfers between devices with their start and end apart: 13, of which 10 were waited for; matrix products, arithmetic and copies ran while one was open for 9% of the time, Pallas kernels for 0%

commit v1 on v0

v1 whole, which is shorter than its diff:
```python
import functools
import math

import jax
import jax.numpy as jnp
from jax import lax
from jax.experimental import pallas as pl
from jax.experimental.pallas import tpu as pltpu
from jax.sharding import PartitionSpec as P

HD = 64
EPSILON = 1e-05
THETA = 1000000.0
BIG_NEGATIVE = -1e30
CHUNKS = 4
BLK = 256
F32 = jnp.float32
BF16 = jnp.bfloat16
SCALE = 1.0 / math.sqrt(HD)
EXP2_SCALE = SCALE * math.log2(math.e)
NT = (((1,), (1,)), ((), ()))
ANY = pl.BlockSpec(memory_space=pl.ANY)


def sds(shape, dtype):
    return jax.ShapeDtypeStruct(shape, dtype)


def whole(shape):
    return pl.BlockSpec(shape, lambda i, *s: (0,) * len(shape))


def dot(left, right):
    return jnp.dot(left, right, preferred_element_type=F32)


def dot_nt(left, right):
    return lax.dot_general(left, right, NT, preferred_element_type=F32)


def cost(micros):
    return pl.CostEstimate(flops=0, bytes_accessed=int(micros * 3.4e6), transcendentals=0)


def after(value, *others):
    return lax.optimization_barrier((value, others))[0]


def params():
    return pltpu.CompilerParams(
        dimension_semantics=("arbitrary",), vmem_limit_bytes=56 * 1024 * 1024
    )


def low_half(shape, period):
    lane = lax.broadcasted_iota(jnp.int32, shape, 1)
    return lax.rem(lane, period) < period // 2


def swap_halves(values):
    left = pltpu.roll(values, 128 - HD // 2, 1)
    right = pltpu.roll(values, HD // 2, 1)
    return jnp.where(low_half(values.shape, HD), left, right)


def pair_mean(values):
    first = low_half(values.shape, 2 * HD)
    low = jnp.sum(jnp.where(first, values, 0.0), axis=1, keepdims=True)
    high = jnp.sum(jnp.where(first, 0.0, values), axis=1, keepdims=True)
    return jnp.where(first, low, high) * (1.0 / HD)


def head_pads(slab, group):
    first = low_half(slab.shape, 2 * HD)
    rolled = pltpu.roll(slab, HD, 1)
    if group == 0:
        pieces = (jnp.where(first, slab, 0.0), jnp.where(first, rolled, 0.0))
    else:
        pieces = (jnp.where(first, 0.0, rolled), jnp.where(first, 0.0, slab))
    return jnp.concatenate(pieces, axis=0).astype(BF16)


def qkv_kernel(
    x_ref, gain_ref, w_ref, cos_ref, sin_ref, qgain_ref, kgain_ref,
    xn_ref, z_ref, q_ref, k_ref, v_ref, kt_ref, vt_ref,
):
    x = x_ref[...].astype(F32)
    rstd = lax.rsqrt(jnp.mean(x * x, axis=1, keepdims=True) + EPSILON)
    xn = (x * rstd * gain_ref[...]).astype(BF16)
    xn_ref[...] = xn
    z = dot(xn, w_ref[...])
    z_ref[...] = z[:, :384]
    cos, sin = cos_ref[...], sin_ref[...]

    def post(values, gain):
        normed = values * lax.rsqrt(pair_mean(values * values) + EPSILON) * gain
        return normed * cos + swap_halves(normed) * sin

    for group in range(2):
        slab = post(z[:, group * 128:(group + 1) * 128], qgain_ref[...])
        q_ref[0, group] = head_pads(slab, group)
    keys = post(z[:, 256:384], kgain_ref[...])
    k_ref[...] = keys.astype(BF16)
    kt_ref[...] = keys.T.astype(BF16)
    values = z[:, 384:512]
    v_ref[...] = values.astype(BF16)
    values_t = values.T.astype(BF16)
    rows = lax.broadcasted_iota(jnp.int32, (16, BLK), 0)
    ones = jnp.where(rows == 0, 1.0, 0.0).astype(BF16)
    for group in range(2):
        vt_ref[group, 0:HD, :] = values_t[group * HD:(group + 1) * HD]
        vt_ref[group, HD:HD + 16, :] = ones


def qkv_call(x, gain, w, cos, sin, qgain, kgain):
    seq, width = x.shape
    blocks = seq // BLK
    row = lambda n: pl.BlockSpec((BLK, n), lambda i: (i, 0))
    return pl.pallas_call(
        qkv_kernel,
        grid=(blocks,),
        in_specs=[
            row(width), whole((1, width)), pl.BlockSpec((width, 512), lambda i: (0, 0)),
            row(128), row(128), whole((1, 128)), whole((1, 128)),
        ],
        out_specs=[
            row(width), row(384),
            pl.BlockSpec((1, 2, 2 * BLK, 128), lambda i: (i, 0, 0, 0)),
            row(128), row(128),
            pl.BlockSpec((128, BLK), lambda i: (0, i)),
            pl.BlockSpec((2, HD + 16, BLK), lambda i: (0, 0, i)),
        ],
        out_shape=[
            sds((seq, width), BF16), sds((seq, 384), F32),
            sds((blocks, 2, 2 * BLK, 128), BF16),
            sds((seq, 128), BF16), sds((seq, 128), BF16),
            sds((128, seq), BF16), sds((2, HD + 16, seq), BF16),
        ],
        compiler_params=params(),
        cost_estimate=cost(12),
        name="qkv",
    )(x, gain, w, cos, sin, qgain, kgain)


class Order:
    def __init__(self, chunk, half, descending):
        self.chunk, self.half, self.descending = chunk, half, descending

    def local(self, i, core):
        half = self.half
        if self.descending:
            return 2 * half - 1 - i
        first = i < half
        base = jnp.where(first, (1 - core) * half, core * half)
        return base + jnp.where(first, i, i - half)

    def block(self, i, core):
        return self.chunk * 2 * self.half + self.local(i, core)

    def is_send(self, i, core):
        if self.descending:
            return jnp.where(core == 0, i < self.half, i >= self.half)
        return i < self.half

    def send(self, i, core):
        half = self.half
        if self.descending:
            return jnp.where(core == 0, jnp.maximum(half - 1 - i, 0), jnp.minimum(half - 1, 2 * half - 1 - i))
        return jnp.minimum(i, half - 1)

    def keep(self, i, core):
        half = self.half
        if self.descending:
            return self.send(i, 1 - core)
        return jnp.maximum(i - half, 0)


def order_specs(order):
    row = lambda n: pl.BlockSpec((BLK, n), lambda i, c, *s: (order.block(i, c[0]), 0))
    local = lambda n: pl.BlockSpec((BLK, n), lambda i, c, *s: (order.local(i, c[0]), 0))
    send = lambda n: pl.BlockSpec((BLK, n), lambda i, c, *s: (order.send(i, c[0]), 0))
    keep = lambda n: pl.BlockSpec((BLK, n), lambda i, c, *s: (order.keep(i, c[0]), 0))
    return row, local, send, keep


def put(is_send, send_ref, keep_ref, value):
    @pl.when(is_send)
    def _():
        send_ref[...] = value

    @pl.when(jnp.logical_not(is_send))
    def _():
        keep_ref[...] = value


def attn_kernel(order, n_prev, core_ref, lo_ref, q_ref, k_ref, vt_ref, start_ref, wo_ref, *rest):
    rest = rest[n_prev:]
    o_ref, lse_ref, send_ref, keep_ref, acc_ref = rest
    i = pl.program_id(0)
    core = core_ref[0]
    block = order.block(i, core)
    start = start_ref[0]
    key_place = lax.broadcasted_iota(jnp.int32, (BLK, 2 * BLK), 0)
    acc_ref[...] = jnp.zeros_like(acc_ref)

    def step(kb, diagonal):
        at = pl.multiple_of(kb * BLK, BLK)
        keys = k_ref[pl.ds(at, BLK), :]
        allowed = key_place >= start - at
        if diagonal:
            lane = lax.broadcasted_iota(jnp.int32, (BLK, 2 * BLK), 1)
            allowed = allowed & (key_place <= lax.rem(lane, BLK))
        for group in range(2):
            scores = dot_nt(keys, q_ref[0, group]) * EXP2_SCALE
            probs = jnp.exp2(jnp.where(allowed, scores, BIG_NEGATIVE)).astype(BF16)
            acc_ref[group] += dot(vt_ref[group, :, pl.ds(at, BLK)], probs)

    def loop_body(kb, carry):
        step(kb, False)
        return carry

    lax.fori_loop(lo_ref[block], block, loop_body, 0)
    step(block, True)
    parts = []
    for group in range(2):
        total = acc_ref[group, HD:HD + 1, :]
        lse_ref[0, group:group + 1, :] = jnp.log2(total)
        heads = acc_ref[group, 0:HD, :] / total
        parts += [heads[:, :BLK], heads[:, BLK:]]
    out = jnp.concatenate(parts, axis=0).T.astype(BF16)
    o_ref[...] = out
    put(order.is_send(i, core), send_ref, keep_ref, dot_nt(out, wo_ref[...]).astype(BF16))


def attn_call(chunk, half, core, lo, q, k, vt, start, w, previous):
    seq = k.shape[0]
    width = w.shape[0]
    blocks = seq // BLK
    order = Order(chunk, half, False)
    row, _, send, keep = order_specs(order)
    n_prev = len(previous)
    by_block = lambda *tail: pl.BlockSpec((1,) + tail, lambda i, c, *s: (order.block(i, c[0]),) + (0,) * len(tail))
    return pl.pallas_call(
        functools.partial(attn_kernel, order, n_prev),
        grid_spec=pltpu.PrefetchScalarGridSpec(
            num_scalar_prefetch=2,
            grid=(2 * half,),
            in_specs=[
                by_block(2, 2 * BLK, 128), whole((seq, 128)), whole((2, HD + 16, seq)),
                by_block(1, 2 * BLK),
                pl.BlockSpec((width, 256), lambda i, *s: (0, 2)),
            ] + [ANY] * n_prev,
            out_specs=[row(256), by_block(2, 2 * BLK), send(width), keep(width)],
            scratch_shapes=[pltpu.VMEM((2, HD + 16, 2 * BLK), F32)],
        ),
        out_shape=[
            sds((seq, 256), BF16), sds((blocks, 2, 2 * BLK), F32),
            sds((half * BLK, width), BF16), sds((half * BLK, width), BF16),
        ],
        input_output_aliases={7 + j: j for j in range(n_prev)},
        compiler_params=params(),
        cost_estimate=cost(3.5 * 2 * half),
        name=f"attn_{chunk}",
    )(core, lo, q, k, vt, start, w, *previous)


def ffn_kernel(order, n_prev, hidden, core_ref, x_ref, own_ref, got_ref, g_ref, gain_ref, w_ref, *rest):
    rest = rest[n_prev:]
    xn_ref, dgu_ref, hid_ref, dsend_ref, dkeep_ref, ysend_ref, ykeep_ref = rest
    i = pl.program_id(0)
    is_send = order.is_send(i, core_ref[0])
    total = jnp.where(is_send, got_ref[...].astype(F32), own_ref[...].astype(F32))
    h = x_ref[...].astype(F32) + total
    rstd = lax.rsqrt(jnp.mean(h * h, axis=1, keepdims=True) + EPSILON)
    xn = (h * rstd * gain_ref[...]).astype(BF16)
    xn_ref[...] = xn
    gate_up = dot(xn, w_ref[:, :2 * hidden])
    gate, up = gate_up[:, :hidden], gate_up[:, hidden:]
    dhid = dot(g_ref[...], w_ref[:, 2 * hidden:])
    sig = 1.0 / (1.0 + jnp.exp(-gate))
    act = gate * sig
    hid = (act * up).astype(BF16)
    hid_ref[...] = hid
    dgate = (dhid * up * (sig * (1.0 + gate * (1.0 - sig)))).astype(BF16)
    dup = (dhid * act).astype(BF16)
    dgu_ref[:, :hidden] = dgate
    dgu_ref[:, hidden:] = dup
    dxn = dot_nt(dgu_ref[...], w_ref[:, :2 * hidden])
    put(is_send, dsend_ref, dkeep_ref, dxn.astype(BF16))
    put(is_send, ysend_ref, ykeep_ref, dot_nt(hid, w_ref[:, 2 * hidden:]).astype(BF16))


def ffn_call(chunk, half, core, x, own, got, g, gain, w, previous, y_previous):
    seq, width = x.shape
    hidden = w.shape[1] // 3
    order = Order(chunk, half, False)
    row, _, send, keep = order_specs(order)
    n_prev = len(previous) + len(y_previous)
    rows = half * BLK
    y_at = (chunk % 2) * half
    y_send = pl.BlockSpec((BLK, width), lambda i, c, *s: (y_at + order.send(i, c[0]), 0))
    y_keep = pl.BlockSpec((BLK, width), lambda i, c, *s: (y_at + order.keep(i, c[0]), 0))
    aliases = {7 + j: j for j in range(len(previous))}
    aliases.update({7 + len(previous) + j: 5 + j for j in range(len(y_previous))})
    return pl.pallas_call(
        functools.partial(ffn_kernel, order, n_prev, hidden),
        grid_spec=pltpu.PrefetchScalarGridSpec(
            num_scalar_prefetch=1,
            grid=(2 * half,),
            in_specs=[
                row(width), keep(width), send(width), row(width), whole((1, width)),
                pl.BlockSpec((width, 3 * hidden), lambda i, *s: (0, 0), pipeline_mode=pl.Buffered(1)),
            ] + [ANY] * n_prev,
            out_specs=[row(width), row(2 * hidden), row(hidden), send(width), keep(width), y_send, y_keep],
        ),
        out_shape=[sds((seq, width), BF16), sds((seq, 2 * hidden), BF16), sds((seq, hidden), BF16)]
        + [sds((rows, width), BF16)] * 2 + [sds((2 * rows, width), BF16)] * 2,
        input_output_aliases=aliases,
        compiler_params=params(),
        cost_estimate=cost(7.5 * 2 * half),
        name=f"ffn_{chunk}",
    )(core, x, own, got, g, gain, w, *previous, *y_previous)


def back_kernel(
    order, n_prev, first, core_ref, lo_ref, x_ref, own_ref, got_ref, down_ref, dgot_ref, g_ref, gain_ref,
    q_ref, k_ref, v_ref, kt_ref, o_ref, lse_ref, start_ref, wo_ref, wqkv_ref, z_ref, cos_ref, sin_ref,
    qgain_ref, kgain_ref, *rest,
):
    carried = () if first else rest[:2]
    rest = rest[n_prev + (0 if first else 2):]
    (dkv_k_ref, dkv_v_ref, dhb_ref, dz_ref, dh_ref, send_ref, keep_ref, fgain_ref, again_ref, hgain_ref,
     do_ref, dq_ref, delta_ref) = rest
    i = pl.program_id(0)
    core = core_ref[0]
    block = order.block(i, core)
    is_send = order.is_send(i, core)

    @pl.when(i == 0)
    def _():
        fgain_ref[...] = jnp.zeros_like(fgain_ref)
        again_ref[...] = jnp.zeros_like(again_ref)
        hgain_ref[...] = jnp.zeros_like(hgain_ref)
        if first:
            dkv_k_ref[...] = jnp.zeros_like(dkv_k_ref)
            dkv_v_ref[...] = jnp.zeros_like(dkv_v_ref)
        else:
            dkv_k_ref[...] = carried[0][...]
            dkv_v_ref[...] = carried[1][...]

    total = jnp.where(is_send, got_ref[...].astype(F32), own_ref[...].astype(F32))
    dxn = jnp.where(is_send, dgot_ref[...].astype(F32), down_ref[...].astype(F32))
    h = x_ref[...].astype(F32) + total
    rstd = lax.rsqrt(jnp.mean(h * h, axis=1, keepdims=True) + EPSILON)
    hhat = h * rstd
    fgain_ref[...] += jnp.sum(dxn * hhat, axis=0, keepdims=True)
    u = dxn * gain_ref[...]
    dh = g_ref[...].astype(F32) + rstd * (u - hhat * jnp.mean(u * hhat, axis=1, keepdims=True))
    dh_ref[...] = dh
    dhb = dh.astype(BF16)
    dhb_ref[...] = dhb
    dheads = dot(dhb, wo_ref[...]).astype(BF16).astype(F32)
    delta_t = (dheads * o_ref[...].astype(F32)).T
    for group in range(2):
        do_ref[group] = head_pads(dheads[:, group * 128:(group + 1) * 128], group)
        sums = [
            jnp.sum(delta_t[(2 * group + r) * HD:(2 * group + r + 1) * HD], axis=0, keepdims=True)
            for r in range(2)
        ]
        delta_ref[group:group + 1, :] = jnp.concatenate(sums, axis=1)
    dq_ref[...] = jnp.zeros_like(dq_ref)
    start = start_ref[0]
    key_place = lax.broadcasted_iota(jnp.int32, (BLK, 2 * BLK), 0)

    def step(kb, diagonal):
        at = pl.multiple_of(kb * BLK, BLK)
        keys = k_ref[pl.ds(at, BLK), :]
        values = v_ref[pl.ds(at, BLK), :]
        allowed = key_place >= start - at
        if diagonal:
            lane = lax.broadcasted_iota(jnp.int32, (BLK, 2 * BLK), 1)
            allowed = allowed & (key_place <= lax.rem(lane, BLK))
        dk = dkv_k_ref[pl.ds(at, BLK), :]
        dv = dkv_v_ref[pl.ds(at, BLK), :]
        for group in range(2):
            queries, douts = q_ref[0, group], do_ref[group]
            scores = dot_nt(keys, queries) * EXP2_SCALE - lse_ref[0, group:group + 1, :]
            probs = jnp.exp2(jnp.where(allowed, scores, BIG_NEGATIVE))
            dprobs = dot_nt(values, douts)
            dscores = (probs * (dprobs - delta_ref[group:group + 1, :])).astype(BF16)
            dv += dot(probs.astype(BF16), douts)
            dk += dot(dscores, queries)
            dq_ref[group] += dot(kt_ref[group * HD:(group + 1) * HD, pl.ds(at, BLK)], dscores)
        dkv_k_ref[pl.ds(at, BLK), :] = dk
        dkv_v_ref[pl.ds(at, BLK), :] = dv

    def loop_body(kb, carry):
        step(kb, False)
        return carry

    lax.fori_loop(lo_ref[block], block, loop_body, 0)
    step(block, True)

    parts = []
    for group in range(2):
        dq_t = dq_ref[group]
        parts += [dq_t[:, :BLK], dq_t[:, BLK:]]
    dq = jnp.concatenate(parts, axis=0).T * SCALE
    cos, sin = cos_ref[...], sin_ref[...]

    def post_back(grad, raw, gain):
        dn = grad * cos - swap_halves(grad) * sin
        rstd = lax.rsqrt(pair_mean(raw * raw) + EPSILON)
        hat = raw * rstd
        gain_grad = jnp.sum(dn * hat, axis=0, keepdims=True)
        dhat = dn * gain
        return rstd * (dhat - hat * pair_mean(dhat * hat)), gain_grad

    at = pl.multiple_of(block * BLK, BLK)
    qg = jnp.zeros((1, 128), F32)
    for group in range(2):
        lanes = slice(group * 128, (group + 1) * 128)
        dzq, gain_grad = post_back(dq[:, lanes], z_ref[:, lanes], qgain_ref[...])
        dz_ref[:, lanes] = dzq.astype(BF16)
        qg += gain_grad
    dzk, kg = post_back(dkv_k_ref[pl.ds(at, BLK), :] * SCALE, z_ref[:, 256:384], kgain_ref[...])
    dz_ref[:, 256:384] = dzk.astype(BF16)
    dz_ref[:, 384:512] = dkv_v_ref[pl.ds(at, BLK), :].astype(BF16)
    hgain_ref[0:1, :] += qg
    hgain_ref[1:2, :] += kg
    dxn_one = dot_nt(dz_ref[...], wqkv_ref[...]).astype(BF16)
    put(is_send, send_ref, keep_ref, dxn_one)
    x = x_ref[...].astype(F32)
    xhat = x * lax.rsqrt(jnp.mean(x * x, axis=1, keepdims=True) + EPSILON)
    again_ref[...] += jnp.sum(dxn_one.astype(F32) * xhat, axis=0, keepdims=True)


def back_call(chunk, half, core, lo, x, own, got, down, dgot, g, gain, q, k, v, kt, o, lse, start, w,
              z, cos, sin, qgain, kgain, carried, previous):
    seq, width = x.shape
    order = Order(chunk, half, True)
    row, local, send, keep = order_specs(order)
    first = len(previous) == 0
    n_prev = len(previous)
    rows = half * BLK
    by_block = lambda *tail: pl.BlockSpec((1,) + tail, lambda i, c, *s: (order.block(i, c[0]),) + (0,) * len(tail))
    n_in = 2 + 21
    extra = [] if first else [whole((seq, 128))] * 2 + [ANY] * n_prev
    return pl.pallas_call(
        functools.partial(back_kernel, order, n_prev, first),
        grid_spec=pltpu.PrefetchScalarGridSpec(
            num_scalar_prefetch=2,
            grid=(2 * half,),
            in_specs=[
                row(width), keep(width), send(width), keep(width), send(width), row(width), whole((1, width)),
                by_block(2, 2 * BLK, 128), whole((seq, 128)), whole((seq, 128)), whole((128, seq)),
                row(256), by_block(2, 2 * BLK), by_block(1, 2 * BLK),
                pl.BlockSpec((width, 256), lambda i, *s: (0, 2)),
                pl.BlockSpec((width, 512), lambda i, *s: (0, 0)),
                row(384), row(128), row(128), whole((1, 128)), whole((1, 128)),
            ] + extra,
            out_specs=[
                whole((seq, 128)), whole((seq, 128)), row(width), row(512), local(width),
                send(width), keep(width), whole((1, width)), whole((1, width)), whole((2, 128)),
            ],
            scratch_shapes=[
                pltpu.VMEM((2, 2 * BLK, 128), BF16),
                pltpu.VMEM((2, HD, 2 * BLK), F32),
                pltpu.VMEM((2, 2 * BLK), F32),
            ],
        ),
        out_shape=[
            sds((seq, 128), F32), sds((seq, 128), F32), sds((seq, width), BF16), sds((seq, 512), BF16),
            sds((2 * rows, width), F32), sds((rows, width), BF16), sds((rows, width), BF16),
            sds((1, width), F32), sds((1, width), F32), sds((2, 128), F32),
        ],
        input_output_aliases={n_in + 2 + j: 2 + j for j in range(n_prev)},
        compiler_params=params(),
        cost_estimate=cost(7.5 * 2 * half),
        name=f"back_{chunk}",
    )(core, lo, x, own, got, down, dgot, g, gain, q, k, v, kt, o, lse, start, w, w, z, cos, sin,
      qgain, kgain, *carried, *previous)


def input_kernel(order, n_prev, core_ref, dh_ref, x_ref, own_ref, got_ref, gain_ref, *rest):
    (out_ref,) = rest[n_prev:]
    i = pl.program_id(0)
    is_send = order.is_send(i, core_ref[0])
    dxn = jnp.where(is_send, got_ref[...].astype(F32), own_ref[...].astype(F32))
    x = x_ref[...].astype(F32)
    rstd = lax.rsqrt(jnp.mean(x * x, axis=1, keepdims=True) + EPSILON)
    xhat = x * rstd
    u = dxn * gain_ref[...]
    out_ref[...] = dh_ref[...] + rstd * (u - xhat * jnp.mean(u * xhat, axis=1, keepdims=True))


def input_call(chunk, half, core, dh, x, own, got, gain, previous):
    seq, width = x.shape
    order = Order(chunk, half, False)
    row, local, send, keep = order_specs(order)
    n_prev = len(previous)
    return pl.pallas_call(
        functools.partial(input_kernel, order, n_prev),
        grid_spec=pltpu.PrefetchScalarGridSpec(
            num_scalar_prefetch=1,
            grid=(2 * half,),
            in_specs=[local(width), row(width), keep(width), send(width), whole((1, width))] + [ANY] * n_prev,
            out_specs=[row(width)],
        ),
        out_shape=[sds((seq, width), F32)],
        input_output_aliases={6 + j: j for j in range(n_prev)},
        compiler_params=params(),
        cost_estimate=cost(2 * 2 * half),
        name=f"grad_input_{chunk}",
    )(core, dh, x, own, got, gain, *previous)


def output_kernel(core_ref, x_ref, *refs):
    (out_ref,) = refs[-1:]
    chunk = pl.program_id(0)
    mine = pl.program_id(1) == core_ref[0]
    for index in range(CHUNKS):
        own_ref, got_ref = refs[2 * index:2 * index + 2]
        yown_ref, ygot_ref = refs[2 * CHUNKS + 2 * (index // 2):2 * CHUNKS + 2 * (index // 2) + 2]
        for kept in range(2):
            @pl.when((chunk == index) & (mine if kept else jnp.logical_not(mine)))
            def _(a_ref=own_ref if kept else got_ref, y_ref=yown_ref if kept else ygot_ref):
                total = a_ref[...].astype(F32) + y_ref[...].astype(F32)
                out_ref[...] = (x_ref[...].astype(F32) + total).astype(BF16)


def output_call(half, core, x, attn_sums, y_sums):
    seq, width = x.shape
    rows = 128
    per = half * BLK // rows
    row = pl.BlockSpec((rows, width), lambda c, h, i, *s: ((c * 2 + h) * per + i, 0))

    def moving(index):
        def at(c, h, i, *s):
            return (jnp.where(c == index, i, jnp.where(c < index, 0, per - 1)), 0)

        return pl.BlockSpec((rows, width), at)

    def y_moving(pair):
        def at(c, h, i, *s):
            here = lax.rem(c, 2) * per + i
            return (jnp.where(c // 2 == pair, here, jnp.where(c // 2 < pair, 0, 2 * per - 1)), 0)

        return pl.BlockSpec((rows, width), at)

    args, specs = [], []
    for index in range(CHUNKS):
        args += list(attn_sums[index])
        specs += [moving(index)] * 2
    for pair in range(CHUNKS // 2):
        args += list(y_sums[pair])
        specs += [y_moving(pair)] * 2
    return pl.pallas_call(
        output_kernel,
        grid_spec=pltpu.PrefetchScalarGridSpec(
            num_scalar_prefetch=1,
            grid=(CHUNKS, 2, per),
            in_specs=[row] + specs,
            out_specs=row,
        ),
        out_shape=sds((seq, width), BF16),
        compiler_params=pltpu.CompilerParams(
            dimension_semantics=("arbitrary",) * 3, vmem_limit_bytes=56 * 1024 * 1024
        ),
        cost_estimate=cost(8),
        name="output",
    )(core, x, *args)


def pack_kernel(wq_ref, wk_ref, wv_ref, wo_ref, gain_ref, wg_ref, wu_ref, wd_ref, attn_ref, ffn_ref):
    queries, keys = wq_ref.shape[1], wk_ref.shape[1]
    hidden = wg_ref.shape[1]
    attn_ref[:, :queries] = wq_ref[...]
    attn_ref[:, queries:queries + keys] = wk_ref[...]
    attn_ref[:, queries + keys:queries + 2 * keys] = wv_ref[...]
    at = queries + 2 * keys
    attn_ref[:, at:at + queries] = wo_ref[...].astype(F32).T.astype(BF16)
    attn_ref[:, at + queries:] = gain_ref[...].astype(F32).T.astype(BF16)
    ffn_ref[:, :hidden] = wg_ref[...]
    ffn_ref[:, hidden:2 * hidden] = wu_ref[...]
    ffn_ref[:, 2 * hidden:] = wd_ref[...].astype(F32).T.astype(BF16)


def pack(w_query, w_key, w_value, w_out, attn_gain, ffn_gain, w_gate, w_up, w_down):
    shard = w_query.shape[0]
    if shard % 128:
        gains = jnp.stack([attn_gain, ffn_gain] + [jnp.zeros_like(attn_gain)] * 126, axis=1)
        return (
            jnp.concatenate([w_query, w_key, w_value, w_out.T, gains], axis=1),
            jnp.concatenate([w_gate, w_up, w_down.T], axis=1),
        )
    gains = jnp.concatenate([attn_gain[None], ffn_gain[None], jnp.zeros((126, shard), BF16)], axis=0)
    columns = 2 * w_query.shape[1] + 2 * w_key.shape[1] + 128
    return pl.pallas_call(
        pack_kernel,
        out_shape=[sds((shard, columns), BF16), sds((shard, 3 * w_gate.shape[1]), BF16)],
        cost_estimate=cost(3),
        name="pack",
    )(w_query, w_key, w_value, w_out, gains, w_gate, w_up, w_down)


def dp_place(n_dp):
    at = lax.axis_index("dp")
    return at // 2, lax.rem(at, 2)


def ring_of(n_dp):
    return [(i, (i + 2) % n_dp) for i in range(n_dp)]


PAIR = [(i, i ^ 1) for i in range(8)]


def place_kernel(at_ref, *refs):
    pieces, out_ref = refs[:8], refs[8]
    i = pl.program_id(0)
    step = lax.rem(at_ref[0] + 4 - i // 2, 4)
    same = lax.rem(i, 2) == at_ref[1]
    for index in range(4):
        for own in range(2):
            @pl.when((step == index) & (same if own else jnp.logical_not(same)))
            def _(ref=pieces[index + 4 * (1 - own)]):
                out_ref[...] = ref[...]


def place_pieces(line, other, z, y):
    rows, columns = line[0].shape
    return pl.pallas_call(
        place_kernel,
        grid_spec=pltpu.PrefetchScalarGridSpec(
            num_scalar_prefetch=1,
            grid=(8,),
            in_specs=[
                pl.BlockSpec((rows, columns), lambda i, *s: (0, 0), pipeline_mode=pl.Buffered(1))
            ] * 8,
            out_specs=pl.BlockSpec((rows, columns), lambda i, *s: (i, 0)),
        ),
        out_shape=sds((8 * rows, columns), line[0].dtype),
        compiler_params=params(),
        cost_estimate=cost(4 * columns / 3456),
        name="place_pieces",
    )(jnp.stack([z, y]).astype(jnp.int32), *line, *other)


class Gather:
    def __init__(self, piece, n_dp):
        self.n_dp, self.piece, self.line, self.other = n_dp, piece, [], []
        if n_dp == 8:
            self.step(piece)

    def step(self, piece):
        self.line.append(piece)
        self.other.append(lax.ppermute(piece, "dp", PAIR))

    def relay(self):
        if self.n_dp == 8:
            self.step(lax.ppermute(self.line[-1], "dp", ring_of(8)))
            return self.line[-1]
        return self.piece

    def result(self):
        if self.n_dp != 8:
            return lax.all_gather(self.piece, "dp", axis=0, tiled=True)
        return place_pieces(self.line, self.other, *dp_place(8))


class Scatter:
    def __init__(self, grad, n_dp):
        self.n_dp = n_dp
        if n_dp != 8:
            self.total = lax.psum_scatter(grad, "dp", scatter_dimension=0, tiled=True).astype(F32)
            return
        z, y = dp_place(n_dp)
        rows, columns = grad.shape[0] // n_dp, grad.shape[1]
        cut = grad.reshape(4, 2, rows, columns)

        def part(step, line):
            return lax.dynamic_slice(
                cut, (lax.rem(z + 4 - step, 4), line, 0, 0), (1, 1, rows, columns)
            ).reshape(rows, columns)

        self.kept = [part(step, y) for step in (1, 2, 3, 4)]
        self.got = [lax.ppermute(part(step, 1 - y), "dp", PAIR) for step in (1, 2, 3, 4)]
        self.total, self.at = None, 0

    def step(self, token):
        if self.n_dp != 8:
            return self.total
        got = after(self.got[self.at], token)
        total = self.kept[self.at].astype(F32) + got.astype(F32)
        if self.total is not None:
            total = total + after(self.total, token).astype(F32)
        self.at += 1
        if self.at == 4:
            self.total = total
            return total
        total = total.astype(BF16)
        self.total = lax.ppermute(total, "dp", ring_of(8))
        return total


def sum_all(value, n_dp):
    for axis, size in (("tensor", 4), ("dp", n_dp)):
        bit = 1
        while bit < size:
            value = value + lax.ppermute(value, axis, [(i, i ^ bit) for i in range(size)])
            bit *= 2
    return value


def body(
    tokens, segment_ids, positions, pad_mask, w_query, w_key, w_value, w_out, w_gate, w_up, w_down,
    attn_gain, ffn_gain, query_gain, key_gain, cotangent,
):
    del segment_ids
    seq, width = tokens.shape
    shard = w_query.shape[0]
    n_dp = width // shard
    hidden = w_gate.shape[1]
    chunks = CHUNKS
    half = seq // chunks // 2 // BLK
    blocks = seq // BLK
    core_id = lax.rem(lax.axis_index("tensor"), 2).astype(jnp.int32).reshape(1)
    near = [(t, t ^ 1) for t in range(4)]
    far = [(t, t ^ 2) for t in range(4)]

    attn_piece, ffn_piece = pack(
        w_query, w_key, w_value, w_out, attn_gain, ffn_gain, w_gate, w_up, w_down
    )
    gather_attn = Gather(attn_piece, n_dp)
    for _ in range(3):
        late = gather_attn.relay()
    w_attn = gather_attn.result()
    gather_ffn = Gather(after(ffn_piece, late), n_dp)
    gain_rows = w_attn[:, 768:770].T.astype(F32)
    attn_scales, ffn_scales = gain_rows[0:1], gain_rows[1:2]
    query_scales = jnp.tile(query_gain.astype(F32), 2)[None]
    key_scales = jnp.tile(key_gain.astype(F32), 2)[None]

    place = jnp.arange(seq, dtype=jnp.int32)
    start = jnp.where(pad_mask == 1, place - positions, place)
    lo = (place[::BLK] - positions[::BLK]) // BLK
    start_rows = jnp.tile(start.reshape(blocks, 1, BLK), (1, 1, 2))
    half_size = HD // 2
    inverse = THETA ** (-(jnp.arange(half_size).astype(F32) * 2.0 / HD))
    angles = positions.astype(F32)[:, None] * inverse[None, :]
    cos_half, sin_half = jnp.cos(angles), jnp.sin(angles)
    cos = jnp.concatenate([cos_half] * 4, axis=1)
    sin = jnp.concatenate([-sin_half, sin_half] * 2, axis=1)

    def pair_sum(send, keep):
        return (keep.astype(F32) + lax.ppermute(send, "tensor", near).astype(F32)).astype(BF16)

    def four_sum(mine):
        own = (mine.astype(F32) + lax.ppermute(mine, "tensor", far).astype(F32)).astype(BF16)
        return own, lax.ppermute(own, "tensor", near)

    xn_one, z, q, k, v, kt, vt = qkv_call(
        tokens, attn_scales, w_attn, cos, sin, query_scales, key_scales
    )
    order = list(range(chunks))[::-1]
    previous = ()
    attn_sum, ffn_grad_sum, input_grad_sum, dhs = {}, {}, {}, {}
    first = gather_ffn.relay()
    pairs = []
    for step, c in enumerate(order):
        turn = after(core_id, first)
        if step >= 2:
            turn = after(turn, pairs[step - 2])
        heads, lse, send, keep = attn_call(c, half, turn, lo, q, k, vt, start_rows, w_attn, previous)
        previous = (heads, lse)
        pairs.append(pair_sum(send, keep))
        attn_sum[c] = four_sum(pairs[-1])
        if step == 1:
            first = gather_ffn.relay()
    gather_ffn.relay()
    w_ffn = gather_ffn.result()
    previous, y_previous = (), ()
    pairs, y_sums = [], {}
    for step, c in enumerate(order):
        own, got = attn_sum[c]
        turn = core_id if step < 2 else after(core_id, pairs[step - 2])
        xn_two, dgu, hid, dsend, dkeep, ysend, ykeep = ffn_call(
            c, half, turn, tokens, own, got, cotangent, ffn_scales, w_ffn, previous, y_previous
        )
        previous = (xn_two, dgu, hid)
        y_previous = (ysend, ykeep) if c % 2 else ()
        pairs.append(pair_sum(dsend, dkeep))
        ffn_grad_sum[c] = four_sum(pairs[-1])
        if c % 2 == 0:
            y_sums[c // 2] = (ysend, ykeep)
    tn = (((0,), (0,)), ((), ()))
    hid = after(hid, pairs[2])
    grad_down_t = lax.dot_general(cotangent, hid, tn, preferred_element_type=F32).astype(BF16)
    dgu = after(dgu, grad_down_t, pairs[3])
    grad_gate_up = lax.dot_general(xn_two, dgu, tn, preferred_element_type=F32).astype(BF16)
    down_scatter = Scatter(grad_down_t, n_dp)
    gate_up_scatter = Scatter(grad_gate_up, n_dp)

    previous, carried = (), ()
    ffn_gain_grad = jnp.zeros((1, width), F32)
    attn_gain_grad = jnp.zeros((1, width), F32)
    head_gain_grad = jnp.zeros((2, 128), F32)
    pairs, before = [], [grad_gate_up]
    y_pairs = {1: y_sums[1], 0: y_sums[0]}
    for step, c in enumerate(order):
        own, got = attn_sum[c]
        down, dgot = ffn_grad_sum[c]
        turn = after(core_id, *before)
        dk, dv, dhb, dz, dhs[c], send, keep, fg, ag, hg = back_call(
            c, half, turn, lo, tokens, own, got, down, dgot, cotangent, ffn_scales, q, k, v, kt,
            heads, lse, start_rows, w_attn, z, cos, sin, query_scales, key_scales, carried, previous,
        )
        carried, previous = (dk, dv), (dhb, dz)
        ffn_gain_grad += fg
        attn_gain_grad += ag
        head_gain_grad += hg
        before = []
        if step < 3:
            before.append(down_scatter.step(hg))
        if 1 <= step < 3:
            before.append(gate_up_scatter.step(hg))
        if step == 0:
            ysend, ykeep = y_sums[1]
            y_sums[1] = four_sum(pair_sum(after(ysend, hg), ykeep))
        if step == 1:
            ysend, ykeep = y_sums[0]
            y_sums[0] = four_sum(pair_sum(after(ysend, hg), ykeep))
        if step >= 1:
            before.append(pairs[-1])
        pairs.append(pair_sum(send, keep))
        input_grad_sum[c] = four_sum(pairs[-1])

    dz = after(dz, *before)
    grad_qkv = lax.dot_general(xn_one, dz, tn, preferred_element_type=F32).astype(BF16)
    grad_out_t = lax.dot_general(dhb, heads, tn, preferred_element_type=F32).astype(BF16)
    grad_attn = jnp.concatenate([grad_qkv, grad_out_t], axis=1)
    attn_scatter = Scatter(grad_attn, n_dp)
    head_gains = head_gain_grad[:, :HD] + head_gain_grad[:, HD:]
    small = jnp.concatenate(
        [attn_gain_grad.reshape(-1), 0.25 * ffn_gain_grad.reshape(-1), head_gains.reshape(-1)]
    )
    small = sum_all(small.reshape(-1, 128), n_dp).reshape(-1)
    mine = lax.axis_index("dp") * shard
    grad_attn_gain = lax.dynamic_slice(small, (mine,), (shard,))
    grad_ffn_gain = lax.dynamic_slice(small, (width + mine,), (shard,))
    down_own = down_scatter.step(grad_attn)
    for _ in range(2):
        gate_up_own = gate_up_scatter.step(grad_attn)
    for _ in range(4):
        attn_own = attn_scatter.step(grad_attn)

    previous_in = ()
    for c in order:
        eown, egot = input_grad_sum[c]
        (grad_input,) = input_call(c, half, core_id, dhs[c], tokens, eown, egot, attn_scales, previous_in)
        previous_in = (grad_input,)
    output = output_call(half, core_id, tokens, attn_sum, y_sums)
    return (
        output,
        grad_input,
        attn_own[:, :256],
        attn_own[:, 256:384],
        attn_own[:, 384:512],
        attn_own[:, 512:768].T,
        gate_up_own[:, :hidden],
        gate_up_own[:, hidden:],
        down_own.T,
        grad_attn_gain,
        grad_ffn_gain,
        small[2 * width:2 * width + HD],
        small[2 * width + HD:],
    )


def solution(mesh):
    rows, flat, both = P("dp", None), P("dp"), P("dp", "tensor")
    columns = P("tensor", "dp")
    return jax.shard_map(
        body,
        mesh=mesh,
        in_specs=(
            rows, flat, flat, flat, both, both, both, columns, both, both, columns, flat, flat, P(), P(), rows,
        ),
        out_specs=(rows, rows, both, both, both, columns, both, both, columns, flat, flat, P(), P()),
        check_vma=False,
    )
```

time: 1200 us -> 572 us (0.48)
  waiting for transfers between devices: 615 us -> 182 us
  blocking collectives: 222 us -> 0 us
  Pallas kernels: 0 us -> 212 us
  matrix products: 223 us -> 28.6 us
  starting transfers between devices: 0.81 us -> 54.9 us
  other arithmetic: 99.4 us -> 50.4 us
  local copies, waits for them, and re-layouts: 15.5 us -> 32.3 us
  between operations: 18 us -> 2.48 us
    reduce_scatter x7 -> x0, waiting for transfers between devices: 368 us -> none  [the longest x1 99.6 us: body(): lax.psum_scatter(grad_gate, 'dp', scatter_dimension=0, tiled=True)]
    pallas_call x0 -> x21, Pallas kernels: none -> 212 us  [the longest x4 64.5 us: back_call(): pl.pallas_call(functools.partial(back_kernel, order, n_prev, first), grid...]
    psum x3 -> x0, waiting for transfers between devices: 200 us -> none  [the longest x1 74.2 us: body(): lax.psum(ffn_input_part.astype(jnp.bfloat16), 'tensor').astype(jnp.float32)]
    dot_general x45 -> x4, matrix products: 223 us -> 28.6 us  [the longest x1 14.3 us: body(): lax.dot_general(xn_two, dgu, tn, preferred_element_type=F32).astype(BF16)]
    ppermute x0 -> x82, waiting for transfers between devices: none -> 182 us  [the longest x14 57.8 us: four_sum(): lax.ppermute(mine, 'tensor', far).astype(F32)]
    all_gather x6 -> x0, blocking collectives: 160 us -> none  [the longest x1 31.7 us: body(): lax.all_gather(w_query, 'dp', axis=0, tiled=True)]
    ppermute x0 -> x82, starting transfers between devices: none -> 54.9 us  [the longest x14 15 us: four_sum(): lax.ppermute(mine, 'tensor', far).astype(F32)]
    all_gather x3 -> x0, waiting for transfers between devices: 45.4 us -> none  [the longest x1 43.5 us: body(): lax.all_gather(w_down, 'dp', axis=1, tiled=True)]
  transfers between devices with their start and end apart: 13 -> 82, of which waited for: 10 -> 29; matrix products, arithmetic and copies ran while one was open for 9% -> 17% of each run, Pallas kernels for 0% -> 29%
where the time goes in v1:
time: 572 us; the launch traced here: 563 us
  Pallas kernels  212 us (37%)
  waiting for transfers between devices  182 us (32%)
  starting transfers between devices  54.9 us (10%)
  other arithmetic  50.4 us (9%)
  local copies, waits for them, and re-layouts  32.3 us (6%)
  matrix products  28.6 us (5%)
    pallas_call x4, Pallas kernels, back_call(): pl.pallas_call(functools.partial(back_kernel, order, n_prev, first), grid...  64.5 us
    pallas_call x4, Pallas kernels, ffn_call(): pl.pallas_call(functools.partial(ffn_kernel, order, n_prev, hidden), grid...  61.3 us
    ppermute x14, waiting for transfers between devices, four_sum(): lax.ppermute(mine, 'tensor', far).astype(F32)  57.8 us
    ppermute x8, waiting for transfers between devices, step(): self.other.append(lax.ppermute(piece, 'dp', PAIR))  48.3 us
    ppermute x9, waiting for transfers between devices, step(): self.total = lax.ppermute(total, 'dp', ring_of(8))  34.6 us
    pallas_call x4, Pallas kernels, attn_call(): pl.pallas_call(functools.partial(attn_kernel, order, n_prev), grid_spec=p...  28.5 us
    ppermute x6, waiting for transfers between devices, relay(): self.step(lax.ppermute(self.line[-1], 'dp', ring_of(8)))  23.6 us
    unnamed x162, local copies, waits for them, and re-layouts  16.3 us
  transfers between devices with their start and end apart: 82, of which 29 were waited for; matrix products, arithmetic and copies ran while one was open for 17% of the time, Pallas kernels for 29%

profile of v1, /device:TPU:0, one launch (start us, length us, event | category | flops | bytes accessed | tf_op | source)
XLA Modules:
  0.0 562.8 jit_solution(8402057422405233400)
XLA Ops:
  4.5 3.1 collective-permute-start
  7.5 7.8 %collective-permute-done.refs_1_ = bf16[128,896]{1,0:T(8,128)(2,1)S(1)} collective-permute-done((bf16[128,896]{1,0:T(8,128)(2,1)}, bf16[128,896]{1,0:T(8,128)(2,1)S(1)}, u32[]{:S(2)}, u32[]{:S(2)}) %collective-permute-start) | collective-permute-done | bytes 229408 | tf_op jit(solution)/shard_map/ppermute | solution.py:662
  16.9 7.0 %collective-permute-done.1.refs_2_ = bf16[128,896]{1,0:T(8,128)(2,1)S(1)} collective-permute-done((bf16[128,896]{1,0:T(8,128)(2,1)S(1)}, bf16[128,896]{1,0:T(8,128)(2,1)S(1)}, u32[]{:S(2)}, u32[]{:S(2)}) %collective-permute-start.1) | collective-permute-done | bytes 229408 | tf_op jit(solution)/shard_map/ppermute | solution.py:662
  24.8 7.0 %collective-permute-done.2.refs_3_ = bf16[128,896]{1,0:T(8,128)(2,1)S(1)} collective-permute-done((bf16[128,896]{1,0:T(8,128)(2,1)S(1)}, bf16[128,896]{1,0:T(8,128)(2,1)S(1)}, u32[]{:S(2)}, u32[]{:S(2)}) %collective-permute-start.2) | collective-permute-done | bytes 229408 | tf_op jit(solution)/shard_map/ppermute | solution.py:662
  31.8 3.7 fusion.19
  35.5 3.1 pad_maximum_fusion.1
  47.1 3.7 collective-permute-done.7.refs_6_
  53.9 5.2 place_pieces.2.w_ref.wo_ref.wqkv_ref
  61.3 12.6 %qkv.1 = (bf16[2048,1024]{1,0:T(8,128)(2,1)}, f32[2048,384]{1,0:T(8,128)}, bf16[8,2,512,128]{3,2,1,0:T(8,128)(2,1)}, bf16[2048,128]{1,0:T(8,128)(2,1)}, bf16[204...) custom-call(bf16[2048,1024]{1,0:T(8,128)(2,1)} %x_ref.27, ...), custom_call_target="tpu_custom_call" | custom-call | bytes 40800000 | tf_op jit(solution)/shard_map/qkv/pallas_call | solution.py:119
  73.9 7.7 %attn_3.1 = (bf16[2048,256]{1,0:T(8,128)(2,1)}, f32[8,2,512]{2,1,0:T(2,128)}, bf16[256,1024]{1,0:T(8,128)(2,1)}, bf16[256,1024]{1,0:T(8,128)(2,1)}) custom-call(s32[1]{0:T(128)} %bitcast.core_ref, s32[8]{0:T(128)} %and_select_fusion.lo_ref, bf16[8,2,512,128]{3,2,1,0:T(8,128)(2,1)} %get-tuple-element.146.q_ref, bf16[2048,128]{1,0:T(8,128)(2,1)} %get-tuple-element.147.k_ref, ...), custom_call_target="tpu_custom_call" | custom-call | bytes 23800000 | tf_op jit(solution)/shard_map/attn_3/pallas_call | solution.py:243
  82.7 7.7 %attn_2.1 = (bf16[2048,256]{1,0:T(8,128)(2,1)}, f32[8,2,512]{2,1,0:T(2,128)}, bf16[256,1024]{1,0:T(8,128)(2,1)}, bf16[256,1024]{1,0:T(8,128)(2,1)}) custom-call(s32[1]{0:T(128)} %bitcast.core_ref, s32[8]{0:T(128)} %and_select_fusion.lo_ref, bf16[8,2,512,128]{3,2,1,0:T(8,128)(2,1)} %get-tuple-element.146.q_ref, ...), custom_call_target="tpu_custom_call", output_to_operand_aliasing={{0}: (7, {}), {1}: (8, {})} | custom-call | bytes 23800000 | tf_op jit(solution)/shard_map/attn_2/pallas_call | solution.py:243
  92.5 7.0 %attn_1.1 = (bf16[2048,256]{1,0:T(8,128)(2,1)}, f32[8,2,512]{2,1,0:T(2,128)}, bf16[256,1024]{1,0:T(8,128)(2,1)}, bf16[256,1024]{1,0:T(8,128)(2,1)}) custom-call(s32[1]{0:T(128)} %bitcast.core_ref, s32[8]{0:T(128)} %and_select_fusion.lo_ref, bf16[8,2,512,128]{3,2,1,0:T(8,128)(2,1)} %get-tuple-element.146.q_ref, ...), custom_call_target="tpu_custom_call", output_to_operand_aliasing={{0}: (7, {}), {1}: (8, {})} | custom-call | bytes 23800000 | tf_op jit(solution)/shard_map/attn_1/pallas_call | solution.py:243
  101.5 6.2 %attn_0.1 = (bf16[2048,256]{1,0:T(8,128)(2,1)}, f32[8,2,512]{2,1,0:T(2,128)}, bf16[256,1024]{1,0:T(8,128)(2,1)}, bf16[256,1024]{1,0:T(8,128)(2,1)}) custom-call(s32[1]{0:T(128)} %bitcast.core_ref, s32[8]{0:T(128)} %and_select_fusion.lo_ref, bf16[8,2,512,128]{3,2,1,0:T(8,128)(2,1)} %get-tuple-element.146.q_ref, ...), custom_call_target="tpu_custom_call", output_to_operand_aliasing={{0}: (7, {}), {1}: (8, {})} | custom-call | bytes 23800000 | tf_op jit(solution)/shard_map/attn_0/pallas_call | solution.py:243
  108.6 3.8 collective-permute-start.24
  116.1 7.0 %collective-permute-done.23.refs_5_ = bf16[128,3456]{1,0:T(8,128)(2,1)S(1)} collective-permute-done((bf16[128,3456]{1,0:T(8,128)(2,1)S(1)}, bf16[128,3456]{1,0:T(8,128)(2,1)S(1)}, u32[]{:S(2)}, u32[]{:S(2)}) %collective-permute-start.23) | collective-permute-done | bytes 884768 | tf_op jit(solution)/shard_map/ppermute | solution.py:658
  125.6 16.4 %collective-permute-done.24.refs_6_ = bf16[128,3456]{1,0:T(8,128)(2,1)S(1)} collective-permute-done((bf16[128,3456]{1,0:T(8,128)(2,1)S(1)}, bf16[128,3456]{1,0:T(8,128)(2,1)S(1)}, u32[]{:S(2)}, u32[]{:S(2)}) %collective-permute-start.24) | collective-permute-done | bytes 884768 | tf_op jit(solution)/shard_map/ppermute | solution.py:658
  143.1 17.5 %collective-permute-done.25.refs_7_ = bf16[128,3456]{1,0:T(8,128)(2,1)} collective-permute-done((bf16[128,3456]{1,0:T(8,128)(2,1)S(1)}, bf16[128,3456]{1,0:T(8,128)(2,1)}, u32[]{:S(2)}, u32[]{:S(2)}) %collective-permute-start.25) | collective-permute-done | bytes 884768 | tf_op jit(solution)/shard_map/ppermute | solution.py:658
  160.6 8.0 %place_pieces.3.w_ref = bf16[1024,3456]{1,0:T(8,128)(2,1)} custom-call(s32[2]{0:T(128)} %pad_add_fusion.at_ref, bf16[128,3456]{1,0:T(8,128)(2,1)} %get-tuple-element.143.refs_0_, bf16[128,3456]{1,0:T(8,128)(2,1)} %copy-done.30, bf16[128,3456]{1,0:T(8,128)(2,1)} %copy-done.31, bf16[128,3456]{1,0:T(8,128)(2,1)} %copy-done.33, bf16[128,3456]{1,0:T(8,128)(2,1)} %copy-done.32, ...), custom_call_target="tpu_custom_call" | custom-call | bytes 13600000 | tf_op jit(solution)/shard_map/place_pieces/pallas_call | solution.py:633
  169.4 15.2 %ffn_3.1 = (bf16[2048,1024]{1,0:T(8,128)(2,1)}, bf16[2048,2304]{1,0:T(8,128)(2,1)}, bf16[2048,1152]{1,0:T(8,128)(2,1)}, bf16[256,1024]{1,0:T(8,128)(2,1)}, bf16[...) custom-call(s32[1]{0:T(128)} %bitcast.core_ref, bf16[2048,1024]{1,0:T(8,128)(2,1)} %x_ref.27, ...), custom_call_target="tpu_custom_call" | custom-call | bytes 51000000 | tf_op jit(solution)/shard_map/ffn_3/pallas_call | solution.py:305
  186.2 15.4 %ffn_2.1 = (bf16[2048,1024]{1,0:T(8,128)(2,1)}, bf16[2048,2304]{1,0:T(8,128)(2,1)}, bf16[2048,1152]{1,0:T(8,128)(2,1)}, bf16[256,1024]{1,0:T(8,128)(2,1)}, bf16[...) custom-call(s32[1]{0:T(128)} %bitcast.core_ref, ...), custom_call_target="tpu_custom_call", output_to_operand_aliasing={{0}: (7, {}), {1}: (8, {}), {2}: (9, {}), {5}: (10, {}), {6... | custom-call | bytes 51000000 | tf_op jit(solution)/shard_map/ffn_2/pallas_call | solution.py:305
  204.8 15.2 %ffn_1.1 = (bf16[2048,1024]{1,0:T(8,128)(2,1)}, bf16[2048,2304]{1,0:T(8,128)(2,1)}, bf16[2048,1152]{1,0:T(8,128)(2,1)}, bf16[256,1024]{1,0:T(8,128)(2,1)}, bf16[...) custom-call(s32[1]{0:T(128)} %bitcast.core_ref, ...), custom_call_target="tpu_custom_call", output_to_operand_aliasing={{0}: (7, {}), {1}: (8, {}), {2}: (9, {})} | custom-call | bytes 51000000 | tf_op jit(solution)/shard_map/ffn_1/pallas_call | solution.py:305
  220.9 15.4 %ffn_0.1 = (bf16[2048,1024]{1,0:T(8,128)(2,1)}, bf16[2048,2304]{1,0:T(8,128)(2,1)}, bf16[2048,1152]{1,0:T(8,128)(2,1)}, bf16[256,1024]{1,0:T(8,128)(2,1)}, bf16[...) custom-call(s32[1]{0:T(128)} %bitcast.core_ref, ...), custom_call_target="tpu_custom_call", output_to_operand_aliasing={{0}: (7, {}), {1}: (8, {}), {2}: (9, {}), {5}: (10, {}), {6... | custom-call | bytes 51000000 | tf_op jit(solution)/shard_map/ffn_0/pallas_call | solution.py:305
  241.0 10.3 %collective-permute-done.33 = bf16[256,1024]{1,0:T(8,128)(2,1)S(1)} collective-permute-done((bf16[256,1024]{1,0:T(8,128)(2,1)S(1)}, bf16[256,1024]{1,0:T(8,128)(2,1)S(1)}, u32[]{:S(2)}, u32[]{:S(2)}) %collective-permute-start.33) | collective-permute-done | bytes 524320 | tf_op jit(solution)/shard_map/ppermute | solution.py:760
  251.6 10.9 %collective-permute-done.31 = bf16[256,1024]{1,0:T(8,128)(2,1)S(1)} collective-permute-done((bf16[256,1024]{1,0:T(8,128)(2,1)S(1)}, bf16[256,1024]{1,0:T(8,128)(2,1)S(1)}, u32[]{:S(2)}, u32[]{:S(2)}) %collective-permute-start.31) | collective-permute-done | bytes 524320 | tf_op jit(solution)/shard_map/ppermute | solution.py:760
  264.1 8.3 %convolution_convert_fusion.1 = bf16[1152,1024]{0,1:T(8,128)(2,1)S(1)} fusion(bf16[2048,1152]{1,0:T(8,128)(2,1)} %get-tuple-element.189, bf16[2048,1024]{1,0:T(8,128)(2,1)S(1)} %copy-done), kind=kOutput, calls=%fused_computation.1 | convolution fusion | flops 4833017856 | bytes 11272192 | tf_op jit(solution)/shard_map/dot_general | solution.py:799
  276.9 14.3 %convolution_convert_fusion = bf16[1024,2304]{1,0:T(8,128)(2,1)S(1)} fusion(bf16[2048,1024]{1,0:T(8,128)(2,1)} %get-tuple-element.190, bf16[2048,2304]{1,0:T(8,128)(2,1)} %get-tuple-element.194), kind=kOutput, calls=%fused_computation | convolution fusion | flops 9666035712 | bytes 18350080 | tf_op jit(solution)/shard_map/dot_general | solution.py:801
  301.3 16.3 %back_3.1 = (f32[2048,128]{1,0:T(8,128)}, f32[2048,128]{1,0:T(8,128)}, bf16[2048,1024]{1,0:T(8,128)(2,1)}, bf16[2048,512]{1,0:T(8,128)(2,1)}, f32[512,1024]{1,0:...) custom-call(s32[1]{0:T(128)} %bitcast.core_ref, ...), custom_call_target="tpu_custom_call" | custom-call | bytes 51000000 | tf_op jit(solution)/shard_map/back_3/pallas_call | solution.py:449
  321.5 17.0 %back_2.1 = (f32[2048,128]{1,0:T(8,128)}, f32[2048,128]{1,0:T(8,128)}, bf16[2048,1024]{1,0:T(8,128)(2,1)}, bf16[2048,512]{1,0:T(8,128)(2,1)}, f32[512,1024]{1,0:...) custom-call(s32[1]{0:T(128)} %bitcast.core_ref, ...), custom_call_target="tpu_custom_call", output_to_operand_aliasing={{2}: (25, {}), {3}: (26, {})} | custom-call | bytes 51000000 | tf_op jit(solution)/shard_map/back_2/pallas_call | solution.py:449
  344.0 4.9 collective-permute-done.43
  354.1 16.1 %back_1.1 = (f32[2048,128]{1,0:T(8,128)}, f32[2048,128]{1,0:T(8,128)}, bf16[2048,1024]{1,0:T(8,128)(2,1)}, bf16[2048,512]{1,0:T(8,128)(2,1)}, f32[512,1024]{1,0:...) custom-call(s32[1]{0:T(128)} %bitcast.core_ref, ...), custom_call_target="tpu_custom_call", output_to_operand_aliasing={{2}: (25, {}), {3}: (26, {})} | custom-call | bytes 51000000 | tf_op jit(solution)/shard_map/back_1/pallas_call | solution.py:449
  376.9 15.2 %back_0.1 = (f32[2048,128]{1,0:T(8,128)}, f32[2048,128]{1,0:T(8,128)}, bf16[2048,1024]{1,0:T(8,128)(2,1)}, bf16[2048,512]{1,0:T(8,128)(2,1)}, f32[512,1024]{1,0:...) custom-call(s32[1]{0:T(128)} %bitcast.core_ref, ...), custom_call_target="tpu_custom_call", output_to_operand_aliasing={{2}: (25, {}), {3}: (26, {})} | custom-call | bytes 51000000 | tf_op jit(solution)/shard_map/back_0/pallas_call | solution.py:449
  396.3 3.0 collective-permute-done.78
  407.6 3.8 collective-permute-start.81
  411.4 3.6 convolution_convert_fusion.3
  422.5 5.9 %collective-permute-done.76 = bf16[128,1152]{0,1:T(8,128)(2,1)S(1)} collective-permute-done((bf16[128,1152]{0,1:T(8,128)(2,1)}, bf16[128,1152]{0,1:T(8,128)(2,1)S(1)}, u32[]{:S(2)}, u32[]{:S(2)}) %collective-permute-start.76) | collective-permute-done | bytes 294944 | tf_op jit(solution)/shard_map/ppermute | solution.py:703
  433.7 9.5 %collective-permute-done.62 = bf16[256,1024]{1,0:T(8,128)(2,1)S(1)} collective-permute-done((bf16[256,1024]{1,0:T(8,128)(2,1)S(1)}, bf16[256,1024]{1,0:T(8,128)(2,1)S(1)}, u32[]{:S(2)}, u32[]{:S(2)}) %collective-permute-start.62) | collective-permute-done | bytes 524320 | tf_op jit(solution)/shard_map/ppermute | solution.py:760
  444.2 8.6 %collective-permute-done.60 = bf16[256,1024]{1,0:T(8,128)(2,1)S(1)} collective-permute-done((bf16[256,1024]{1,0:T(8,128)(2,1)S(1)}, bf16[256,1024]{1,0:T(8,128)(2,1)S(1)}, u32[]{:S(2)}, u32[]{:S(2)}) %collective-permute-start.60) | collective-permute-done | bytes 524320 | tf_op jit(solution)/shard_map/ppermute | solution.py:760
  457.6 3.0 add_convert_fusion.3
  464.0 7.7 %collective-permute-done.67 = bf16[128,768]{1,0:T(8,128)(2,1)S(1)} collective-permute-done((bf16[128,768]{1,0:T(8,128)(2,1)S(1)}, bf16[128,768]{1,0:T(8,128)(2,1)S(1)}, u32[]{:S(2)}, u32[]{:S(2)}) %collective-permute-start.67) | collective-permute-done | bytes 196640 | tf_op jit(solution)/shard_map/ppermute | solution.py:688
  476.3 4.8 collective-permute-done.68
  483.4 3.8 grad_input_3.1.rest_0_
  488.2 3.8 grad_input_2.1.rest_0_
  492.0 9.6 %collective-permute-done.69 = bf16[128,768]{1,0:T(8,128)(2,1)S(1)} collective-permute-done((bf16[128,768]{1,0:T(8,128)(2,1)S(1)}, bf16[128,768]{1,0:T(8,128)(2,1)S(1)}, u32[]{:S(2)}, u32[]{:S(2)}) %collective-permute-start.69) | collective-permute-done | bytes 196640 | tf_op jit(solution)/shard_map/ppermute | solution.py:703
  503.5 7.6 %collective-permute-done.70 = bf16[128,768]{1,0:T(8,128)(2,1)S(1)} collective-permute-done((bf16[128,768]{1,0:T(8,128)(2,1)S(1)}, bf16[128,768]{1,0:T(8,128)(2,1)S(1)}, u32[]{:S(2)}, u32[]{:S(2)}) %collective-permute-start.70) | collective-permute-done | bytes 196640 | tf_op jit(solution)/shard_map/ppermute | solution.py:703
  515.0 18.5 %collective-permute-done.36 = bf16[512,1024]{1,0:T(8,128)(2,1)} collective-permute-done((bf16[512,1024]{1,0:T(8,128)(2,1)}, bf16[512,1024]{1,0:T(8,128)(2,1)}, u32[]{:S(2)}, u32[]{:S(2)}) %collective-permute-start.36) | collective-permute-done | bytes 1048608 | tf_op jit(solution)/shard_map/ppermute | solution.py:760
  538.3 3.8 grad_input_1.1.rest_0_
  542.1 3.8 grad_input_0.1
  547.9 14.4 %output.1 = bf16[2048,1024]{1,0:T(8,128)(2,1)} custom-call(s32[1]{0:T(128)} %bitcast.core_ref, bf16[2048,1024]{1,0:T(8,128)(2,1)} %x_ref.27, bf16[256,1024]{1,0:T(8,128)(2,1)} %copy-done.6, bf16[256,1024]{1,0:T(8,128)(2,1)} %copy-done.10, bf16[256,1024]{1,0:T(8,128)(2,1)} %copy-done.3, bf16[256,1024]{1,0:T(8,128)(2,1)} %copy-done.7, ...), custom_call_target="tpu_custom_call" | custom-call | bytes 27200000 | tf_op jit(solution)/shard_map/output/pallas_call | solution.py:558
  (389 shorter events, 136.4 us)
Async XLA Ops:
  15.4 30.4 %collective-permute-start.5 = (bf16[128,896]{1,0:T(8,128)(2,1)}, bf16[128,896]{1,0:T(8,128)(2,1)S(1)}, u32[]{:S(2)}, u32[]{:S(2)}) collective-permute-start(bf16[128,896]{1,0:T(8,128)(2,1)} %get-tuple-element.142.refs_0_), channel_id=1, source_target_pairs={{0,4},{4,0},{8,12},{12,8},{16,20},{20,16},{24,28},{28,24},{1,5},{5... | collective-permute-start | bytes 688136 | tf_op jit(solution)/shard_map/ppermute | solution.py:658
  31.8 27.4 %collective-permute-start.3 = (bf16[128,3456]{1,0:T(8,128)(2,1)}, bf16[128,3456]{1,0:T(8,128)(2,1)S(1)}, u32[]{:S(2)}, u32[]{:S(2)}) collective-permute-start(bf16[128,3456]{1,0:T(8,128)(2,1)} %get-tuple-element.143.refs_0_), channel_id=1, source_target_pairs={{0,8},{4,12},{8,16},{12,20},{16,24},{20,28},{24,0},{28,4},{1,9},{5... | collective-permute-start | bytes 2654216 | tf_op jit(solution)/shard_map/ppermute | solution.py:662
  59.2 31.3 %collective-permute-start.4 = (bf16[128,3456]{1,0:T(8,128)(2,1)S(1)}, bf16[128,3456]{1,0:T(8,128)(2,1)S(1)}, u32[]{:S(2)}, u32[]{:S(2)}) collective-permute-start(bf16[128,3456]{1,0:T(8,128)(2,1)S(1)} %collective-permute-done.3.refs_1_), channel_id=1, source_target_pairs={{0,8},{4,12},{8,16},{12,20},{16,24},{20,28},{24,0},{28,4},{1,9},{5... | collective-permute-start | bytes 2654216 | tf_op jit(solution)/shard_map/ppermute | solution.py:662
  81.5 26.2 %collective-permute-start.22 = (bf16[128,3456]{1,0:T(8,128)(2,1)S(1)}, bf16[128,3456]{1,0:T(8,128)(2,1)S(1)}, u32[]{:S(2)}, u32[]{:S(2)}) collective-permute-start(bf16[128,3456]{1,0:T(8,128)(2,1)S(1)} %copy-done.29), channel_id=1, source_target_pairs={{0,4},{4,0},{8,12},{12,8},{16,20},{20,16},{24,28},{28,24},{1,5},{5... | collective-permute-start | bytes 2654216 | tf_op jit(solution)/shard_map/ppermute | solution.py:658
  90.5 23.9 %collective-permute-start.21 = (bf16[128,3456]{1,0:T(8,128)(2,1)S(1)}, bf16[128,3456]{1,0:T(8,128)(2,1)S(1)}, u32[]{:S(2)}, u32[]{:S(2)}) collective-permute-start(bf16[128,3456]{1,0:T(8,128)(2,1)S(1)} %collective-permute-done.4.refs_2_), channel_id=1, source_target_pairs={{0,8},{4,12},{8,16},{12,20},{16,24},{20,28},{24,0},{28,4},{1,9},{5... | collective-permute-start | bytes 2654216 | tf_op jit(solution)/shard_map/ppermute | solution.py:662
  90.9 17.7 %collective-permute-start.19 = (bf16[256,1024]{1,0:T(8,128)(2,1)S(1)}, bf16[256,1024]{1,0:T(8,128)(2,1)S(1)}, u32[]{:S(2)}, u32[]{:S(2)}) collective-permute-start(bf16[256,1024]{1,0:T(8,128)(2,1)S(1)} %add_convert_fusion.26), channel_id=1, source_target_pairs={{0,2},{1,3},{2,0},{3,1},{4,6},{5,7},{6,4},{7,5},{8,10},{9,11},{10,... | collective-permute-start | bytes 1572872 | tf_op jit(solution)/shard_map/ppermute | solution.py:760
  92.5 30.6 %collective-permute-start.23 = (bf16[128,3456]{1,0:T(8,128)(2,1)S(1)}, bf16[128,3456]{1,0:T(8,128)(2,1)S(1)}, u32[]{:S(2)}, u32[]{:S(2)}) collective-permute-start(bf16[128,3456]{1,0:T(8,128)(2,1)S(1)} %collective-permute-done.3.refs_1_), channel_id=1, source_target_pairs={{0,4},{4,0},{8,12},{12,8},{16,20},{20,16},{24,28},{28,24},{1,5},{5... | collective-permute-start | bytes 2654216 | tf_op jit(solution)/shard_map/ppermute | solution.py:658
  108.6 33.5 %collective-permute-start.24 = (bf16[128,3456]{1,0:T(8,128)(2,1)S(1)}, bf16[128,3456]{1,0:T(8,128)(2,1)S(1)}, u32[]{:S(2)}, u32[]{:S(2)}) collective-permute-start(bf16[128,3456]{1,0:T(8,128)(2,1)S(1)} %collective-permute-done.4.refs_2_), channel_id=1, source_target_pairs={{0,4},{4,0},{8,12},{12,8},{16,20},{20,16},{24,28},{28,24},{1,5},{5... | collective-permute-start | bytes 2654216 | tf_op jit(solution)/shard_map/ppermute | solution.py:658
  114.4 46.2 %collective-permute-start.25 = (bf16[128,3456]{1,0:T(8,128)(2,1)S(1)}, bf16[128,3456]{1,0:T(8,128)(2,1)}, u32[]{:S(2)}, u32[]{:S(2)}) collective-permute-start(bf16[128,3456]{1,0:T(8,128)(2,1)S(1)} %collective-permute-done.21.refs_3_), channel_id=1, source_target_pairs={{0,4},{4,0},{8,12},{12,8},{16,20},{20,16},{24,28},{28,24},{1,5},{5... | collective-permute-start | bytes 2654216 | tf_op jit(solution)/shard_map/ppermute | solution.py:658
  123.1 45.4 %collective-permute-start.20 = (bf16[256,1024]{1,0:T(8,128)(2,1)S(1)}, bf16[256,1024]{1,0:T(8,128)(2,1)S(1)}, u32[]{:S(2)}, u32[]{:S(2)}) collective-permute-start(bf16[256,1024]{1,0:T(8,128)(2,1)S(1)} %add_convert_fusion.20.own_ref.refs_6_), channel_id=1, source_target_pairs={{0,1},{1,0},{2,3},{3,2},{4,5},{5,4},{6,7},{7,6},{8,9},{9,8},{10,11... | collective-permute-start | bytes 1572872 | tf_op jit(solution)/shard_map/ppermute | solution.py:761
  124.0 60.6 %collective-permute-start.15 = (bf16[256,1024]{1,0:T(8,128)(2,1)S(1)}, bf16[256,1024]{1,0:T(8,128)(2,1)S(1)}, u32[]{:S(2)}, u32[]{:S(2)}) collective-permute-start(bf16[256,1024]{1,0:T(8,128)(2,1)S(1)} %add_convert_fusion.23), channel_id=1, source_target_pairs={{0,2},{1,3},{2,0},{3,1},{4,6},{5,7},{6,4},{7,5},{8,10},{9,11},{10,... | collective-permute-start | bytes 1572872 | tf_op jit(solution)/shard_map/ppermute | solution.py:760
  125.3 60.1 %collective-permute-start.18 = (bf16[256,1024]{1,0:T(8,128)(2,1)S(1)}, bf16[256,1024]{1,0:T(8,128)(2,1)S(1)}, u32[]{:S(2)}, u32[]{:S(2)}) collective-permute-start(bf16[256,1024]{1,0:T(8,128)(2,1)S(1)} %add_convert_fusion.21.own_ref.refs_4_), channel_id=1, source_target_pairs={{0,1},{1,0},{2,3},{3,2},{4,5},{5,4},{6,7},{7,6},{8,9},{9,8},{10,11... | collective-permute-start | bytes 1572872 | tf_op jit(solution)/shard_map/ppermute | solution.py:761
  142.1 59.7 %collective-permute-start.12 = (bf16[256,1024]{1,0:T(8,128)(2,1)S(1)}, bf16[256,1024]{1,0:T(8,128)(2,1)S(1)}, u32[]{:S(2)}, u32[]{:S(2)}) collective-permute-start(bf16[256,1024]{1,0:T(8,128)(2,1)S(1)} %add_convert_fusion.25), channel_id=1, source_target_pairs={{0,2},{1,3},{2,0},{3,1},{4,6},{5,7},{6,4},{7,5},{8,10},{9,11},{10,... | collective-permute-start | bytes 1572872 | tf_op jit(solution)/shard_map/ppermute | solution.py:760
  184.6 17.9 %collective-permute-start.27 = (bf16[256,1024]{1,0:T(8,128)(2,1)}, bf16[256,1024]{1,0:T(8,128)(2,1)S(1)}, u32[]{:S(2)}, u32[]{:S(2)}) collective-permute-start(bf16[256,1024]{1,0:T(8,128)(2,1)} %get-tuple-element.174), channel_id=1, source_target_pairs={{0,1},{1,0},{2,3},{3,2},{4,5},{5,4},{6,7},{7,6},{8,9},{9,8},{10,11... | collective-permute-start | bytes 1572872 | tf_op jit(solution)/shard_map/ppermute | solution.py:757
  184.9 19.2 %collective-permute-start.16 = (bf16[256,1024]{1,0:T(8,128)(2,1)S(1)}, bf16[256,1024]{1,0:T(8,128)(2,1)S(1)}, u32[]{:S(2)}, u32[]{:S(2)}) collective-permute-start(bf16[256,1024]{1,0:T(8,128)(2,1)S(1)} %add_convert_fusion.22.own_ref.refs_2_), channel_id=1, source_target_pairs={{0,1},{1,0},{2,3},{3,2},{4,5},{5,4},{6,7},{7,6},{8,9},{9,8},{10,11... | collective-permute-start | bytes 1572872 | tf_op jit(solution)/shard_map/ppermute | solution.py:761
  202.0 18.1 %collective-permute-start.13 = (bf16[256,1024]{1,0:T(8,128)(2,1)S(1)}, bf16[256,1024]{1,0:T(8,128)(2,1)S(1)}, u32[]{:S(2)}, u32[]{:S(2)}) collective-permute-start(bf16[256,1024]{1,0:T(8,128)(2,1)S(1)} %add_convert_fusion.24.own_ref.refs_0_), channel_id=1, source_target_pairs={{0,1},{1,0},{2,3},{3,2},{4,5},{5,4},{6,7},{7,6},{8,9},{9,8},{10,11... | collective-permute-start | bytes 1572872 | tf_op jit(solution)/shard_map/ppermute | solution.py:761
  237.5 25.0 %collective-permute-start.31 = (bf16[256,1024]{1,0:T(8,128)(2,1)S(1)}, bf16[256,1024]{1,0:T(8,128)(2,1)S(1)}, u32[]{:S(2)}, u32[]{:S(2)}) collective-permute-start(bf16[256,1024]{1,0:T(8,128)(2,1)S(1)} %add_convert_fusion.18), channel_id=1, source_target_pairs={{0,2},{1,3},{2,0},{3,1},{4,6},{5,7},{6,4},{7,5},{8,10},{9,11},{10,... | collective-permute-start | bytes 1572872 | tf_op jit(solution)/shard_map/ppermute | solution.py:760
  238.5 24.3 %collective-permute-start.28 = (bf16[256,1024]{1,0:T(8,128)(2,1)S(1)}, bf16[256,1024]{1,0:T(8,128)(2,1)S(1)}, u32[]{:S(2)}, u32[]{:S(2)}) collective-permute-start(bf16[256,1024]{1,0:T(8,128)(2,1)S(1)} %copy-done.74), channel_id=1, source_target_pairs={{0,1},{1,0},{2,3},{3,2},{4,5},{5,4},{6,7},{7,6},{8,9},{9,8},{10,11... | collective-permute-start | bytes 1572872 | tf_op jit(solution)/shard_map/ppermute | solution.py:757
  239.8 99.3 %collective-permute-start.52 = (bf16[256,1024]{1,0:T(8,128)(2,1)S(1)}, bf16[256,1024]{1,0:T(8,128)(2,1)}, u32[]{:S(2)}, u32[]{:S(2)}) collective-permute-start(bf16[256,1024]{1,0:T(8,128)(2,1)S(1)} %add_convert_fusion.16), channel_id=1, source_target_pairs={{0,2},{1,3},{2,0},{3,1},{4,6},{5,7},{6,4},{7,5},{8,10},{9,11},{10,... | collective-permute-start | bytes 1572872 | tf_op jit(solution)/shard_map/ppermute | solution.py:760
  251.5 69.5 %collective-permute-start.34 = (bf16[256,1024]{1,0:T(8,128)(2,1)S(1)}, bf16[256,1024]{1,0:T(8,128)(2,1)}, u32[]{:S(2)}, u32[]{:S(2)}) collective-permute-start(bf16[256,1024]{1,0:T(8,128)(2,1)S(1)} %add_convert_fusion.14.down_ref), channel_id=1, source_target_pairs={{0,1},{1,0},{2,3},{3,2},{4,5},{5,4},{6,7},{7,6},{8,9},{9,8},{10,11... | collective-permute-start | bytes 1572872 | tf_op jit(solution)/shard_map/ppermute | solution.py:761
  262.7 38.0 %collective-permute-start.32 = (bf16[256,1024]{1,0:T(8,128)(2,1)S(1)}, bf16[256,1024]{1,0:T(8,128)(2,1)}, u32[]{:S(2)}, u32[]{:S(2)}) collective-permute-start(bf16[256,1024]{1,0:T(8,128)(2,1)S(1)} %add_convert_fusion.15.down_ref), channel_id=1, source_target_pairs={{0,1},{1,0},{2,3},{3,2},{4,5},{5,4},{6,7},{7,6},{8,9},{9,8},{10,11... | collective-permute-start | bytes 1572872 | tf_op jit(solution)/shard_map/ppermute | solution.py:761
  263.0 77.9 %collective-permute-start.46 = (bf16[256,1024]{1,0:T(8,128)(2,1)S(1)}, bf16[256,1024]{1,0:T(8,128)(2,1)}, u32[]{:S(2)}, u32[]{:S(2)}) collective-permute-start(bf16[256,1024]{1,0:T(8,128)(2,1)S(1)} %add_convert_fusion.17), channel_id=1, source_target_pairs={{0,2},{1,3},{2,0},{3,1},{4,6},{5,7},{6,4},{7,5},{8,10},{9,11},{10,... | collective-permute-start | bytes 1572872 | tf_op jit(solution)/shard_map/ppermute | solution.py:760
  275.4 42.2 %collective-permute-start.29 = (bf16[128,1152]{0,1:T(8,128)(2,1)}, bf16[128,1152]{0,1:T(8,128)(2,1)}, u32[]{:S(2)}, u32[]{:S(2)}) collective-permute-start(bf16[128,1152]{0,1:T(8,128)(2,1)} %bitcast.101), channel_id=1, source_target_pairs={{0,4},{4,0},{8,12},{12,8},{16,20},{20,16},{24,28},{28,24},{1,5},{5... | collective-permute-start | bytes 884744 | tf_op jit(solution)/shard_map/ppermute | solution.py:688
  300.7 41.8 %collective-permute-start.44 = (bf16[128,2304]{1,0:T(8,128)(2,1)}, bf16[128,2304]{1,0:T(8,128)(2,1)S(1)}, u32[]{:S(2)}, u32[]{:S(2)}) collective-permute-start(bf16[128,2304]{1,0:T(8,128)(2,1)} %get-tuple-element.311), channel_id=1, source_target_pairs={{0,4},{4,0},{8,12},{12,8},{16,20},{20,16},{24,28},{28,24},{1,5},{5... | collective-permute-start | bytes 1769480 | tf_op jit(solution)/shard_map/ppermute | solution.py:688
  317.6 20.8 %collective-permute-start.42 = (bf16[128,1152]{0,1:T(8,128)(2,1)S(1)}, bf16[128,1152]{0,1:T(8,128)(2,1)S(1)}, u32[]{:S(2)}, u32[]{:S(2)}) collective-permute-start(bf16[128,1152]{0,1:T(8,128)(2,1)S(1)} %bitcast.100), channel_id=1, source_target_pairs={{0,4},{4,0},{8,12},{12,8},{16,20},{20,16},{24,28},{28,24},{1,5},{5... | collective-permute-start | bytes 884744 | tf_op jit(solution)/shard_map/ppermute | solution.py:688
  321.0 49.3 %collective-permute-start.49 = (bf16[128,2304]{1,0:T(8,128)(2,1)S(1)}, bf16[128,2304]{1,0:T(8,128)(2,1)S(1)}, u32[]{:S(2)}, u32[]{:S(2)}) collective-permute-start(bf16[128,2304]{1,0:T(8,128)(2,1)S(1)} %copy-done.36), channel_id=1, source_target_pairs={{0,4},{4,0},{8,12},{12,8},{16,20},{20,16},{24,28},{28,24},{1,5},{5... | collective-permute-start | bytes 1769480 | tf_op jit(solution)/shard_map/ppermute | solution.py:688
  338.5 31.8 %collective-permute-start.41 = (bf16[128,1152]{0,1:T(8,128)(2,1)}, bf16[128,1152]{0,1:T(8,128)(2,1)}, u32[]{:S(2)}, u32[]{:S(2)}) collective-permute-start(bf16[128,1152]{0,1:T(8,128)(2,1)} %bitcast.12), channel_id=1, source_target_pairs={{0,4},{4,0},{8,12},{12,8},{16,20},{20,16},{24,28},{28,24},{1,5},{5... | collective-permute-start | bytes 884744 | tf_op jit(solution)/shard_map/ppermute | solution.py:688
  350.0 20.3 %collective-permute-start.48 = (bf16[128,1152]{0,1:T(8,128)(2,1)S(1)}, bf16[128,1152]{0,1:T(8,128)(2,1)S(1)}, u32[]{:S(2)}, u32[]{:S(2)}) collective-permute-start(bf16[128,1152]{0,1:T(8,128)(2,1)S(1)} %fusion.9), channel_id=1, source_target_pairs={{0,8},{4,12},{8,16},{12,20},{16,24},{20,28},{24,0},{28,4},{1,9},{5... | collective-permute-start | bytes 884744 | tf_op jit(solution)/shard_map/ppermute | solution.py:703
  350.8 23.1 %collective-permute-start.50 = (bf16[128,2304]{1,0:T(8,128)(2,1)S(1)}, bf16[128,2304]{1,0:T(8,128)(2,1)S(1)}, u32[]{:S(2)}, u32[]{:S(2)}) collective-permute-start(bf16[128,2304]{1,0:T(8,128)(2,1)S(1)} %fusion.5), channel_id=1, source_target_pairs={{0,8},{4,12},{8,16},{12,20},{16,24},{20,28},{24,0},{28,4},{1,9},{5... | collective-permute-start | bytes 1769480 | tf_op jit(solution)/shard_map/ppermute | solution.py:703
  353.4 22.7 %collective-permute-start.53 = (bf16[256,1024]{1,0:T(8,128)(2,1)S(1)}, bf16[256,1024]{1,0:T(8,128)(2,1)S(1)}, u32[]{:S(2)}, u32[]{:S(2)}) collective-permute-start(bf16[256,1024]{1,0:T(8,128)(2,1)S(1)} %add_convert_fusion.10.down_ref), channel_id=1, source_target_pairs={{0,1},{1,0},{2,3},{3,2},{4,5},{5,4},{6,7},{7,6},{8,9},{9,8},{10,11... | collective-permute-start | bytes 1572872 | tf_op jit(solution)/shard_map/ppermute | solution.py:761
  403.9 18.5 %collective-permute-start.75 = (bf16[128,1152]{0,1:T(8,128)(2,1)}, bf16[128,1152]{0,1:T(8,128)(2,1)}, u32[]{:S(2)}, u32[]{:S(2)}) collective-permute-start(bf16[128,1152]{0,1:T(8,128)(2,1)} %bitcast.34), channel_id=1, source_target_pairs={{0,4},{4,0},{8,12},{12,8},{16,20},{20,16},{24,28},{28,24},{1,5},{5... | collective-permute-start | bytes 884744 | tf_op jit(solution)/shard_map/ppermute | solution.py:688
  405.5 49.0 %collective-permute-start.71 = (bf16[128,2304]{1,0:T(8,128)(2,1)}, bf16[128,2304]{1,0:T(8,128)(2,1)}, u32[]{:S(2)}, u32[]{:S(2)}) collective-permute-start(bf16[128,2304]{1,0:T(8,128)(2,1)} %get-tuple-element.308), channel_id=1, source_target_pairs={{0,4},{4,0},{8,12},{12,8},{16,20},{20,16},{24,28},{28,24},{1,5},{5... | collective-permute-start | bytes 1769480 | tf_op jit(solution)/shard_map/ppermute | solution.py:688
  406.2 49.4 %collective-permute-start.72 = (bf16[128,2304]{1,0:T(8,128)(2,1)}, bf16[128,2304]{1,0:T(8,128)(2,1)}, u32[]{:S(2)}, u32[]{:S(2)}) collective-permute-start(bf16[128,2304]{1,0:T(8,128)(2,1)} %get-tuple-element.309), channel_id=1, source_target_pairs={{0,4},{4,0},{8,12},{12,8},{16,20},{20,16},{24,28},{28,24},{1,5},{5... | collective-permute-start | bytes 1769480 | tf_op jit(solution)/shard_map/ppermute | solution.py:688
  407.6 23.7 %collective-permute-start.38 = (bf16[512,1024]{1,0:T(8,128)(2,1)}, bf16[512,1024]{1,0:T(8,128)(2,1)S(1)}, u32[]{:S(2)}, u32[]{:S(2)}) collective-permute-start(bf16[512,1024]{1,0:T(8,128)(2,1)} %get-tuple-element.212), channel_id=1, source_target_pairs={{0,1},{1,0},{2,3},{3,2},{4,5},{5,4},{6,7},{7,6},{8,9},{9,8},{10,11... | collective-permute-start | bytes 3145736 | tf_op jit(solution)/shard_map/ppermute | solution.py:757
  422.4 33.2 %collective-permute-start.35 = (bf16[512,1024]{1,0:T(8,128)(2,1)}, bf16[512,1024]{1,0:T(8,128)(2,1)}, u32[]{:S(2)}, u32[]{:S(2)}) collective-permute-start(bf16[512,1024]{1,0:T(8,128)(2,1)} %get-tuple-element.209), channel_id=1, source_target_pairs={{0,1},{1,0},{2,3},{3,2},{4,5},{5,4},{6,7},{7,6},{8,9},{9,8},{10,11... | collective-permute-start | bytes 3145736 | tf_op jit(solution)/shard_map/ppermute | solution.py:757
  431.2 21.5 %collective-permute-start.60 = (bf16[256,1024]{1,0:T(8,128)(2,1)S(1)}, bf16[256,1024]{1,0:T(8,128)(2,1)S(1)}, u32[]{:S(2)}, u32[]{:S(2)}) collective-permute-start(bf16[256,1024]{1,0:T(8,128)(2,1)S(1)} %add_convert_fusion.11), channel_id=1, source_target_pairs={{0,2},{1,3},{2,0},{3,1},{4,6},{5,7},{6,4},{7,5},{8,10},{9,11},{10,... | collective-permute-start | bytes 1572872 | tf_op jit(solution)/shard_map/ppermute | solution.py:760
  443.2 18.8 %collective-permute-start.73 = (bf16[128,2304]{1,0:T(8,128)(2,1)}, bf16[128,2304]{1,0:T(8,128)(2,1)}, u32[]{:S(2)}, u32[]{:S(2)}) collective-permute-start(bf16[128,2304]{1,0:T(8,128)(2,1)} %fusion.4), channel_id=1, source_target_pairs={{0,8},{4,12},{8,16},{12,20},{16,24},{20,28},{24,0},{28,4},{1,9},{5... | collective-permute-start | bytes 1769480 | tf_op jit(solution)/shard_map/ppermute | solution.py:703
  454.5 26.7 %collective-permute-start.58 = (bf16[256,1024]{1,0:T(8,128)(2,1)}, bf16[256,1024]{1,0:T(8,128)(2,1)S(1)}, u32[]{:S(2)}, u32[]{:S(2)}) collective-permute-start(bf16[256,1024]{1,0:T(8,128)(2,1)} %add_convert_fusion.7), channel_id=1, source_target_pairs={{0,2},{1,3},{2,0},{3,1},{4,6},{5,7},{6,4},{7,5},{8,10},{9,11},{10,... | collective-permute-start | bytes 1572872 | tf_op jit(solution)/shard_map/ppermute | solution.py:760
  455.5 16.3 %collective-permute-start.64 = (bf16[128,768]{1,0:T(8,128)(2,1)S(1)}, bf16[128,768]{1,0:T(8,128)(2,1)S(1)}, u32[]{:S(2)}, u32[]{:S(2)}) collective-permute-start(bf16[128,768]{1,0:T(8,128)(2,1)S(1)} %get-tuple-element.320), channel_id=1, source_target_pairs={{0,4},{4,0},{8,12},{12,8},{16,20},{20,16},{24,28},{28,24},{1,5},{5... | collective-permute-start | bytes 589832 | tf_op jit(solution)/shard_map/ppermute | solution.py:688
  455.6 16.8 %collective-permute-start.65 = (bf16[128,768]{1,0:T(8,128)(2,1)S(1)}, bf16[128,768]{1,0:T(8,128)(2,1)S(1)}, u32[]{:S(2)}, u32[]{:S(2)}) collective-permute-start(bf16[128,768]{1,0:T(8,128)(2,1)S(1)} %get-tuple-element.323), channel_id=1, source_target_pairs={{0,4},{4,0},{8,12},{12,8},{16,20},{20,16},{24,28},{28,24},{1,5},{5... | collective-permute-start | bytes 589832 | tf_op jit(solution)/shard_map/ppermute | solution.py:688
  475.2 26.4 %collective-permute-start.55 = (bf16[256,1024]{1,0:T(8,128)(2,1)S(1)}, bf16[256,1024]{1,0:T(8,128)(2,1)S(1)}, u32[]{:S(2)}, u32[]{:S(2)}) collective-permute-start(bf16[256,1024]{1,0:T(8,128)(2,1)S(1)} %add_convert_fusion.9), channel_id=1, source_target_pairs={{0,2},{1,3},{2,0},{3,1},{4,6},{5,7},{6,4},{7,5},{8,10},{9,11},{10,... | collective-permute-start | bytes 1572872 | tf_op jit(solution)/shard_map/ppermute | solution.py:760
  481.1 21.9 %collective-permute-start.74 = (bf16[128,2304]{1,0:T(8,128)(2,1)S(1)}, bf16[128,2304]{1,0:T(8,128)(2,1)S(1)}, u32[]{:S(2)}, u32[]{:S(2)}) collective-permute-start(bf16[128,2304]{1,0:T(8,128)(2,1)S(1)} %fusion.1), channel_id=1, source_target_pairs={{0,8},{4,12},{8,16},{12,20},{16,24},{20,28},{24,0},{28,4},{1,9},{5... | collective-permute-start | bytes 1769480 | tf_op jit(solution)/shard_map/ppermute | solution.py:703
  481.2 20.4 %collective-permute-start.69 = (bf16[128,768]{1,0:T(8,128)(2,1)S(1)}, bf16[128,768]{1,0:T(8,128)(2,1)S(1)}, u32[]{:S(2)}, u32[]{:S(2)}) collective-permute-start(bf16[128,768]{1,0:T(8,128)(2,1)S(1)} %fusion.15), channel_id=1, source_target_pairs={{0,8},{4,12},{8,16},{12,20},{16,24},{20,28},{24,0},{28,4},{1,9},{5... | collective-permute-start | bytes 589832 | tf_op jit(solution)/shard_map/ppermute | solution.py:703
  482.3 31.0 %collective-permute-start.39 = (bf16[512,1024]{1,0:T(8,128)(2,1)S(1)}, bf16[512,1024]{1,0:T(8,128)(2,1)}, u32[]{:S(2)}, u32[]{:S(2)}) collective-permute-start(bf16[512,1024]{1,0:T(8,128)(2,1)S(1)} %copy-done.12), channel_id=1, source_target_pairs={{0,2},{1,3},{2,0},{3,1},{4,6},{5,7},{6,4},{7,5},{8,10},{9,11},{10,... | collective-permute-start | bytes 3145736 | tf_op jit(solution)/shard_map/ppermute | solution.py:760
  487.2 46.3 %collective-permute-start.36 = (bf16[512,1024]{1,0:T(8,128)(2,1)}, bf16[512,1024]{1,0:T(8,128)(2,1)}, u32[]{:S(2)}, u32[]{:S(2)}) collective-permute-start(bf16[512,1024]{1,0:T(8,128)(2,1)} %add_convert_fusion.3), channel_id=1, source_target_pairs={{0,2},{1,3},{2,0},{3,1},{4,6},{5,7},{6,4},{7,5},{8,10},{9,11},{10,... | collective-permute-start | bytes 3145736 | tf_op jit(solution)/shard_map/ppermute | solution.py:760
  501.5 36.8 %collective-permute-start.59 = (bf16[256,1024]{1,0:T(8,128)(2,1)S(1)}, bf16[256,1024]{1,0:T(8,128)(2,1)}, u32[]{:S(2)}, u32[]{:S(2)}) collective-permute-start(bf16[256,1024]{1,0:T(8,128)(2,1)S(1)} %add_convert_fusion.6.own_ref), channel_id=1, source_target_pairs={{0,1},{1,0},{2,3},{3,2},{4,5},{5,4},{6,7},{7,6},{8,9},{9,8},{10,11... | collective-permute-start | bytes 1572872 | tf_op jit(solution)/shard_map/ppermute | solution.py:761
  503.0 39.1 %collective-permute-start.56 = (bf16[256,1024]{1,0:T(8,128)(2,1)}, bf16[256,1024]{1,0:T(8,128)(2,1)}, u32[]{:S(2)}, u32[]{:S(2)}) collective-permute-start(bf16[256,1024]{1,0:T(8,128)(2,1)} %add_convert_fusion.8.own_ref), channel_id=1, source_target_pairs={{0,1},{1,0},{2,3},{3,2},{4,5},{5,4},{6,7},{7,6},{8,9},{9,8},{10,11... | collective-permute-start | bytes 1572872 | tf_op jit(solution)/shard_map/ppermute | solution.py:761
  514.9 31.0 %collective-permute-start.40 = (bf16[512,1024]{1,0:T(8,128)(2,1)S(1)}, bf16[512,1024]{1,0:T(8,128)(2,1)S(1)}, u32[]{:S(2)}, u32[]{:S(2)}) collective-permute-start(bf16[512,1024]{1,0:T(8,128)(2,1)S(1)} %add_convert_fusion.refs_10_), channel_id=1, source_target_pairs={{0,1},{1,0},{2,3},{3,2},{4,5},{5,4},{6,7},{7,6},{8,9},{9,8},{10,11... | collective-permute-start | bytes 3145736 | tf_op jit(solution)/shard_map/ppermute | solution.py:761
  (112 other events, 1227.1 us)

commit v2 on v1

--- a/solution.py
+++ b/solution.py
@@ -137,7 +137,7 @@
             sds((128, seq), BF16), sds((2, HD + 16, seq), BF16),
         ],
         compiler_params=params(),
-        cost_estimate=cost(12),
+        cost_estimate=cost(0.6),
         name="qkv",
     )(x, gain, w, cos, sin, qgain, kgain)
 
@@ -259,7 +259,7 @@
         ],
         input_output_aliases={7 + j: j for j in range(n_prev)},
         compiler_params=params(),
-        cost_estimate=cost(3.5 * 2 * half),
+        cost_estimate=cost(0.2 * 2 * half),
         name=f"attn_{chunk}",
     )(core, lo, q, k, vt, start, w, *previous)
 
@@ -317,7 +317,7 @@
         + [sds((rows, width), BF16)] * 2 + [sds((2 * rows, width), BF16)] * 2,
         input_output_aliases=aliases,
         compiler_params=params(),
-        cost_estimate=cost(7.5 * 2 * half),
+        cost_estimate=cost(5 * 7.5 * 2 * half),
         name=f"ffn_{chunk}",
     )(core, x, own, got, g, gain, w, *previous, *y_previous)
 
@@ -476,7 +476,7 @@
         ],
         input_output_aliases={n_in + 2 + j: 2 + j for j in range(n_prev)},
         compiler_params=params(),
-        cost_estimate=cost(7.5 * 2 * half),
+        cost_estimate=cost(5 * 7.5 * 2 * half),
         name=f"back_{chunk}",
     )(core, lo, x, own, got, down, dgot, g, gain, q, k, v, kt, o, lse, start, w, w, z, cos, sin,
       qgain, kgain, *carried, *previous)
@@ -510,7 +510,7 @@
         out_shape=[sds((seq, width), F32)],
         input_output_aliases={6 + j: j for j in range(n_prev)},
         compiler_params=params(),
-        cost_estimate=cost(2 * 2 * half),
+        cost_estimate=cost(5 * 2 * 2 * half),
         name=f"grad_input_{chunk}",
     )(core, dh, x, own, got, gain, *previous)
 
@@ -531,7 +531,7 @@
 
 def output_call(half, core, x, attn_sums, y_sums):
     seq, width = x.shape
-    rows = 128
+    rows = BLK
     per = half * BLK // rows
     row = pl.BlockSpec((rows, width), lambda c, h, i, *s: ((c * 2 + h) * per + i, 0))
 
@@ -567,7 +567,7 @@
         compiler_params=pltpu.CompilerParams(
             dimension_semantics=("arbitrary",) * 3, vmem_limit_bytes=56 * 1024 * 1024
         ),
-        cost_estimate=cost(8),
+        cost_estimate=cost(5 * 8),
         name="output",
     )(core, x, *args)
 
@@ -642,26 +642,32 @@
         ),
         out_shape=sds((8 * rows, columns), line[0].dtype),
         compiler_params=params(),
-        cost_estimate=cost(4 * columns / 3456),
+        cost_estimate=cost(0.2),
         name="place_pieces",
     )(jnp.stack([z, y]).astype(jnp.int32), *line, *other)
 
 
 class Gather:
-    def __init__(self, piece, n_dp):
+    def __init__(self, piece, n_dp, *clear):
         self.n_dp, self.piece, self.line, self.other = n_dp, piece, [], []
         if n_dp == 8:
-            self.step(piece)
-
-    def step(self, piece):
+            self.step(piece, *clear)
+
+    def step(self, piece, *clear):
         self.line.append(piece)
-        self.other.append(lax.ppermute(piece, "dp", PAIR))
+        self.other.append(lax.ppermute(after(piece, *clear) if clear else piece, "dp", PAIR))
 
     def relay(self):
         if self.n_dp == 8:
-            self.step(lax.ppermute(self.line[-1], "dp", ring_of(8)))
+            piece = self.line[-1]
+            if len(self.line) > 1:
+                piece = after(piece, self.other[-2])
+            self.step(lax.ppermute(piece, "dp", ring_of(8)))
             return self.line[-1]
         return self.piece
+
+    def crossed(self, at):
+        return self.other[at] if self.n_dp == 8 else self.piece
 
     def result(self):
         if self.n_dp != 8:
@@ -674,15 +680,14 @@
         self.n_dp = n_dp
         if n_dp != 8:
             self.total = lax.psum_scatter(grad, "dp", scatter_dimension=0, tiled=True).astype(F32)
+            self.got = [self.total] * 4
             return
         z, y = dp_place(n_dp)
         rows, columns = grad.shape[0] // n_dp, grad.shape[1]
-        cut = grad.reshape(4, 2, rows, columns)
 
         def part(step, line):
-            return lax.dynamic_slice(
-                cut, (lax.rem(z + 4 - step, 4), line, 0, 0), (1, 1, rows, columns)
-            ).reshape(rows, columns)
+            at = (lax.rem(z + 4 - step, 4) * 2 + line) * rows
+            return lax.dynamic_slice(grad, (at, 0), (rows, columns))
 
         self.kept = [part(step, y) for step in (1, 2, 3, 4)]
         self.got = [lax.ppermute(part(step, 1 - y), "dp", PAIR) for step in (1, 2, 3, 4)]
@@ -736,7 +741,7 @@
     for _ in range(3):
         late = gather_attn.relay()
     w_attn = gather_attn.result()
-    gather_ffn = Gather(after(ffn_piece, late), n_dp)
+    gather_ffn = Gather(after(ffn_piece, late), n_dp, *gather_attn.other)
     gain_rows = w_attn[:, 768:770].T.astype(F32)
     attn_scales, ffn_scales = gain_rows[0:1], gain_rows[1:2]
     query_scales = jnp.tile(query_gain.astype(F32), 2)[None]
@@ -760,31 +765,42 @@
         own = (mine.astype(F32) + lax.ppermute(mine, "tensor", far).astype(F32)).astype(BF16)
         return own, lax.ppermute(own, "tensor", near)
 
+    line_one = gather_ffn.relay()
     xn_one, z, q, k, v, kt, vt = qkv_call(
         tokens, attn_scales, w_attn, cos, sin, query_scales, key_scales
     )
     order = list(range(chunks))[::-1]
     previous = ()
     attn_sum, ffn_grad_sum, input_grad_sum, dhs = {}, {}, {}, {}
-    first = gather_ffn.relay()
     pairs = []
     for step, c in enumerate(order):
-        turn = after(core_id, first)
-        if step >= 2:
-            turn = after(turn, pairs[step - 2])
+        turn = core_id
+        if step == 0:
+            turn = after(turn, line_one, gather_ffn.crossed(0))
+            line_two = gather_ffn.relay()
+        if step == 2:
+            turn = after(turn, pairs[0], line_two, gather_ffn.crossed(1))
+            gather_ffn.relay()
+        if step == 3:
+            turn = after(turn, pairs[1])
         heads, lse, send, keep = attn_call(c, half, turn, lo, q, k, vt, start_rows, w_attn, previous)
         previous = (heads, lse)
         pairs.append(pair_sum(send, keep))
         attn_sum[c] = four_sum(pairs[-1])
-        if step == 1:
-            first = gather_ffn.relay()
-    gather_ffn.relay()
     w_ffn = gather_ffn.result()
     previous, y_previous = (), ()
-    pairs, y_sums = [], {}
+    pairs, y_sums, y_pairs = [], {}, {}
     for step, c in enumerate(order):
         own, got = attn_sum[c]
-        turn = core_id if step < 2 else after(core_id, pairs[step - 2])
+        turn = core_id
+        if step == 0:
+            turn = after(turn, attn_sum[order[1]], attn_sum[order[2]][0])
+        if step == 1:
+            turn = after(turn, attn_sum[order[3]][0])
+        if step >= 2:
+            turn = after(turn, pairs[step - 2])
+        if step == 3:
+            turn = after(turn, ffn_grad_sum[order[0]][0])
         xn_two, dgu, hid, dsend, dkeep, ysend, ykeep = ffn_call(
             c, half, turn, tokens, own, got, cotangent, ffn_scales, w_ffn, previous, y_previous
         )
@@ -793,11 +809,11 @@
         pairs.append(pair_sum(dsend, dkeep))
         ffn_grad_sum[c] = four_sum(pairs[-1])
         if c % 2 == 0:
-            y_sums[c // 2] = (ysend, ykeep)
+            y_pairs[c // 2] = pair_sum(ysend, ykeep)
     tn = (((0,), (0,)), ((), ()))
-    hid = after(hid, pairs[2])
+    hid = after(hid, pairs[2], ffn_grad_sum[order[1]][0], y_pairs[1])
     grad_down_t = lax.dot_general(cotangent, hid, tn, preferred_element_type=F32).astype(BF16)
-    dgu = after(dgu, grad_down_t, pairs[3])
+    dgu = after(dgu, grad_down_t, pairs[3], ffn_grad_sum[order[2]][0], ffn_grad_sum[order[0]][1], y_pairs[0])
     grad_gate_up = lax.dot_general(xn_two, dgu, tn, preferred_element_type=F32).astype(BF16)
     down_scatter = Scatter(grad_down_t, n_dp)
     gate_up_scatter = Scatter(grad_gate_up, n_dp)
@@ -806,8 +822,8 @@
     ffn_gain_grad = jnp.zeros((1, width), F32)
     attn_gain_grad = jnp.zeros((1, width), F32)
     head_gain_grad = jnp.zeros((2, 128), F32)
-    pairs, before = [], [grad_gate_up]
-    y_pairs = {1: y_sums[1], 0: y_sums[0]}
+    pairs = []
+    before = [down_scatter.step(grad_gate_up), down_scatter.got[:3], ffn_grad_sum[order[3]][0]]
     for step, c in enumerate(order):
         own, got = attn_sum[c]
         down, dgot = ffn_grad_sum[c]
@@ -820,21 +836,24 @@
         ffn_gain_grad += fg
         attn_gain_grad += ag
         head_gain_grad += hg
-        before = []
+        before = [gate_up_scatter.step(hg), down_scatter.got[3]]
         if step < 3:
             before.append(down_scatter.step(hg))
-        if 1 <= step < 3:
-            before.append(gate_up_scatter.step(hg))
         if step == 0:
-            ysend, ykeep = y_sums[1]
-            y_sums[1] = four_sum(pair_sum(after(ysend, hg), ykeep))
+            y_sums[1] = four_sum(y_pairs[1])
+            before.append(y_sums[1][0])
         if step == 1:
-            ysend, ykeep = y_sums[0]
-            y_sums[0] = four_sum(pair_sum(after(ysend, hg), ykeep))
+            y_sums[0] = four_sum(y_pairs[0])
+            before.append((y_sums[0][0], y_sums[1][1]))
         if step >= 1:
-            before.append(pairs[-1])
+            before.append(pairs[step - 1])
+        if step >= 2:
+            before.append(input_grad_sum[order[step - 2]][0])
+        if step >= 3:
+            before.append((input_grad_sum[order[step - 3]][1], y_sums[0][1]))
         pairs.append(pair_sum(send, keep))
         input_grad_sum[c] = four_sum(pairs[-1])
+    down_own, gate_up_own = down_scatter.total, gate_up_scatter.total
 
     dz = after(dz, *before)
     grad_qkv = lax.dot_general(xn_one, dz, tn, preferred_element_type=F32).astype(BF16)
@@ -845,22 +864,23 @@
     small = jnp.concatenate(
         [attn_gain_grad.reshape(-1), 0.25 * ffn_gain_grad.reshape(-1), head_gains.reshape(-1)]
     )
-    small = sum_all(small.reshape(-1, 128), n_dp).reshape(-1)
+    sent = attn_scatter.step(grad_attn)
+    small = sum_all(after(small, sent).reshape(-1, 128), n_dp).reshape(-1)
     mine = lax.axis_index("dp") * shard
     grad_attn_gain = lax.dynamic_slice(small, (mine,), (shard,))
     grad_ffn_gain = lax.dynamic_slice(small, (width + mine,), (shard,))
-    down_own = down_scatter.step(grad_attn)
-    for _ in range(2):
-        gate_up_own = gate_up_scatter.step(grad_attn)
-    for _ in range(4):
-        attn_own = attn_scatter.step(grad_attn)
-
+    output = output_call(half, after(core_id, grad_attn), tokens, attn_sum, y_sums)
     previous_in = ()
-    for c in order:
+    for step, c in enumerate(order):
         eown, egot = input_grad_sum[c]
-        (grad_input,) = input_call(c, half, core_id, dhs[c], tokens, eown, egot, attn_scales, previous_in)
+        turn = after(core_id, sent, output, attn_scatter.got) if step == 0 else core_id
+        (grad_input,) = input_call(c, half, turn, dhs[c], tokens, eown, egot, attn_scales, previous_in)
         previous_in = (grad_input,)
-    output = output_call(half, core_id, tokens, attn_sum, y_sums)
+        if step == 0:
+            sent = attn_scatter.step(grad_attn)
+        if step == 2:
+            sent = attn_scatter.step(grad_attn)
+    attn_own = attn_scatter.step(grad_attn)
     return (
         output,
         grad_input,

time: 572 us -> 498 us (0.87)
  waiting for transfers between devices: 182 us -> 123 us
  local copies, waits for them, and re-layouts: 32.3 us -> 18.9 us
  starting transfers between devices: 54.9 us -> 62.3 us
  other arithmetic: 50.4 us -> 43.5 us
    ppermute x14, waiting for transfers between devices: 71.9 us -> 47.8 us  [the longest x6 28.2 us: relay(): self.step(lax.ppermute(piece, 'dp', ring_of(8)))]
    ppermute x9, waiting for transfers between devices: 34.6 us -> 14.6 us  [step(): self.total = lax.ppermute(total, 'dp', ring_of(8))]
    ppermute x14, waiting for transfers between devices: 57.8 us -> 41.3 us  [four_sum(): lax.ppermute(mine, 'tensor', far).astype(F32)]
    convert_element_type x14, other arithmetic: 12.8 us -> 4.93 us  [pair_sum(): (keep.astype(F32) + lax.ppermute(send, 'tensor', near).astype(F32)).astyp...]
    ppermute x12, waiting for transfers between devices: 8.94 us -> 16.6 us  [__init__(): lax.ppermute(part(step, 1 - y), 'dp', PAIR)]
    unnamed x162 -> x158, local copies, waits for them, and re-layouts: 16.3 us -> 8.83 us
  transfers between devices with their start and end apart: 82 -> 82, of which waited for: 29 -> 21; matrix products, arithmetic and copies ran while one was open for 17% -> 17% of each run, Pallas kernels for 29% -> 42%
where the time goes in v2:
time: 498 us; the launch traced here: 489 us
  Pallas kernels  211 us (42%)
  waiting for transfers between devices  123 us (25%)
  starting transfers between devices  62.3 us (13%)
  other arithmetic  43.5 us (9%)
  matrix products  28 us (6%)
  local copies, waits for them, and re-layouts  18.9 us (4%)
    pallas_call x4, Pallas kernels, back_call(): pl.pallas_call(functools.partial(back_kernel, order, n_prev, first), grid...  66.5 us
    pallas_call x4, Pallas kernels, ffn_call(): pl.pallas_call(functools.partial(ffn_kernel, order, n_prev, hidden), grid...  61.5 us
    ppermute x14, waiting for transfers between devices, four_sum(): lax.ppermute(mine, 'tensor', far).astype(F32)  41.3 us
    pallas_call x4, Pallas kernels, attn_call(): pl.pallas_call(functools.partial(attn_kernel, order, n_prev), grid_spec=p...  29.9 us
    ppermute x6, waiting for transfers between devices, relay(): self.step(lax.ppermute(piece, 'dp', ring_of(8)))  28.2 us
    ppermute x8, waiting for transfers between devices, step(): lax.ppermute(after(piece, *clear) if clear else piece, 'dp', PAIR)  19.5 us
    ppermute x14, starting transfers between devices, four_sum(): lax.ppermute(mine, 'tensor', far).astype(F32)  16.9 us
    ppermute x12, waiting for transfers between devices, __init__(): lax.ppermute(part(step, 1 - y), 'dp', PAIR)  16.6 us
  transfers between devices with their start and end apart: 82, of which 21 were waited for; matrix products, arithmetic and copies ran while one was open for 17% of the time, Pallas kernels for 42%

profile of v2, /device:TPU:0, one launch (start us, length us, event | category | flops | bytes accessed | tf_op | source)
XLA Modules:
  0.0 489.3 jit_solution(13036951599393158650)
XLA Ops:
  2.1 2.4 pack.1
  4.5 3.1 collective-permute-start
  9.0 6.3 %collective-permute-done.refs_1_ = bf16[128,896]{1,0:T(8,128)(2,1)S(1)} collective-permute-done((bf16[128,896]{1,0:T(8,128)(2,1)}, bf16[128,896]{1,0:T(8,128)(2,1)S(1)}, u32[]{:S(2)}, u32[]{:S(2)}) %collective-permute-start) | collective-permute-done | bytes 229408 | tf_op jit(solution)/shard_map/ppermute | solution.py:665
  17.9 6.1 %collective-permute-done.2.refs_2_ = bf16[128,896]{1,0:T(8,128)(2,1)S(1)} collective-permute-done((bf16[128,896]{1,0:T(8,128)(2,1)S(1)}, bf16[128,896]{1,0:T(8,128)(2,1)S(1)}, u32[]{:S(2)}, u32[]{:S(2)}) %collective-permute-start.2) | collective-permute-done | bytes 229408 | tf_op jit(solution)/shard_map/ppermute | solution.py:665
  26.3 5.6 %collective-permute-done.4.refs_3_ = bf16[128,896]{1,0:T(8,128)(2,1)S(1)} collective-permute-done((bf16[128,896]{1,0:T(8,128)(2,1)S(1)}, bf16[128,896]{1,0:T(8,128)(2,1)S(1)}, u32[]{:S(2)}, u32[]{:S(2)}) %collective-permute-start.4) | collective-permute-done | bytes 229408 | tf_op jit(solution)/shard_map/ppermute | solution.py:665
  40.6 3.7 fusion.6
  44.3 3.1 pad_maximum_fusion.1
  47.5 5.2 %place_pieces.2.w_ref.wo_ref.wqkv_ref = bf16[1024,896]{1,0:T(8,128)(2,1)} custom-call(s32[2]{0:T(128)} %pad_add_fusion.at_ref, bf16[128,896]{1,0:T(8,128)(2,1)} %get-tuple-element.149.refs_0_, bf16[128,896]{1,0:T(8,128)(2,1)} %copy-done.51, bf16[128,896]{1,0:T(8,128)(2,1)} %copy-done.53, bf16[128,896]{1,0:T(8,128)(2,1)} %copy-done.55, ...), custom_call_target="tpu_custom_call" | custom-call | bytes 680000 | tf_op jit(solution)/shard_map/place_pieces/pallas_call | solution.py:633
  52.7 5.4 %collective-permute-done.7.refs_1_ = bf16[128,3456]{1,0:T(8,128)(2,1)S(1)} collective-permute-done((bf16[128,3456]{1,0:T(8,128)(2,1)}, bf16[128,3456]{1,0:T(8,128)(2,1)S(1)}, u32[]{:S(2)}, u32[]{:S(2)}) %collective-permute-start.7) | collective-permute-done | bytes 884768 | tf_op jit(solution)/shard_map/ppermute | solution.py:665
  61.0 12.6 %qkv.1 = (bf16[2048,1024]{1,0:T(8,128)(2,1)}, f32[2048,384]{1,0:T(8,128)}, bf16[8,2,512,128]{3,2,1,0:T(8,128)(2,1)}, bf16[2048,128]{1,0:T(8,128)(2,1)}, bf16[204...) custom-call(bf16[2048,1024]{1,0:T(8,128)(2,1)} %x_ref.27, ...), custom_call_target="tpu_custom_call" | custom-call | bytes 2040000 | tf_op jit(solution)/shard_map/qkv/pallas_call | solution.py:119
  73.7 6.9 %attn_3.1 = (bf16[2048,256]{1,0:T(8,128)(2,1)}, f32[8,2,512]{2,1,0:T(2,128)}, bf16[256,1024]{1,0:T(8,128)(2,1)}, bf16[256,1024]{1,0:T(8,128)(2,1)}) custom-call(s32[1]{0:T(128)} %bitcast.core_ref, s32[8]{0:T(128)} %and_select_fusion.lo_ref, bf16[8,2,512,128]{3,2,1,0:T(8,128)(2,1)} %get-tuple-element.153.q_ref, bf16[2048,128]{1,0:T(8,128)(2,1)} %get-tuple-element.154.k_ref, ...), custom_call_target="tpu_custom_call" | custom-call | bytes 1360000 | tf_op jit(solution)/shard_map/attn_3/pallas_call | solution.py:243
  80.5 7.7 %attn_2.1 = (bf16[2048,256]{1,0:T(8,128)(2,1)}, f32[8,2,512]{2,1,0:T(2,128)}, bf16[256,1024]{1,0:T(8,128)(2,1)}, bf16[256,1024]{1,0:T(8,128)(2,1)}) custom-call(s32[1]{0:T(128)} %bitcast.core_ref, s32[8]{0:T(128)} %and_select_fusion.lo_ref, bf16[8,2,512,128]{3,2,1,0:T(8,128)(2,1)} %get-tuple-element.153.q_ref, ...), custom_call_target="tpu_custom_call", output_to_operand_aliasing={{0}: (7, {}), {1}: (8, {})} | custom-call | bytes 1360000 | tf_op jit(solution)/shard_map/attn_2/pallas_call | solution.py:243
  92.2 9.0 %attn_1.1 = (bf16[2048,256]{1,0:T(8,128)(2,1)}, f32[8,2,512]{2,1,0:T(2,128)}, bf16[256,1024]{1,0:T(8,128)(2,1)}, bf16[256,1024]{1,0:T(8,128)(2,1)}) custom-call(s32[1]{0:T(128)} %bitcast.core_ref, s32[8]{0:T(128)} %and_select_fusion.lo_ref, bf16[8,2,512,128]{3,2,1,0:T(8,128)(2,1)} %get-tuple-element.153.q_ref, ...), custom_call_target="tpu_custom_call", output_to_operand_aliasing={{0}: (7, {}), {1}: (8, {})} | custom-call | bytes 1360000 | tf_op jit(solution)/shard_map/attn_1/pallas_call | solution.py:243
  101.5 6.3 %attn_0.1 = (bf16[2048,256]{1,0:T(8,128)(2,1)}, f32[8,2,512]{2,1,0:T(2,128)}, bf16[256,1024]{1,0:T(8,128)(2,1)}, bf16[256,1024]{1,0:T(8,128)(2,1)}) custom-call(s32[1]{0:T(128)} %bitcast.core_ref, s32[8]{0:T(128)} %and_select_fusion.lo_ref, bf16[8,2,512,128]{3,2,1,0:T(8,128)(2,1)} %get-tuple-element.153.q_ref, ...), custom_call_target="tpu_custom_call", output_to_operand_aliasing={{0}: (7, {}), {1}: (8, {})} | custom-call | bytes 1360000 | tf_op jit(solution)/shard_map/attn_0/pallas_call | solution.py:243
  108.8 4.9 collective-permute-done.17.refs_3_
  117.6 11.7 %collective-permute-done.21 = bf16[256,1024]{1,0:T(8,128)(2,1)S(1)} collective-permute-done((bf16[256,1024]{1,0:T(8,128)(2,1)S(1)}, bf16[256,1024]{1,0:T(8,128)(2,1)S(1)}, u32[]{:S(2)}, u32[]{:S(2)}) %collective-permute-start.21) | collective-permute-done | bytes 524320 | tf_op jit(solution)/shard_map/ppermute | solution.py:765
  131.1 18.1 %collective-permute-done.19.refs_7_ = bf16[128,3456]{1,0:T(8,128)(2,1)S(1)} collective-permute-done((bf16[128,3456]{1,0:T(8,128)(2,1)S(1)}, bf16[128,3456]{1,0:T(8,128)(2,1)S(1)}, u32[]{:S(2)}, u32[]{:S(2)}) %collective-permute-start.19) | collective-permute-done | bytes 884768 | tf_op jit(solution)/shard_map/ppermute | solution.py:658
  150.2 7.9 %place_pieces.3.w_ref = bf16[1024,3456]{1,0:T(8,128)(2,1)} custom-call(s32[2]{0:T(128)} %pad_add_fusion.at_ref, bf16[128,3456]{1,0:T(8,128)(2,1)} %get-tuple-element.158.refs_0_, bf16[128,3456]{1,0:T(8,128)(2,1)} %copy-done.26, bf16[128,3456]{1,0:T(8,128)(2,1)} %collective-permute-done.11.refs_2_, bf16[128,3456]{1,0:T(8,128)(2,1)} %copy-done.28, ...), custom_call_target="tpu_custom_call" | custom-call | bytes 680000 | tf_op jit(solution)/shard_map/place_pieces/pallas_call | solution.py:633
  158.9 15.2 %ffn_3.1 = (bf16[2048,1024]{1,0:T(8,128)(2,1)}, bf16[2048,2304]{1,0:T(8,128)(2,1)}, bf16[2048,1152]{1,0:T(8,128)(2,1)}, bf16[256,1024]{1,0:T(8,128)(2,1)}, bf16[...) custom-call(s32[1]{0:T(128)} %bitcast.core_ref, bf16[2048,1024]{1,0:T(8,128)(2,1)} %x_ref.27, ...), custom_call_target="tpu_custom_call" | custom-call | bytes 255000000 | tf_op jit(solution)/shard_map/ffn_3/pallas_call | solution.py:305
  174.9 15.7 %ffn_2.1 = (bf16[2048,1024]{1,0:T(8,128)(2,1)}, bf16[2048,2304]{1,0:T(8,128)(2,1)}, bf16[2048,1152]{1,0:T(8,128)(2,1)}, bf16[256,1024]{1,0:T(8,128)(2,1)}, bf16[...) custom-call(s32[1]{0:T(128)} %bitcast.core_ref, ...), custom_call_target="tpu_custom_call", output_to_operand_aliasing={{0}: (7, {}), {1}: (8, {}), {2}: (9, {}), {5}: (10, {}), {6... | custom-call | bytes 255000000 | tf_op jit(solution)/shard_map/ffn_2/pallas_call | solution.py:305
  194.4 15.3 %ffn_1.1 = (bf16[2048,1024]{1,0:T(8,128)(2,1)}, bf16[2048,2304]{1,0:T(8,128)(2,1)}, bf16[2048,1152]{1,0:T(8,128)(2,1)}, bf16[256,1024]{1,0:T(8,128)(2,1)}, bf16[...) custom-call(s32[1]{0:T(128)} %bitcast.core_ref, ...), custom_call_target="tpu_custom_call", output_to_operand_aliasing={{0}: (7, {}), {1}: (8, {}), {2}: (9, {})} | custom-call | bytes 255000000 | tf_op jit(solution)/shard_map/ffn_1/pallas_call | solution.py:305
  211.8 15.3 %ffn_0.1 = (bf16[2048,1024]{1,0:T(8,128)(2,1)}, bf16[2048,2304]{1,0:T(8,128)(2,1)}, bf16[2048,1152]{1,0:T(8,128)(2,1)}, bf16[256,1024]{1,0:T(8,128)(2,1)}, bf16[...) custom-call(s32[1]{0:T(128)} %bitcast.core_ref, ...), custom_call_target="tpu_custom_call", output_to_operand_aliasing={{0}: (7, {}), {1}: (8, {}), {2}: (9, {}), {5}: (10, {}), {6... | custom-call | bytes 255000000 | tf_op jit(solution)/shard_map/ffn_0/pallas_call | solution.py:305
  231.2 7.9 %convolution_convert_fusion.1 = bf16[1152,1024]{1,0:T(8,128)(2,1)S(1)} fusion(bf16[2048,1152]{1,0:T(8,128)(2,1)} %get-tuple-element.212, bf16[2048,1024]{1,0:T(8,128)(2,1)S(1)} %copy-done), kind=kOutput, calls=%fused_computation.10 | convolution fusion | flops 4833017856 | bytes 11272192 | tf_op jit(solution)/shard_map/dot_general | solution.py:815
  248.4 11.2 %convolution_convert_fusion = bf16[1024,2304]{1,0:T(8,128)(2,1)S(1)} fusion(bf16[2048,1024]{1,0:T(8,128)(2,1)S(1)} %copy-done.2, bf16[2048,2304]{1,0:T(8,128)(2,1)S(1)} %bitcast.54), kind=kOutput, calls=%fused_computation | convolution fusion | flops 9666035712 | bytes 18350080 | tf_op jit(solution)/shard_map/dot_general | solution.py:817
  260.6 17.4 %collective-permute-done.42 = bf16[256,1024]{1,0:T(8,128)(2,1)S(1)} collective-permute-done((bf16[256,1024]{1,0:T(8,128)(2,1)S(1)}, bf16[256,1024]{1,0:T(8,128)(2,1)S(1)}, u32[]{:S(2)}, u32[]{:S(2)}) %collective-permute-start.42) | collective-permute-done | bytes 524320 | tf_op jit(solution)/shard_map/ppermute | solution.py:765
  280.8 2.7 collective-permute-start.44
  283.5 15.2 %back_3.1 = (f32[2048,128]{1,0:T(8,128)}, f32[2048,128]{1,0:T(8,128)}, bf16[2048,1024]{1,0:T(8,128)(2,1)}, bf16[2048,512]{1,0:T(8,128)(2,1)}, f32[512,1024]{1,0:...) custom-call(s32[1]{0:T(128)} %bitcast.core_ref, ...), custom_call_target="tpu_custom_call" | custom-call | bytes 255000000 | tf_op jit(solution)/shard_map/back_3/pallas_call | solution.py:449
  301.9 2.8 collective-permute-start.36
  307.2 11.6 %collective-permute-done.36 = bf16[128,2304]{1,0:T(8,128)(2,1)S(1)} collective-permute-done((bf16[128,2304]{1,0:T(8,128)(2,1)S(1)}, bf16[128,2304]{1,0:T(8,128)(2,1)S(1)}, u32[]{:S(2)}, u32[]{:S(2)}) %collective-permute-start.36) | collective-permute-done | bytes 589856 | tf_op jit(solution)/shard_map/ppermute | solution.py:693
  320.7 17.3 %back_2.1 = (f32[2048,128]{1,0:T(8,128)}, f32[2048,128]{1,0:T(8,128)}, bf16[2048,1024]{1,0:T(8,128)(2,1)}, bf16[2048,512]{1,0:T(8,128)(2,1)}, f32[512,1024]{1,0:...) custom-call(s32[1]{0:T(128)} %bitcast.core_ref, ...), custom_call_target="tpu_custom_call", output_to_operand_aliasing={{2}: (25, {}), {3}: (26, {})} | custom-call | bytes 255000000 | tf_op jit(solution)/shard_map/back_2/pallas_call | solution.py:449
  341.1 2.7 add_convert_fusion.refs_8_
  343.8 8.2 %collective-permute-done.56 = bf16[256,1024]{1,0:T(8,128)(2,1)S(1)} collective-permute-done((bf16[256,1024]{1,0:T(8,128)(2,1)S(1)}, bf16[256,1024]{1,0:T(8,128)(2,1)S(1)}, u32[]{:S(2)}, u32[]{:S(2)}) %collective-permute-start.56) | collective-permute-done | bytes 524320 | tf_op jit(solution)/shard_map/ppermute | solution.py:765
  354.0 4.0 collective-permute-done.47
  361.4 18.7 %back_1.1 = (f32[2048,128]{1,0:T(8,128)}, f32[2048,128]{1,0:T(8,128)}, bf16[2048,1024]{1,0:T(8,128)(2,1)}, bf16[2048,512]{1,0:T(8,128)(2,1)}, f32[512,1024]{1,0:...) custom-call(s32[1]{0:T(128)} %bitcast.core_ref, ...), custom_call_target="tpu_custom_call", output_to_operand_aliasing={{2}: (25, {}), {3}: (26, {})} | custom-call | bytes 255000000 | tf_op jit(solution)/shard_map/back_1/pallas_call | solution.py:449
  388.3 15.3 %back_0.1 = (f32[2048,128]{1,0:T(8,128)}, f32[2048,128]{1,0:T(8,128)}, bf16[2048,1024]{1,0:T(8,128)(2,1)}, bf16[2048,512]{1,0:T(8,128)(2,1)}, f32[512,1024]{1,0:...) custom-call(s32[1]{0:T(128)} %bitcast.core_ref, ...), custom_call_target="tpu_custom_call", output_to_operand_aliasing={{2}: (25, {}), {3}: (26, {})} | custom-call | bytes 255000000 | tf_op jit(solution)/shard_map/back_0/pallas_call | solution.py:449
  403.8 4.3 convolution_convert_fusion.3
  408.4 2.6 convert_add_fusion
  411.0 4.6 convolution_convert_fusion.2
  418.6 5.0 %collective-permute-done.70 = bf16[128,768]{0,1:T(8,128)(2,1)S(1)} collective-permute-done((bf16[128,768]{0,1:T(8,128)(2,1)S(1)}, bf16[128,768]{0,1:T(8,128)(2,1)S(1)}, u32[]{:S(2)}, u32[]{:S(2)}) %collective-permute-start.70) | collective-permute-done | bytes 196640 | tf_op jit(solution)/shard_map/ppermute | solution.py:693
  432.3 3.2 collective-permute-start.80
  439.2 2.4 collective-permute-start.81
  442.7 9.6 %output.1 = bf16[2048,1024]{1,0:T(8,128)(2,1)} custom-call(s32[1]{0:T(128)} %bitcast.core_ref, bf16[2048,1024]{1,0:T(8,128)(2,1)} %x_ref.27, bf16[256,1024]{1,0:T(8,128)(2,1)} %copy-done.9, bf16[256,1024]{1,0:T(8,128)(2,1)} %copy-done.13, bf16[256,1024]{1,0:T(8,128)(2,1)} %copy-done.6, bf16[256,1024]{1,0:T(8,128)(2,1)} %copy-done.10, ...), custom_call_target="tpu_custom_call" | custom-call | bytes 136000000 | tf_op jit(solution)/shard_map/output/pallas_call | solution.py:558
  455.9 4.0 grad_input_3.1.rest_0_
  460.7 3.8 grad_input_2.1.rest_0_
  466.7 3.8 grad_input_1.1.rest_0_
  470.5 3.3 collective-permute-done.75
  474.2 7.3 %collective-permute-done.76 = bf16[128,768]{0,1:T(8,128)(2,1)S(1)} collective-permute-done((bf16[128,768]{0,1:T(8,128)(2,1)S(1)}, bf16[128,768]{0,1:T(8,128)(2,1)S(1)}, u32[]{:S(2)}, u32[]{:S(2)}) %collective-permute-start.76) | collective-permute-done | bytes 196640 | tf_op jit(solution)/shard_map/ppermute | solution.py:708
  485.3 3.8 grad_input_0.1
  (380 shorter events, 107.0 us)
Async XLA Ops:
  37.8 20.3 %collective-permute-start.7 = (bf16[128,3456]{1,0:T(8,128)(2,1)}, bf16[128,3456]{1,0:T(8,128)(2,1)S(1)}, u32[]{:S(2)}, u32[]{:S(2)}) collective-permute-start(bf16[128,3456]{1,0:T(8,128)(2,1)} %get-tuple-element.158.refs_0_), channel_id=1, source_target_pairs={{0,8},{4,12},{8,16},{12,20},{16,24},{20,28},{24,0},{28,4},{1,9},{5... | collective-permute-start | bytes 2654216 | tf_op jit(solution)/shard_map/ppermute | solution.py:665
  38.3 20.7 %collective-permute-start.8 = (bf16[128,3456]{1,0:T(8,128)(2,1)}, bf16[128,3456]{1,0:T(8,128)(2,1)S(1)}, u32[]{:S(2)}, u32[]{:S(2)}) collective-permute-start(bf16[128,3456]{1,0:T(8,128)(2,1)} %get-tuple-element.158.refs_0_), channel_id=1, source_target_pairs={{0,4},{4,0},{8,12},{12,8},{16,20},{20,16},{24,28},{28,24},{1,5},{5... | collective-permute-start | bytes 2654216 | tf_op jit(solution)/shard_map/ppermute | solution.py:658
  58.1 30.6 %collective-permute-start.12 = (bf16[128,3456]{1,0:T(8,128)(2,1)S(1)}, bf16[128,3456]{1,0:T(8,128)(2,1)}, u32[]{:S(2)}, u32[]{:S(2)}) collective-permute-start(bf16[128,3456]{1,0:T(8,128)(2,1)S(1)} %collective-permute-done.7.refs_1_), channel_id=1, source_target_pairs={{0,4},{4,0},{8,12},{12,8},{16,20},{20,16},{24,28},{28,24},{1,5},{5... | collective-permute-start | bytes 2654216 | tf_op jit(solution)/shard_map/ppermute | solution.py:658
  59.1 29.6 %collective-permute-start.11 = (bf16[128,3456]{1,0:T(8,128)(2,1)S(1)}, bf16[128,3456]{1,0:T(8,128)(2,1)}, u32[]{:S(2)}, u32[]{:S(2)}) collective-permute-start(bf16[128,3456]{1,0:T(8,128)(2,1)S(1)} %collective-permute-done.7.refs_1_), channel_id=1, source_target_pairs={{0,8},{4,12},{8,16},{12,20},{16,24},{20,28},{24,0},{28,4},{1,9},{5... | collective-permute-start | bytes 2654216 | tf_op jit(solution)/shard_map/ppermute | solution.py:665
  88.7 25.0 %collective-permute-start.17 = (bf16[128,3456]{1,0:T(8,128)(2,1)}, bf16[128,3456]{1,0:T(8,128)(2,1)S(1)}, u32[]{:S(2)}, u32[]{:S(2)}) collective-permute-start(bf16[128,3456]{1,0:T(8,128)(2,1)} %collective-permute-done.11.refs_2_), channel_id=1, source_target_pairs={{0,8},{4,12},{8,16},{12,20},{16,24},{20,28},{24,0},{28,4},{1,9},{5... | collective-permute-start | bytes 2654216 | tf_op jit(solution)/shard_map/ppermute | solution.py:665
  90.0 18.4 %collective-permute-start.22 = (bf16[256,1024]{1,0:T(8,128)(2,1)S(1)}, bf16[256,1024]{1,0:T(8,128)(2,1)S(1)}, u32[]{:S(2)}, u32[]{:S(2)}) collective-permute-start(bf16[256,1024]{1,0:T(8,128)(2,1)S(1)} %add_convert_fusion.29), channel_id=1, source_target_pairs={{0,2},{1,3},{2,0},{3,1},{4,6},{5,7},{6,4},{7,5},{8,10},{9,11},{10,... | collective-permute-start | bytes 1572872 | tf_op jit(solution)/shard_map/ppermute | solution.py:765
  108.4 22.7 %collective-permute-start.18 = (bf16[128,3456]{1,0:T(8,128)(2,1)}, bf16[128,3456]{1,0:T(8,128)(2,1)S(1)}, u32[]{:S(2)}, u32[]{:S(2)}) collective-permute-start(bf16[128,3456]{1,0:T(8,128)(2,1)} %collective-permute-done.11.refs_2_), channel_id=1, source_target_pairs={{0,4},{4,0},{8,12},{12,8},{16,20},{20,16},{24,28},{28,24},{1,5},{5... | collective-permute-start | bytes 2654216 | tf_op jit(solution)/shard_map/ppermute | solution.py:658
  108.6 49.5 %collective-permute-start.23 = (bf16[256,1024]{1,0:T(8,128)(2,1)S(1)}, bf16[256,1024]{1,0:T(8,128)(2,1)S(1)}, u32[]{:S(2)}, u32[]{:S(2)}) collective-permute-start(bf16[256,1024]{1,0:T(8,128)(2,1)S(1)} %add_convert_fusion.23.own_ref.refs_6_), channel_id=1, source_target_pairs={{0,1},{1,0},{2,3},{3,2},{4,5},{5,4},{6,7},{7,6},{8,9},{9,8},{10,11... | collective-permute-start | bytes 1572872 | tf_op jit(solution)/shard_map/ppermute | solution.py:766
  113.6 35.5 %collective-permute-start.19 = (bf16[128,3456]{1,0:T(8,128)(2,1)S(1)}, bf16[128,3456]{1,0:T(8,128)(2,1)S(1)}, u32[]{:S(2)}, u32[]{:S(2)}) collective-permute-start(bf16[128,3456]{1,0:T(8,128)(2,1)S(1)} %collective-permute-done.17.refs_3_), channel_id=1, source_target_pairs={{0,4},{4,0},{8,12},{12,8},{16,20},{20,16},{24,28},{28,24},{1,5},{5... | collective-permute-start | bytes 2654216 | tf_op jit(solution)/shard_map/ppermute | solution.py:658
  129.2 45.5 %collective-permute-start.14 = (bf16[256,1024]{1,0:T(8,128)(2,1)S(1)}, bf16[256,1024]{1,0:T(8,128)(2,1)S(1)}, u32[]{:S(2)}, u32[]{:S(2)}) collective-permute-start(bf16[256,1024]{1,0:T(8,128)(2,1)S(1)} %add_convert_fusion.28), channel_id=1, source_target_pairs={{0,2},{1,3},{2,0},{3,1},{4,6},{5,7},{6,4},{7,5},{8,10},{9,11},{10,... | collective-permute-start | bytes 1572872 | tf_op jit(solution)/shard_map/ppermute | solution.py:765
  174.2 16.7 %collective-permute-start.25 = (bf16[256,1024]{1,0:T(8,128)(2,1)}, bf16[256,1024]{1,0:T(8,128)(2,1)S(1)}, u32[]{:S(2)}, u32[]{:S(2)}) collective-permute-start(bf16[256,1024]{1,0:T(8,128)(2,1)} %get-tuple-element.189), channel_id=1, source_target_pairs={{0,1},{1,0},{2,3},{3,2},{4,5},{5,4},{6,7},{7,6},{8,9},{9,8},{10,11... | collective-permute-start | bytes 1572872 | tf_op jit(solution)/shard_map/ppermute | solution.py:762
  174.2 19.4 %collective-permute-start.28 = (bf16[256,1024]{1,0:T(8,128)(2,1)S(1)}, bf16[256,1024]{1,0:T(8,128)(2,1)S(1)}, u32[]{:S(2)}, u32[]{:S(2)}) collective-permute-start(bf16[256,1024]{1,0:T(8,128)(2,1)S(1)} %add_convert_fusion.24.own_ref.refs_2_), channel_id=1, source_target_pairs={{0,1},{1,0},{2,3},{3,2},{4,5},{5,4},{6,7},{7,6},{8,9},{9,8},{10,11... | collective-permute-start | bytes 1572872 | tf_op jit(solution)/shard_map/ppermute | solution.py:766
  190.7 19.2 %collective-permute-start.24 = (bf16[256,1024]{1,0:T(8,128)(2,1)}, bf16[256,1024]{1,0:T(8,128)(2,1)S(1)}, u32[]{:S(2)}, u32[]{:S(2)}) collective-permute-start(bf16[256,1024]{1,0:T(8,128)(2,1)} %get-tuple-element.186), channel_id=1, source_target_pairs={{0,1},{1,0},{2,3},{3,2},{4,5},{5,4},{6,7},{7,6},{8,9},{9,8},{10,11... | collective-permute-start | bytes 1572872 | tf_op jit(solution)/shard_map/ppermute | solution.py:762
  191.0 19.6 %collective-permute-start.26 = (bf16[256,1024]{1,0:T(8,128)(2,1)S(1)}, bf16[256,1024]{1,0:T(8,128)(2,1)S(1)}, u32[]{:S(2)}, u32[]{:S(2)}) collective-permute-start(bf16[256,1024]{1,0:T(8,128)(2,1)S(1)} %add_convert_fusion.21), channel_id=1, source_target_pairs={{0,2},{1,3},{2,0},{3,1},{4,6},{5,7},{6,4},{7,5},{8,10},{9,11},{10,... | collective-permute-start | bytes 1572872 | tf_op jit(solution)/shard_map/ppermute | solution.py:765
  193.1 17.7 %collective-permute-start.27 = (bf16[256,1024]{1,0:T(8,128)(2,1)S(1)}, bf16[256,1024]{1,0:T(8,128)(2,1)S(1)}, u32[]{:S(2)}, u32[]{:S(2)}) collective-permute-start(bf16[256,1024]{1,0:T(8,128)(2,1)S(1)} %add_convert_fusion.27.own_ref.refs_0_), channel_id=1, source_target_pairs={{0,1},{1,0},{2,3},{3,2},{4,5},{5,4},{6,7},{7,6},{8,9},{9,8},{10,11... | collective-permute-start | bytes 1572872 | tf_op jit(solution)/shard_map/ppermute | solution.py:766
  193.2 37.4 %collective-permute-start.38 = (bf16[512,1024]{1,0:T(8,128)(2,1)}, bf16[512,1024]{1,0:T(8,128)(2,1)S(1)}, u32[]{:S(2)}, u32[]{:S(2)}) collective-permute-start(bf16[512,1024]{1,0:T(8,128)(2,1)} %get-tuple-element.211), channel_id=1, source_target_pairs={{0,1},{1,0},{2,3},{3,2},{4,5},{5,4},{6,7},{7,6},{8,9},{9,8},{10,11... | collective-permute-start | bytes 3145736 | tf_op jit(solution)/shard_map/ppermute | solution.py:762
  209.7 17.9 %collective-permute-start.30 = (bf16[256,1024]{1,0:T(8,128)(2,1)}, bf16[256,1024]{1,0:T(8,128)(2,1)S(1)}, u32[]{:S(2)}, u32[]{:S(2)}) collective-permute-start(bf16[256,1024]{1,0:T(8,128)(2,1)} %get-tuple-element.205), channel_id=1, source_target_pairs={{0,1},{1,0},{2,3},{3,2},{4,5},{5,4},{6,7},{7,6},{8,9},{9,8},{10,11... | collective-permute-start | bytes 1572872 | tf_op jit(solution)/shard_map/ppermute | solution.py:762
  210.1 17.9 %collective-permute-start.37 = (bf16[256,1024]{1,0:T(8,128)(2,1)S(1)}, bf16[256,1024]{1,0:T(8,128)(2,1)S(1)}, u32[]{:S(2)}, u32[]{:S(2)}) collective-permute-start(bf16[256,1024]{1,0:T(8,128)(2,1)S(1)} %add_convert_fusion.22), channel_id=1, source_target_pairs={{0,2},{1,3},{2,0},{3,1},{4,6},{5,7},{6,4},{7,5},{8,10},{9,11},{10,... | collective-permute-start | bytes 1572872 | tf_op jit(solution)/shard_map/ppermute | solution.py:765
  210.8 36.8 %collective-permute-start.32 = (bf16[256,1024]{1,0:T(8,128)(2,1)S(1)}, bf16[256,1024]{1,0:T(8,128)(2,1)S(1)}, u32[]{:S(2)}, u32[]{:S(2)}) collective-permute-start(bf16[256,1024]{1,0:T(8,128)(2,1)S(1)} %add_convert_fusion.20.down_ref), channel_id=1, source_target_pairs={{0,1},{1,0},{2,3},{3,2},{4,5},{5,4},{6,7},{7,6},{8,9},{9,8},{10,11... | collective-permute-start | bytes 1572872 | tf_op jit(solution)/shard_map/ppermute | solution.py:766
  227.1 17.7 %collective-permute-start.29 = (bf16[256,1024]{1,0:T(8,128)(2,1)}, bf16[256,1024]{1,0:T(8,128)(2,1)S(1)}, u32[]{:S(2)}, u32[]{:S(2)}) collective-permute-start(bf16[256,1024]{1,0:T(8,128)(2,1)} %get-tuple-element.203), channel_id=1, source_target_pairs={{0,1},{1,0},{2,3},{3,2},{4,5},{5,4},{6,7},{7,6},{8,9},{9,8},{10,11... | collective-permute-start | bytes 1572872 | tf_op jit(solution)/shard_map/ppermute | solution.py:762
  227.6 17.7 %collective-permute-start.33 = (bf16[512,1024]{1,0:T(8,128)(2,1)}, bf16[512,1024]{1,0:T(8,128)(2,1)S(1)}, u32[]{:S(2)}, u32[]{:S(2)}) collective-permute-start(bf16[512,1024]{1,0:T(8,128)(2,1)} %get-tuple-element.207), channel_id=1, source_target_pairs={{0,1},{1,0},{2,3},{3,2},{4,5},{5,4},{6,7},{7,6},{8,9},{9,8},{10,11... | collective-permute-start | bytes 3145736 | tf_op jit(solution)/shard_map/ppermute | solution.py:762
  230.6 89.6 %collective-permute-start.46 = (bf16[256,1024]{1,0:T(8,128)(2,1)}, bf16[256,1024]{1,0:T(8,128)(2,1)}, u32[]{:S(2)}, u32[]{:S(2)}) collective-permute-start(bf16[256,1024]{1,0:T(8,128)(2,1)} %add_convert_fusion.16.down_ref), channel_id=1, source_target_pairs={{0,1},{1,0},{2,3},{3,2},{4,5},{5,4},{6,7},{7,6},{8,9},{9,8},{10,11... | collective-permute-start | bytes 1572872 | tf_op jit(solution)/shard_map/ppermute | solution.py:766
  242.2 57.9 %collective-permute-start.45 = (bf16[512,1024]{1,0:T(8,128)(2,1)S(1)}, bf16[512,1024]{1,0:T(8,128)(2,1)}, u32[]{:S(2)}, u32[]{:S(2)}) collective-permute-start(bf16[512,1024]{1,0:T(8,128)(2,1)S(1)} %add_convert_fusion.2), channel_id=1, source_target_pairs={{0,2},{1,3},{2,0},{3,1},{4,6},{5,7},{6,4},{7,5},{8,10},{9,11},{10,... | collective-permute-start | bytes 3145736 | tf_op jit(solution)/shard_map/ppermute | solution.py:765
  245.3 34.0 %collective-permute-start.40 = (bf16[128,1152]{0,1:T(8,128)(2,1)S(1)}, bf16[128,1152]{0,1:T(8,128)(2,1)S(1)}, u32[]{:S(2)}, u32[]{:S(2)}) collective-permute-start(bf16[128,1152]{0,1:T(8,128)(2,1)S(1)} %get-tuple-element.317), channel_id=1, source_target_pairs={{0,4},{4,0},{8,12},{12,8},{16,20},{20,16},{24,28},{28,24},{1,5},{5... | collective-permute-start | bytes 884744 | tf_op jit(solution)/shard_map/ppermute | solution.py:693
  247.6 30.5 %collective-permute-start.42 = (bf16[256,1024]{1,0:T(8,128)(2,1)S(1)}, bf16[256,1024]{1,0:T(8,128)(2,1)S(1)}, u32[]{:S(2)}, u32[]{:S(2)}) collective-permute-start(bf16[256,1024]{1,0:T(8,128)(2,1)S(1)} %add_convert_fusion.19), channel_id=1, source_target_pairs={{0,2},{1,3},{2,0},{3,1},{4,6},{5,7},{6,4},{7,5},{8,10},{9,11},{10,... | collective-permute-start | bytes 1572872 | tf_op jit(solution)/shard_map/ppermute | solution.py:765
  259.6 21.2 %collective-permute-start.41 = (bf16[128,1152]{0,1:T(8,128)(2,1)S(1)}, bf16[128,1152]{0,1:T(8,128)(2,1)S(1)}, u32[]{:S(2)}, u32[]{:S(2)}) collective-permute-start(bf16[128,1152]{0,1:T(8,128)(2,1)S(1)} %get-tuple-element.316), channel_id=1, source_target_pairs={{0,4},{4,0},{8,12},{12,8},{16,20},{20,16},{24,28},{28,24},{1,5},{5... | collective-permute-start | bytes 884744 | tf_op jit(solution)/shard_map/ppermute | solution.py:693
  278.0 42.2 %collective-permute-start.43 = (bf16[128,1152]{0,1:T(8,128)(2,1)}, bf16[128,1152]{0,1:T(8,128)(2,1)}, u32[]{:S(2)}, u32[]{:S(2)}) collective-permute-start(bf16[128,1152]{0,1:T(8,128)(2,1)} %get-tuple-element.315), channel_id=1, source_target_pairs={{0,4},{4,0},{8,12},{12,8},{16,20},{20,16},{24,28},{28,24},{1,5},{5... | collective-permute-start | bytes 884744 | tf_op jit(solution)/shard_map/ppermute | solution.py:693
  279.3 61.8 %collective-permute-start.49 = (bf16[512,1024]{1,0:T(8,128)(2,1)S(1)}, bf16[512,1024]{1,0:T(8,128)(2,1)}, u32[]{:S(2)}, u32[]{:S(2)}) collective-permute-start(bf16[512,1024]{1,0:T(8,128)(2,1)S(1)} %add_convert_fusion.3), channel_id=1, source_target_pairs={{0,2},{1,3},{2,0},{3,1},{4,6},{5,7},{6,4},{7,5},{8,10},{9,11},{10,... | collective-permute-start | bytes 3145736 | tf_op jit(solution)/shard_map/ppermute | solution.py:765
  280.8 21.0 %collective-permute-start.44 = (bf16[128,1152]{0,1:T(8,128)(2,1)S(1)}, bf16[128,1152]{0,1:T(8,128)(2,1)}, u32[]{:S(2)}, u32[]{:S(2)}) collective-permute-start(bf16[128,1152]{0,1:T(8,128)(2,1)S(1)} %fusion.5), channel_id=1, source_target_pairs={{0,8},{4,12},{8,16},{12,20},{16,24},{20,28},{24,0},{28,4},{1,9},{5... | collective-permute-start | bytes 884744 | tf_op jit(solution)/shard_map/ppermute | solution.py:708
  301.9 17.0 %collective-permute-start.36 = (bf16[128,2304]{1,0:T(8,128)(2,1)S(1)}, bf16[128,2304]{1,0:T(8,128)(2,1)S(1)}, u32[]{:S(2)}, u32[]{:S(2)}) collective-permute-start(bf16[128,2304]{1,0:T(8,128)(2,1)S(1)} %get-tuple-element.312), channel_id=1, source_target_pairs={{0,4},{4,0},{8,12},{12,8},{16,20},{20,16},{24,28},{28,24},{1,5},{5... | collective-permute-start | bytes 1769480 | tf_op jit(solution)/shard_map/ppermute | solution.py:693
  306.6 34.2 %collective-permute-start.35 = (bf16[128,2304]{1,0:T(8,128)(2,1)}, bf16[128,2304]{1,0:T(8,128)(2,1)}, u32[]{:S(2)}, u32[]{:S(2)}) collective-permute-start(bf16[128,2304]{1,0:T(8,128)(2,1)} %get-tuple-element.313), channel_id=1, source_target_pairs={{0,4},{4,0},{8,12},{12,8},{16,20},{20,16},{24,28},{28,24},{1,5},{5... | collective-permute-start | bytes 1769480 | tf_op jit(solution)/shard_map/ppermute | solution.py:693
  318.8 19.2 %collective-permute-start.48 = (bf16[128,1152]{0,1:T(8,128)(2,1)}, bf16[128,1152]{0,1:T(8,128)(2,1)}, u32[]{:S(2)}, u32[]{:S(2)}) collective-permute-start(bf16[128,1152]{0,1:T(8,128)(2,1)} %fusion.4), channel_id=1, source_target_pairs={{0,8},{4,12},{8,16},{12,20},{16,24},{20,28},{24,0},{28,4},{1,9},{5... | collective-permute-start | bytes 884744 | tf_op jit(solution)/shard_map/ppermute | solution.py:708
  320.2 41.2 %collective-permute-start.52 = (bf16[256,1024]{1,0:T(8,128)(2,1)S(1)}, bf16[256,1024]{1,0:T(8,128)(2,1)}, u32[]{:S(2)}, u32[]{:S(2)}) collective-permute-start(bf16[256,1024]{1,0:T(8,128)(2,1)S(1)} %copy-done.21), channel_id=1, source_target_pairs={{0,1},{1,0},{2,3},{3,2},{4,5},{5,4},{6,7},{7,6},{8,9},{9,8},{10,11... | collective-permute-start | bytes 1572872 | tf_op jit(solution)/shard_map/ppermute | solution.py:766
  320.2 41.0 %collective-permute-start.50 = (bf16[512,1024]{1,0:T(8,128)(2,1)S(1)}, bf16[512,1024]{1,0:T(8,128)(2,1)}, u32[]{:S(2)}, u32[]{:S(2)}) collective-permute-start(bf16[512,1024]{1,0:T(8,128)(2,1)S(1)} %add_convert_fusion.1.refs_10_), channel_id=1, source_target_pairs={{0,1},{1,0},{2,3},{3,2},{4,5},{5,4},{6,7},{7,6},{8,9},{9,8},{10,11... | collective-permute-start | bytes 3145736 | tf_op jit(solution)/shard_map/ppermute | solution.py:766
  340.8 17.2 %collective-permute-start.47 = (bf16[128,2304]{1,0:T(8,128)(2,1)}, bf16[128,2304]{1,0:T(8,128)(2,1)S(1)}, u32[]{:S(2)}, u32[]{:S(2)}) collective-permute-start(bf16[128,2304]{1,0:T(8,128)(2,1)} %add_convert_fusion.6), channel_id=1, source_target_pairs={{0,8},{4,12},{8,16},{12,20},{16,24},{20,28},{24,0},{28,4},{1,9},{5... | collective-permute-start | bytes 1769480 | tf_op jit(solution)/shard_map/ppermute | solution.py:708
  352.0 30.5 %collective-permute-start.34 = (bf16[128,2304]{1,0:T(8,128)(2,1)}, bf16[128,2304]{1,0:T(8,128)(2,1)}, u32[]{:S(2)}, u32[]{:S(2)}) collective-permute-start(bf16[128,2304]{1,0:T(8,128)(2,1)} %get-tuple-element.314), channel_id=1, source_target_pairs={{0,4},{4,0},{8,12},{12,8},{16,20},{20,16},{24,28},{28,24},{1,5},{5... | collective-permute-start | bytes 1769480 | tf_op jit(solution)/shard_map/ppermute | solution.py:693
  353.8 26.3 %collective-permute-start.54 = (bf16[128,1152]{0,1:T(8,128)(2,1)}, bf16[128,1152]{0,1:T(8,128)(2,1)S(1)}, u32[]{:S(2)}, u32[]{:S(2)}) collective-permute-start(bf16[128,1152]{0,1:T(8,128)(2,1)} %fusion.2), channel_id=1, source_target_pairs={{0,8},{4,12},{8,16},{12,20},{16,24},{20,28},{24,0},{28,4},{1,9},{5... | collective-permute-start | bytes 884744 | tf_op jit(solution)/shard_map/ppermute | solution.py:708
  358.0 24.5 %collective-permute-start.61 = (bf16[256,1024]{1,0:T(8,128)(2,1)S(1)}, bf16[256,1024]{1,0:T(8,128)(2,1)}, u32[]{:S(2)}, u32[]{:S(2)}) collective-permute-start(bf16[256,1024]{1,0:T(8,128)(2,1)S(1)} %add_convert_fusion.13), channel_id=1, source_target_pairs={{0,2},{1,3},{2,0},{3,1},{4,6},{5,7},{6,4},{7,5},{8,10},{9,11},{10,... | collective-permute-start | bytes 1572872 | tf_op jit(solution)/shard_map/ppermute | solution.py:765
  361.3 27.0 %collective-permute-start.57 = (bf16[256,1024]{1,0:T(8,128)(2,1)S(1)}, bf16[256,1024]{1,0:T(8,128)(2,1)}, u32[]{:S(2)}, u32[]{:S(2)}) collective-permute-start(bf16[256,1024]{1,0:T(8,128)(2,1)S(1)} %copy-done.20), channel_id=1, source_target_pairs={{0,1},{1,0},{2,3},{3,2},{4,5},{5,4},{6,7},{7,6},{8,9},{9,8},{10,11... | collective-permute-start | bytes 1572872 | tf_op jit(solution)/shard_map/ppermute | solution.py:766
  361.4 24.7 %collective-permute-start.53 = (bf16[128,2304]{1,0:T(8,128)(2,1)S(1)}, bf16[128,2304]{1,0:T(8,128)(2,1)S(1)}, u32[]{:S(2)}, u32[]{:S(2)}) collective-permute-start(bf16[128,2304]{1,0:T(8,128)(2,1)S(1)} %add_convert_fusion.5), channel_id=1, source_target_pairs={{0,8},{4,12},{8,16},{12,20},{16,24},{20,28},{24,0},{28,4},{1,9},{5... | collective-permute-start | bytes 1769480 | tf_op jit(solution)/shard_map/ppermute | solution.py:708
  382.5 25.8 %collective-permute-start.58 = (bf16[128,2304]{1,0:T(8,128)(2,1)}, bf16[128,2304]{1,0:T(8,128)(2,1)}, u32[]{:S(2)}, u32[]{:S(2)}) collective-permute-start(bf16[128,2304]{1,0:T(8,128)(2,1)} %get-tuple-element.311), channel_id=1, source_target_pairs={{0,4},{4,0},{8,12},{12,8},{16,20},{20,16},{24,28},{28,24},{1,5},{5... | collective-permute-start | bytes 1769480 | tf_op jit(solution)/shard_map/ppermute | solution.py:693
  382.5 28.5 %collective-permute-start.63 = (bf16[512,1024]{1,0:T(8,128)(2,1)}, bf16[512,1024]{1,0:T(8,128)(2,1)}, u32[]{:S(2)}, u32[]{:S(2)}) collective-permute-start(bf16[512,1024]{1,0:T(8,128)(2,1)} %add_convert_fusion.refs_8_), channel_id=1, source_target_pairs={{0,1},{1,0},{2,3},{3,2},{4,5},{5,4},{6,7},{7,6},{8,9},{9,8},{10,11... | collective-permute-start | bytes 3145736 | tf_op jit(solution)/shard_map/ppermute | solution.py:766
  384.8 26.2 %collective-permute-start.62 = (bf16[256,1024]{1,0:T(8,128)(2,1)}, bf16[256,1024]{1,0:T(8,128)(2,1)}, u32[]{:S(2)}, u32[]{:S(2)}) collective-permute-start(bf16[256,1024]{1,0:T(8,128)(2,1)} %add_convert_fusion.12.own_ref), channel_id=1, source_target_pairs={{0,1},{1,0},{2,3},{3,2},{4,5},{5,4},{6,7},{7,6},{8,9},{9,8},{10,11... | collective-permute-start | bytes 1572872 | tf_op jit(solution)/shard_map/ppermute | solution.py:766
  386.1 44.2 %collective-permute-start.67 = (bf16[256,1024]{1,0:T(8,128)(2,1)}, bf16[256,1024]{1,0:T(8,128)(2,1)}, u32[]{:S(2)}, u32[]{:S(2)}) collective-permute-start(bf16[256,1024]{1,0:T(8,128)(2,1)} %add_convert_fusion.11), channel_id=1, source_target_pairs={{0,2},{1,3},{2,0},{3,1},{4,6},{5,7},{6,4},{7,5},{8,10},{9,11},{10,... | collective-permute-start | bytes 1572872 | tf_op jit(solution)/shard_map/ppermute | solution.py:765
  388.3 20.1 %collective-permute-start.59 = (bf16[128,2304]{1,0:T(8,128)(2,1)}, bf16[128,2304]{1,0:T(8,128)(2,1)S(1)}, u32[]{:S(2)}, u32[]{:S(2)}) collective-permute-start(bf16[128,2304]{1,0:T(8,128)(2,1)} %add_convert_fusion.4), channel_id=1, source_target_pairs={{0,8},{4,12},{8,16},{12,20},{16,24},{20,28},{24,0},{28,4},{1,9},{5... | collective-permute-start | bytes 1769480 | tf_op jit(solution)/shard_map/ppermute | solution.py:708
  426.6 33.2 %collective-permute-start.69 = (bf16[256,1024]{1,0:T(8,128)(2,1)S(1)}, bf16[256,1024]{1,0:T(8,128)(2,1)S(1)}, u32[]{:S(2)}, u32[]{:S(2)}) collective-permute-start(bf16[256,1024]{1,0:T(8,128)(2,1)S(1)} %copy-done.22), channel_id=1, source_target_pairs={{0,1},{1,0},{2,3},{3,2},{4,5},{5,4},{6,7},{7,6},{8,9},{9,8},{10,11... | collective-permute-start | bytes 1572872 | tf_op jit(solution)/shard_map/ppermute | solution.py:766
  439.2 25.4 %collective-permute-start.81 = (f32[17,128]{1,0:T(8,128)S(1)}, f32[17,128]{1,0:T(8,128)S(1)}, u32[]{:S(2)}, u32[]{:S(2)}) collective-permute-start(f32[17,128]{1,0:T(8,128)S(1)} %add.399), channel_id=1, source_target_pairs={{0,16},{4,20},{8,24},{12,28},{16,0},{20,4},{24,8},{28,12},{1,17},{... | collective-permute-start | bytes 26120 | tf_op jit(solution)/shard_map/ppermute | solution.py:716
  452.4 21.5 %collective-permute-start.65 = (bf16[256,1024]{1,0:T(8,128)(2,1)S(1)}, bf16[256,1024]{1,0:T(8,128)(2,1)S(1)}, u32[]{:S(2)}, u32[]{:S(2)}) collective-permute-start(bf16[256,1024]{1,0:T(8,128)(2,1)S(1)} %add_convert_fusion.9), channel_id=1, source_target_pairs={{0,2},{1,3},{2,0},{3,1},{4,6},{5,7},{6,4},{7,5},{8,10},{9,11},{10,... | collective-permute-start | bytes 1572872 | tf_op jit(solution)/shard_map/ppermute | solution.py:765
  (111 other events, 1319.3 us)
